TPU v7x, 32 devices: a whole 2x2x4 slice. The times are simulated.
32 devices in a mesh: dp: 16 (over z, y, x), head: 2 (over core).
Axes of the slice: x: 2, y: 2, z: 4, core: 2. Of those that a mesh axis runs over, the one named last changes fastest.
Arguments:
- tokens: bfloat16 [32768, 768], P(('dp', 'head')), may hold values from -6 to 6
- lengths: int32 [16, 4], P('dp'), may hold values from 1 to 1024, 2048 in all within a row
- norm_gains: float32 [2, 768], replicated, may hold values from 0.5 to 1.5
- joined_weight: float32 [2, 1152, 768], P('head', 'dp'), may hold values from -0.21875 to 0.21875
- mixer_weight: float32 [2, 768, 384], P('head', 'dp'), may hold values from -0.875 to 0.875
- expand_weight: float32 [2, 1152, 768], P('head', 'dp'), may hold values from -0.21875 to 0.21875
- shrink_weight: float32 [2, 768, 576], P('head', 'dp'), may hold values from -0.1875 to 0.1875
- joined_momentum: float32 [2, 1152, 768], P('head', 'dp'), may hold values from -320 to 320
- mixer_momentum: float32 [2, 768, 384], P('head', 'dp'), may hold values from -320 to 320
- expand_momentum: float32 [2, 1152, 768], P('head', 'dp'), may hold values from -320 to 320
- shrink_momentum: float32 [2, 768, 576], P('head', 'dp'), may hold values from -320 to 320
- gain_momentum: float32 [2, 768], replicated, may hold values from -320 to 320
- cotangent: bfloat16 [32768, 768], P('dp'), may hold values from -6 to 6
Outputs:
- layer_output: bfloat16 [32768, 768], P(('dp', 'head'))
- input_gradient: float32 [32768, 768], P(('dp', 'head'))
- momentum_joined: float32 [2, 1152, 768], P('head', 'dp')
- momentum_mixer: float32 [2, 768, 384], P('head', 'dp')
- momentum_expand: float32 [2, 1152, 768], P('head', 'dp')
- momentum_shrink: float32 [2, 768, 576], P('head', 'dp')
- updated_joined: float32 [2, 1152, 768], P('head', 'dp')
- updated_mixer: float32 [2, 768, 384], P('head', 'dp')
- updated_expand: float32 [2, 1152, 768], P('head', 'dp')
- updated_shrink: float32 [2, 768, 576], P('head', 'dp')
- momentum_gains: float32 [2, 768], replicated
- updated_gains: float32 [2, 768], replicated
Inputs may be any that keep to these rules, and one draw needn't show every extreme that they name: Each row of lengths sums to 2048, and its largest entry is 1024.
All inputs are finite; a program needn't handle non-finite values.
Results may differ from a plain program's by a relative error of at most 0.015.
Values may be sent and summed in bfloat16 or wider, within the bound.
No kernel may reach another device: no remote copies, remote signals or barrier semaphores. Data moves between devices by JAX's collectives and lax.ppermute only.
A program may use at most 256 MiB of HBM per device.

v0:
```python
import functools
import math

import jax
import jax.numpy as jnp
from jax import lax
from jax.experimental import pallas as pl
from jax.experimental.pallas import tpu as pltpu
from jax.sharding import PartitionSpec as P

HEAD_DIM = 64
NS_ITERS = 3

theta_base = 160000.0
norm_epsilon = 1e-05
ns_first = 3.4445
ns_second = -4.775
ns_third = 2.0315
muon_rate = 1.0
gain_rate = 0.3

bf16 = jnp.bfloat16
f32 = jnp.float32
LOG2E = math.log2(math.e)
QUERY_SCALE = 0.125 * LOG2E
SAFE_SCORE = 60.0
DEPTH = 128
TILE_Q = 256
TILE_K = 256
FWD_SKEW = 6
BWD_SKEW = 2

NN = (((1,), (0,)), ((), ()))
NT = (((1,), (1,)), ((), ()))
TN = (((0,), (0,)), ((), ()))
TT = (((0,), (1,)), ((), ()))
QUARTERS = 4


def dot(left, right, dims):
    return lax.dot_general(left, right, dims, preferred_element_type=f32)


def key_bounds(length_row, row_count):
    ends = jnp.cumsum(length_row)
    starts = ends - length_row
    first = jnp.arange(row_count // TILE_Q, dtype=jnp.int32) * TILE_Q
    labels = jnp.arange(length_row.shape[0], dtype=jnp.int32)

    def pick(places, table):
        segment = jnp.sum((places[:, None] >= ends[None, :]).astype(jnp.int32), axis=1)
        return jnp.sum(jnp.where(segment[:, None] == labels[None, :], table[None, :], 0), axis=1)

    low = pick(first, starts) // TILE_K
    high = (pick(first + TILE_Q - 1, ends) + TILE_K - 1) // TILE_K
    return low.astype(jnp.int32), high.astype(jnp.int32)


def doc_tables(length_row, row_count):
    ends = jnp.cumsum(length_row)
    starts = ends - length_row
    count = length_row.shape[0]
    places = jnp.arange(row_count, dtype=jnp.int32)[None, :]
    member = (places >= starts[:, None]) & (places < ends[:, None])
    rest = jnp.zeros((16 - count, row_count), f32)
    key_rows = jnp.concatenate([member.astype(f32), rest], axis=0).astype(bf16)
    query_rows = jnp.concatenate([jnp.where(member, 0.0, -1e30), rest], axis=0).astype(bf16)
    doc_first = jnp.sum(jnp.where(member, starts[:, None], 0), axis=0, keepdims=True)
    position = (places - doc_first).astype(f32)
    half_dim = HEAD_DIM // 2
    frequency = jnp.exp(
        jnp.arange(half_dim, dtype=f32) * (-2.0 * math.log(theta_base) / HEAD_DIM)
    )
    angles = frequency[:, None] * position
    return key_rows, query_rows, jnp.cos(angles), jnp.sin(angles)


def rotate(values, cosine, sine):
    half = HEAD_DIM // 2
    heads = values.reshape(-1, HEAD_DIM, values.shape[1])
    low, high = heads[:, :half], heads[:, half:]
    turned = jnp.concatenate([low * cosine - high * sine, high * cosine + low * sine], axis=1)
    return turned.reshape(values.shape)


def unrotate(values, cosine, sine):
    return rotate(values, cosine, -sine)


def rows16(parts):
    rest = jnp.zeros((16 - len(parts), parts[0].shape[1]), f32)
    return jnp.concatenate([part.astype(f32) for part in parts] + [rest], axis=0).astype(bf16)


def split3(value):
    first = value.astype(bf16)
    left = value - first.astype(f32)
    second = left.astype(bf16)
    third = (left - second.astype(f32)).astype(bf16)
    return [first, second, third]


def three_ones(count):
    return jnp.concatenate([jnp.ones((3, count), f32), jnp.zeros((13, count), f32)], axis=0).astype(
        bf16
    )


def forward_kernel(
    low, high, queries, keys, values, key_rows, query_rows, out, logsum, keys_in, values_in, queries_in, safe
):
    heads = queries.shape[0] // HEAD_DIM
    rows = keys.shape[1]
    step = pl.program_id(0)

    @pl.when(step == 0)
    def _():
        worst = jnp.zeros((1, 1), f32)
        ones = rows16([jnp.ones((1, rows), f32)])
        for h in range(heads):
            band = slice(h * HEAD_DIM, (h + 1) * HEAD_DIM)
            key = keys[band, :]
            pad = jnp.zeros((DEPTH - HEAD_DIM - 16, rows), bf16)
            keys_in[h] = jnp.concatenate([key, key_rows[...], pad], axis=0).T
            values_in[h, :HEAD_DIM, :] = values[band, :]
            values_in[h, HEAD_DIM:, :] = ones
            query_full = queries[band, :].astype(f32)
            key_full = key.astype(f32)
            query_top = jnp.max(
                jnp.sum(query_full * query_full, axis=0, keepdims=True), axis=1, keepdims=True
            )
            key_top = jnp.max(
                jnp.sum(key_full * key_full, axis=0, keepdims=True), axis=1, keepdims=True
            )
            worst = jnp.maximum(worst, query_top * key_top)
        safe[0] = jnp.where(worst[0, 0] <= SAFE_SCORE * SAFE_SCORE, 1, 0)

    first = pl.multiple_of(step * TILE_Q, TILE_Q)
    for h in range(heads):
        queries_in[h, :HEAD_DIM, :] = queries[h * HEAD_DIM : (h + 1) * HEAD_DIM, pl.ds(first, TILE_Q)]
        queries_in[h, HEAD_DIM : HEAD_DIM + 16, :] = query_rows[...]
        queries_in[h, HEAD_DIM + 16 :, :] = jnp.zeros((DEPTH - HEAD_DIM - 16, TILE_Q), bf16)

    def finish(peaks, totals):
        for h in range(heads):
            weight = totals[h][HEAD_DIM : HEAD_DIM + 1, :]
            out[h * HEAD_DIM : (h + 1) * HEAD_DIM, :] = (totals[h][:HEAD_DIM, :] / weight).astype(bf16)
            level = jnp.log2(weight)
            logsum[h : h + 1, :] = level if peaks is None else peaks[h] + level

    empty = tuple(jnp.zeros((HEAD_DIM + 16, TILE_Q), f32) for _ in range(heads))

    @pl.when(safe[0] == 1)
    def _():
        def block(j, totals):
            span = pl.ds(pl.multiple_of(j * TILE_K, TILE_K), TILE_K)
            result = [None] * heads
            waiting = {}
            for t in range(heads + FWD_SKEW):
                if t < heads:
                    waiting[t] = dot(keys_in[t, span, :], queries_in[t], NN)
                h = t - FWD_SKEW
                if h >= 0:
                    raised = jnp.exp2(waiting.pop(h)).astype(bf16)
                    result[h] = totals[h] + dot(values_in[h, :, span], raised, NN)
            return tuple(result)

        finish(None, lax.fori_loop(low[step], high[step], block, empty))

    @pl.when(safe[0] == 0)
    def _():
        def block(j, carry):
            peaks, totals = carry
            span = pl.ds(pl.multiple_of(j * TILE_K, TILE_K), TILE_K)
            new_peaks = []
            new_totals = []
            for h in range(heads):
                scores = dot(keys_in[h, span, :], queries_in[h], NN)
                peak = jnp.maximum(peaks[h], jnp.max(scores, axis=0, keepdims=True))
                raised = jnp.exp2(scores - peak).astype(bf16)
                new_totals.append(
                    totals[h] * jnp.exp2(peaks[h] - peak) + dot(values_in[h, :, span], raised, NN)
                )
                new_peaks.append(peak)
            return tuple(new_peaks), tuple(new_totals)

        lowest = tuple(jnp.full((1, TILE_Q), -3e38, f32) for _ in range(heads))
        finish(*lax.fori_loop(low[step], high[step], block, (lowest, empty)))


def attention_forward(low, high, queries, keys, values, key_rows, query_rows):
    width, rows = queries.shape
    heads = width // HEAD_DIM

    def full(count):
        return pl.BlockSpec((count, rows), lambda i, low, high: (0, 0))

    def tile(count):
        return pl.BlockSpec((count, TILE_Q), lambda i, low, high: (0, i))

    return pl.pallas_call(
        forward_kernel,
        out_shape=(
            jax.ShapeDtypeStruct((width, rows), bf16),
            jax.ShapeDtypeStruct((heads, rows), f32),
        ),
        grid_spec=pltpu.PrefetchScalarGridSpec(
            num_scalar_prefetch=2,
            grid=(rows // TILE_Q,),
            in_specs=[full(width), full(width), full(width), full(16), tile(16)],
            out_specs=[tile(width), tile(heads)],
            scratch_shapes=[
                pltpu.VMEM((heads, rows, DEPTH), bf16),
                pltpu.VMEM((heads, HEAD_DIM + 16, rows), bf16),
                pltpu.VMEM((heads, DEPTH, TILE_Q), bf16),
                pltpu.SMEM((1,), jnp.int32),
            ],
        ),
        compiler_params=pltpu.CompilerParams(
            dimension_semantics=("arbitrary",), vmem_limit_bytes=40 << 20
        ),
        name="attention_forward",
    )(low, high, queries, keys, values, key_rows, query_rows)


def backward_kernel(
    low, high, queries, keys, values, grads, outs, logsum, key_rows, query_rows,
    query_grad, key_grad, value_grad, *scratch
):
    heads = queries.shape[0] // HEAD_DIM
    rows = keys.shape[1]
    keys_in, values_in, queries_in, grads_in = scratch[:4]
    key_sum = scratch[4 : 4 + heads]
    value_sum = scratch[4 + heads : 4 + 2 * heads]
    query_sum = scratch[4 + 2 * heads : 4 + 3 * heads]
    step = pl.program_id(0)

    @pl.when(step == 0)
    def _():
        ones = three_ones(rows)
        for h in range(heads):
            band = slice(h * HEAD_DIM, (h + 1) * HEAD_DIM)
            pad = jnp.zeros((DEPTH - HEAD_DIM - 32, rows), bf16)
            keys_in[h] = jnp.concatenate([keys[band, :], key_rows[...], ones, pad], axis=0).T
            pad = jnp.zeros((DEPTH - HEAD_DIM - 16, rows), bf16)
            values_in[h] = jnp.concatenate([values[band, :], ones, pad], axis=0).T
            key_sum[h][...] = jnp.zeros((HEAD_DIM, rows), f32)
            value_sum[h][...] = jnp.zeros((HEAD_DIM, rows), f32)

    for h in range(heads):
        band = slice(h * HEAD_DIM, (h + 1) * HEAD_DIM)
        queries_in[h, :HEAD_DIM, :] = queries[band, :]
        queries_in[h, HEAD_DIM : HEAD_DIM + 16, :] = query_rows[...]
        queries_in[h, HEAD_DIM + 16 : HEAD_DIM + 32, :] = rows16(split3(-logsum[h : h + 1, :]))
        queries_in[h, HEAD_DIM + 32 :, :] = jnp.zeros((DEPTH - HEAD_DIM - 32, TILE_Q), bf16)
        inner = jnp.sum(grads[band, :].astype(f32) * outs[band, :].astype(f32), axis=0, keepdims=True)
        grads_in[h, :HEAD_DIM, :] = grads[band, :]
        grads_in[h, HEAD_DIM : HEAD_DIM + 16, :] = rows16(split3(-inner))
        grads_in[h, HEAD_DIM + 16 :, :] = jnp.zeros((DEPTH - HEAD_DIM - 16, TILE_Q), bf16)
        query_sum[h][...] = jnp.zeros((HEAD_DIM, TILE_Q), f32)

    def block(j, carry):
        span = pl.ds(pl.multiple_of(j * TILE_K, TILE_K), TILE_K)
        waiting = {}
        for t in range(heads + BWD_SKEW):
            if t < heads:
                waiting[t] = (
                    dot(keys_in[t, span, :], queries_in[t], NN),
                    dot(values_in[t, span, :], grads_in[t], NN),
                )
            h = t - BWD_SKEW
            if h < 0:
                continue
            band = slice(h * HEAD_DIM, (h + 1) * HEAD_DIM)
            scores, weight_grad = waiting.pop(h)
            softmax = jnp.exp2(scores)
            score_grad = (softmax * weight_grad).astype(bf16)
            value_sum[h][:, span] += dot(grads[band, :], softmax.astype(bf16), NT)
            key_sum[h][:, span] += dot(queries[band, :], score_grad, NT)
            query_sum[h][...] += dot(keys[band, span], score_grad, NN)
        return carry

    lax.fori_loop(low[step], high[step], block, 0)
    for h in range(heads):
        query_grad[h * HEAD_DIM : (h + 1) * HEAD_DIM, :] = query_sum[h][...] * 0.125

    @pl.when(step == pl.num_programs(0) - 1)
    def _():
        for h in range(heads):
            band = slice(h * HEAD_DIM, (h + 1) * HEAD_DIM)
            key_grad[band, :] = key_sum[h][...] * (1.0 / LOG2E)
            value_grad[band, :] = value_sum[h][...]


def attention_backward(low, high, queries, keys, values, grads, outs, logsum, key_rows, query_rows):
    width, rows = queries.shape
    heads = width // HEAD_DIM

    def full(count):
        return pl.BlockSpec((count, rows), lambda i, low, high: (0, 0))

    def tile(count):
        return pl.BlockSpec((count, TILE_Q), lambda i, low, high: (0, i))

    result = jax.ShapeDtypeStruct((width, rows), f32)
    return pl.pallas_call(
        backward_kernel,
        out_shape=(result, result, result),
        grid_spec=pltpu.PrefetchScalarGridSpec(
            num_scalar_prefetch=2,
            grid=(rows // TILE_Q,),
            in_specs=[
                tile(width), full(width), full(width), tile(width), tile(width), tile(heads),
                full(16), tile(16),
            ],
            out_specs=[tile(width), full(width), full(width)],
            scratch_shapes=[
                pltpu.VMEM((heads, rows, DEPTH), bf16),
                pltpu.VMEM((heads, rows, DEPTH), bf16),
                pltpu.VMEM((heads, DEPTH, TILE_Q), bf16),
                pltpu.VMEM((heads, DEPTH, TILE_Q), bf16),
            ]
            + [pltpu.VMEM((HEAD_DIM, rows), f32)] * (2 * heads)
            + [pltpu.VMEM((HEAD_DIM, TILE_Q), f32)] * heads,
        ),
        compiler_params=pltpu.CompilerParams(
            dimension_semantics=("arbitrary",), vmem_limit_bytes=52 << 20
        ),
        name="attention_backward",
    )(low, high, queries, keys, values, grads, outs, logsum, key_rows, query_rows)


def swap(value, axis, bit):
    count = lax.axis_size(axis)
    return lax.ppermute(value, axis, [(i, i ^ bit) for i in range(count)])


def bit_orders():
    bits = lax.axis_size("dp").bit_length() - 1
    return [[(start + k) % (bits - 1) for k in range(bits - 1)] + [bits - 1] for start in range(3)]


def steps_count():
    return lax.axis_size("dp").bit_length() - 1


def reduce_start(value):
    bits = steps_count()
    rows = value.shape[0] >> bits
    return value.reshape((2,) * bits + (rows, value.shape[1]))


def reduce_step(held, step, which):
    bits = steps_count()
    bit = bit_orders()[which][step]
    axis = bits - 1 - bit
    side = (lax.axis_index("dp") >> bit) & 1
    kept = lax.dynamic_slice_in_dim(held, side, 1, axis)
    sent = lax.dynamic_slice_in_dim(held, 1 - side, 1, axis)
    total = kept.astype(f32) + swap(sent, "dp", 1 << bit).astype(f32)
    if step + 1 == bits:
        return total.reshape(held.shape[-2:])
    return total.astype(bf16)


def gather_start(value):
    return value[(None,) * steps_count()]


def gather_step(held, step, which):
    bits = steps_count()
    bit = bit_orders()[which][bits - 1 - step]
    return jnp.concatenate([held, swap(held, "dp", 1 << bit)], axis=bits - 1 - bit)


def ordered_step(held, step, which):
    bits = steps_count()
    bit = bit_orders()[which][bits - 1 - step]
    got = swap(held, "dp", 1 << bit)
    low_side = ((lax.axis_index("dp") >> bit) & 1) == 0
    return jnp.concatenate(
        [jnp.where(low_side, held, got), jnp.where(low_side, got, held)], axis=bits - 1 - bit
    )


def gather_rows(held):
    return held.reshape(-1, held.shape[-1])


def thirds(value):
    unit = value.shape[1] // 3 // 128 * 128
    return [value[:, :unit], value[:, unit : 2 * unit], value[:, 2 * unit :]]


def halves_of(value):
    unit = value.shape[1] // 256 * 128
    return [value[:, :unit], value[:, unit:]]


def quarter(step, states, part, first=0):
    bits = steps_count()
    for index in range(bits * part // QUARTERS, bits * (part + 1) // QUARTERS):
        states = [step(state, index, first + which) for which, state in enumerate(states)]
    return states


def tie(*values):
    return lax.optimization_barrier(values)


def total_step(value, part):
    if part == 0:
        return value + swap(value, "head", 1)
    bits = steps_count()
    for bit in range(bits * (part - 1) // QUARTERS, bits * part // QUARTERS):
        value = value + swap(value, "dp", 1 << bit)
    return value


def halves(own, other, head):
    first = jnp.where(head == 0, own, other)
    second = jnp.where(head == 0, other, own)
    return jnp.concatenate([first, second], axis=0)


def layer_norm(values, gain_row):
    centred = values - jnp.mean(values, axis=-1, keepdims=True)
    inverse = lax.rsqrt(jnp.mean(centred * centred, axis=-1, keepdims=True) + norm_epsilon)
    normal = centred * inverse
    return normal * gain_row, normal, inverse


def norm_back(upstream, gain_row, normal, inverse):
    scaled = upstream * gain_row
    inner_mean = jnp.mean(scaled * normal, axis=-1, keepdims=True)
    return inverse * (scaled - jnp.mean(scaled, axis=-1, keepdims=True) - normal * inner_mean)


def gated(active_in, linear_in):
    return jax.nn.gelu(active_in, approximate=False) * linear_in


def schulz_start(own, gathered):
    gram = dot(gathered, gathered, TN)
    norm_value = jnp.sqrt(jnp.trace(gram)) + 1e-07
    return own / norm_value, gram / (norm_value * norm_value)


def schulz_step(state, last=False):
    rows, gram = state
    low_gram = gram.astype(bf16)
    change = (ns_second * gram + ns_third * dot(low_gram, low_gram, NN)).astype(bf16)
    rows = ns_first * rows + dot(rows.astype(bf16), change, NN)
    if last:
        return rows
    once = ns_first * gram + dot(low_gram, change, NN)
    return rows, ns_first * once + dot(once.astype(bf16), change, NN)


def schulz_rest(state):
    for iteration in range(NS_ITERS):
        state = schulz_step(state, iteration + 1 == NS_ITERS)
    return state


def shards(
    tokens,
    lengths,
    norm_gains,
    joined_weight,
    mixer_weight,
    expand_weight,
    shrink_weight,
    joined_momentum,
    mixer_momentum,
    expand_momentum,
    shrink_momentum,
    gain_momentum,
    cotangent,
):
    row_count = cotangent.shape[0]
    local_rows = tokens.shape[0]
    head = lax.axis_index("head")
    mixer_width = mixer_weight.shape[2]

    def own_half(value):
        return lax.dynamic_slice_in_dim(value, head * local_rows, local_rows, 0)

    def other_half(value):
        return lax.dynamic_slice_in_dim(value, (1 - head) * local_rows, local_rows, 0)

    joined_parts = [gather_start(part) for part in thirds(joined_weight[0].astype(bf16))]
    joined_parts = quarter(ordered_step, joined_parts, 0)
    others = [gather_start(part) for part in halves_of(expand_weight[0].astype(bf16))] + [
        gather_start(jnp.concatenate([mixer_weight[0], shrink_weight[0]], axis=1).astype(bf16))
    ]
    key_rows, query_rows, cosine, sine = doc_tables(lengths[0], row_count)
    low, high = key_bounds(lengths[0], row_count)
    residual = halves(tokens, swap(tokens, "head", 1), head).astype(f32)
    first_normed, first_normal, first_inverse = layer_norm(residual, norm_gains[0])
    first_low = first_normed.astype(bf16)

    joined_parts, others = tie(joined_parts, others)
    joined_parts = quarter(ordered_step, joined_parts, 1)
    others = quarter(ordered_step, others, 0)
    joined_parts, others = tie(joined_parts, others)
    joined_parts = quarter(ordered_step, joined_parts, 2)
    moved = quarter(ordered_step, others, 1)
    joined_parts, first_low = tie(joined_parts, first_low)
    joined_parts = quarter(ordered_step, joined_parts, 3)
    joined_parts, others = tie(joined_parts, moved)

    moved = quarter(ordered_step, others, 2)
    joined_low = jnp.concatenate([gather_rows(part) for part in joined_parts], axis=1)
    joined = dot(joined_low, first_low, NT)
    width = joined.shape[0] // 3
    queries = (rotate(joined[:width], cosine, sine) * QUERY_SCALE).astype(bf16)
    keys = rotate(joined[width : 2 * width], cosine, sine).astype(bf16)
    values = joined[2 * width :].astype(bf16)
    others, queries, keys, values, low = tie(moved, queries, keys, values, low)
    moved = quarter(ordered_step, others, 3)
    attended, logsum = attention_forward(low, high, queries, keys, values, key_rows, query_rows)
    others, attended, logsum = tie(moved, attended, logsum)
    attended_other = swap(attended, "head", 1)
    expand_low = jnp.concatenate([gather_rows(part) for part in others[:2]], axis=1)
    both_low = gather_rows(others[2])
    mixer_low, shrink_low = both_low[:, :mixer_width], both_low[:, mixer_width:]
    mixer_other = swap(mixer_low, "head", 1)

    middle = residual + dot(attended, mixer_low, TT) + dot(attended_other, mixer_other, TT)
    second_normed, second_normal, second_inverse = layer_norm(middle, norm_gains[1])
    second_low = second_normed.astype(bf16)

    expanded = dot(second_low, expand_low, NT)
    hidden_width = expanded.shape[1] // 2
    activated, linear_part = expanded[:, :hidden_width], expanded[:, hidden_width:]
    hidden = gated(activated, linear_part).astype(bf16)

    hidden_grad = dot(cotangent, shrink_low, NN)
    unused, gate_pull = jax.vjp(gated, activated, linear_part)
    active_grad, linear_grad = gate_pull(hidden_grad)
    expand_back = jnp.concatenate([active_grad, linear_grad], axis=1).astype(bf16)
    second_part = dot(expand_back, expand_low, NN)
    second_other = swap(second_part.astype(bf16), "head", 1)
    shrink_grad = dot(cotangent, hidden, TN).astype(bf16)
    expand_grad = dot(expand_back, second_low, TN).astype(bf16)

    sums, second_other = tie(
        [reduce_start(part) for part in halves_of(expand_grad) + [shrink_grad]], second_other
    )
    moved = quarter(reduce_step, sums, 0)
    second_back = second_part + second_other.astype(f32)
    middle_grad = cotangent.astype(f32) + norm_back(
        second_back, norm_gains[1], second_normal, second_inverse
    )
    middle_low = middle_grad.astype(bf16)
    attended_grad = dot(mixer_low, middle_low, TT).astype(bf16)

    sums, attended_grad, middle_low = tie(moved, attended_grad, middle_low)
    moved = quarter(reduce_step, sums, 1)
    mixer_grad = lax.dot_general(
        middle_low, attended, (((0,), (1,)), ((), ())), preferred_element_type=f32
    ).astype(bf16)
    second_gain_grad = jnp.sum(own_half(second_back * second_normal), axis=0)

    sums, mixer_grad, second_gain_grad, shrink_now = tie(
        moved, mixer_grad, second_gain_grad, shrink_low
    )
    moved = quarter(reduce_step, sums, 2)
    mixer_moved = quarter(reduce_step, [reduce_start(mixer_grad)], 0, 2)
    fed_own = dot(own_half(hidden), shrink_now, NT)
    fed_other = dot(other_half(hidden), shrink_now, NT).astype(bf16)

    sums, mixer_sum, fed_other, low = tie(moved, mixer_moved, fed_other, low)
    moved = quarter(reduce_step, sums, 3)
    mixer_moved = quarter(reduce_step, mixer_sum, 1, 2)
    fed_other = swap(fed_other, "head", 1)
    query_grad, key_grad, value_grad = attention_backward(
        low, high, queries, keys, values, attended_grad, attended, logsum, key_rows, query_rows
    )
    sums, mixer_sum, query_grad, key_grad, value_grad = tie(
        moved, mixer_moved, query_grad, key_grad, value_grad
    )
    expand_next = 0.5 * expand_momentum[0] + jnp.concatenate(sums[:2], axis=1)
    shrink_next = 0.5 * shrink_momentum[0] + sums[2]
    gathers = [gather_start(part) for part in halves_of(expand_next.astype(bf16))]
    gathers.append(gather_start(shrink_next.astype(bf16)))

    moved = quarter(gather_step, gathers, 0)
    mixer_moved = quarter(reduce_step, mixer_sum, 2, 2)
    joined_back = jnp.concatenate(
        [unrotate(query_grad, cosine, sine), unrotate(key_grad, cosine, sine), value_grad], axis=0
    ).astype(bf16)
    joined_grad = dot(joined_back, first_low, NN).astype(bf16)

    def first_part(start, weight):
        columns = lax.dynamic_slice_in_dim(joined_back, start, local_rows, 1)
        return dot(columns, weight, TN)

    gathers, mixer_sum, joined_grad, joined_now = tie(moved, mixer_moved, joined_grad, joined_low)
    sums = quarter(reduce_step, [reduce_start(part) for part in thirds(joined_grad)], 0)
    moved = quarter(gather_step, gathers, 1)
    mixer_moved = quarter(reduce_step, mixer_sum, 3, 2)
    first_other = swap(
        first_part((1 - head) * local_rows, joined_now).astype(bf16), "head", 1
    )
    first_mine = first_part(head * local_rows, joined_now)
    layer_output = (own_half(middle) + fed_own + fed_other.astype(f32)).astype(bf16)

    sums, gathers, mixer_sum, first_other, first_mine = tie(
        sums, moved, mixer_moved, first_other, first_mine
    )
    mixer_next = 0.5 * mixer_momentum[0] + mixer_sum[0]
    moved = quarter(reduce_step, sums, 1)
    gathers_moved = quarter(gather_step, gathers, 2)
    first_back = first_mine + first_other.astype(f32)
    own_normal = own_half(first_normal)
    first_gain_grad = jnp.sum(first_back * own_normal, axis=0)

    sums, gathers, first_gain_grad, first_gain = tie(
        moved, gathers_moved, first_gain_grad, norm_gains[0]
    )
    moved = quarter(reduce_step, sums, 2)
    gathers_moved = quarter(gather_step, gathers, 3)
    input_gradient = own_half(middle_grad) + norm_back(
        first_back, first_gain, own_normal, own_half(first_inverse)
    )

    sums, gathers, input_gradient = tie(moved, gathers_moved, input_gradient)
    mixer_gather = [gather_start(mixer_next.astype(bf16))]
    gain_totals = jnp.stack([first_gain_grad, second_gain_grad])
    expand_full = jnp.concatenate([gather_rows(state) for state in gathers[:2]], axis=1)
    shrink_full = gather_rows(gathers[2])

    moved = quarter(reduce_step, sums, 3)
    mixer_moved = quarter(gather_step, mixer_gather, 0, 2)
    gain_moved = total_step(gain_totals, 0)
    shrink_state = schulz_step(schulz_start(shrink_next, shrink_full))
    sums, mixer_gather, gain_totals, shrink_state, expand_full = tie(
        moved, mixer_moved, gain_moved, shrink_state, expand_full
    )
    joined_next = 0.5 * joined_momentum[0] + jnp.concatenate(sums, axis=1)
    joined_gather = [gather_start(part) for part in thirds(joined_next.astype(bf16))]

    moved = quarter(gather_step, joined_gather, 0)
    mixer_moved = quarter(gather_step, mixer_gather, 1, 2)
    gain_moved = total_step(gain_totals, 1)
    shrink_rows = schulz_step(schulz_step(shrink_state), True)
    expand_state = schulz_start(expand_next, expand_full)
    joined_gather, mixer_gather, gain_totals, shrink_rows, expand_state = tie(
        moved, mixer_moved, gain_moved, shrink_rows, expand_state
    )

    moved = quarter(gather_step, joined_gather, 1)
    mixer_moved = quarter(gather_step, mixer_gather, 2, 2)
    gain_moved = total_step(gain_totals, 2)
    expand_state = schulz_step(expand_state)
    joined_gather, mixer_gather, gain_totals, expand_state = tie(
        moved, mixer_moved, gain_moved, expand_state
    )

    moved = quarter(gather_step, joined_gather, 2)
    mixer_moved = quarter(gather_step, mixer_gather, 3, 2)
    gain_moved = total_step(gain_totals, 3)
    expand_rows = schulz_step(schulz_step(expand_state), True)
    joined_gather, mixer_gather, gain_totals, expand_rows = tie(
        moved, mixer_moved, gain_moved, expand_rows
    )

    moved = quarter(gather_step, joined_gather, 3)
    gain_totals = total_step(gain_totals, 4)
    mixer_rows = schulz_rest(schulz_start(mixer_next, gather_rows(mixer_gather[0])))
    joined_gather, mixer_rows = tie(moved, mixer_rows)
    joined_full = jnp.concatenate([gather_rows(state) for state in joined_gather], axis=1)
    joined_rows = schulz_rest(schulz_start(joined_next, joined_full))

    dp_count = lax.axis_size("dp")
    updated = []
    for weight, rows in (
        (joined_weight, joined_rows),
        (mixer_weight, mixer_rows),
        (expand_weight, expand_rows),
        (shrink_weight, shrink_rows),
    ):
        shape_scale = math.sqrt(rows.shape[0] * dp_count / rows.shape[1])
        updated.append((weight[0] - muon_rate * shape_scale * rows)[None])

    momentum_gains = 0.5 * gain_momentum + gain_totals
    updated_gains = norm_gains - gain_rate * momentum_gains * lax.rsqrt(
        jnp.mean(momentum_gains * momentum_gains, axis=-1, keepdims=True) + 1e-06
    )
    return (
        layer_output,
        input_gradient,
        joined_next[None],
        mixer_next[None],
        expand_next[None],
        shrink_next[None],
        updated[0],
        updated[1],
        updated[2],
        updated[3],
        momentum_gains,
        updated_gains,
    )


def solution(mesh):
    rows = P(("dp", "head"), None)
    weight = P("head", "dp", None)
    return jax.shard_map(
        shards,
        mesh=mesh,
        in_specs=(rows, P("dp", None), P()) + (weight,) * 8 + (P(), P("dp", None)),
        out_specs=(rows, rows) + (weight,) * 8 + (P(), P()),
        check_vma=False,
    )
```

profile of v0, /device:TPU:0, one launch (start us, length us, event | category | flops | bytes accessed | tf_op | source)
XLA Modules:
  0.0 470.2 jit_solution(7833826929219979629)
XLA Ops:
  1.7 4.1 collective-permute-start.1
  5.9 2.8 collective-permute-start.3
  18.3 5.1 %collective-permute-done.8 = bf16[1,1,1,1,72,384]{5,4,3,2,1,0:T(8,128)(2,1)S(1)} collective-permute-done((bf16[1,1,1,1,72,384]{5,4,3,2,1,0:T(8,128)(2,1)S(1)}, bf16[1,1,1,1,72,384]{5,4,3,2,1,0:T(8,128)(2,1)S(1)}, u32[]{:S(2)}, u32[]{:S(2)}) %collective-permute-start.8) | collective-permute-done | bytes 55328 | tf_op jit(solution)/shard_map/ppermute | solution.py:335
  27.8 2.8 collective-permute-done.4
  37.3 3.4 collective-permute-done.17
  45.6 3.3 fusion
  51.9 3.8 collective-permute-done.15
  56.7 3.8 fusion.174
  67.3 2.8 collective-permute-done.20
  70.2 2.6 collective-permute-done.19
  77.3 18.7 %attention_forward.1 = (bf16[384,2048]{1,0:T(8,128)(2,1)S(1)}, f32[6,2048]{1,0:T(8,128)S(1)}) custom-call(s32[8]{0:T(128)S(1)} %get-tuple-element.195.low, s32[8]{0:T(128)S(1)} %get-tuple-element.429.high, bf16[384,2048]{1,0:T(8,128)(2,1)S(1)} %bitcast.243, bf16[384,2048]{1,0:T(8,128)(2,1)S(1)} %bitcast.241, bf16[384,2048]{1,0:T(8,128)(2,1)S(1)} %slice.221.values, ...), custom_call_target="tpu_custom_call" | custom-call | tf_op jit(solution)/shard_map/attention_forward/pallas_call | solution.py:201
  107.0 4.0 fusion.74
  110.9 11.4 %multiply_convert_fusion.2 = (bf16[2048,576]{0,1:T(8,128)(2,1)}, f32[2048,576]{0,1:T(8,128)S(1)}) fusion(f32[2048,1152]{0,1:T(8,128)S(1)} %fusion.74), kind=kLoop, calls=%fused_computation.23 | loop fusion | flops 77856768 | bytes 16515072 | tf_op jit(solution)/shard_map/convert_element_type | solution.py:537
  122.3 7.9 %add_convert_fusion = (bf16[2048,576]{0,1:T(8,128)(2,1)}, bf16[2048,576]{0,1:T(8,128)(2,1)}) fusion(f32[2048,576]{0,1:T(8,128)S(1)} %get-tuple-element.322, f32[2048,1152]{0,1:T(8,128)S(1)} %fusion.74, bf16[2048,768]{1,0:T(8,128)(2,1)} %param.25, bf16[768,960]{1,0:T(8,128)(2,1)S(1)} %bitcast.257), kind=kOutput, calls=%fused_computation.22 | convolution fusion | flops 1833172992 | bytes 23003136 | tf_op jit(solution)/shard_map/dot_general | solution.py:41
  130.3 10.4 %fusion.182 = (bf16[2048,768]{0,1:T(8,128)(2,1)}, f32[2048,768]{0,1:T(8,128)}) fusion(bf16[1152,384]{1,0:T(8,128)(2,1)S(1)} %bitcast.289, bf16[1152,384]{1,0:T(8,128)(2,1)S(1)} %bitcast.291, bf16[2048,576]{0,1:T(8,128)(2,1)} %get-tuple-element.326, bf16[2048,576]{0,1:T(8,128)(2,1)} %get-tuple-element.325), kind=kOutput, calls=%fused_computation.492 | convolution fusion | flops 3638427648 | bytes 15925248 | tf_op jit(solution)/shard_map/dot_general | solution.py:41
  140.8 4.8 %copy.52 = bf16[2048,768]{0,1:T(8,128)(2,1)} copy(bf16[2048,768]{1,0:T(8,128)(2,1)} %param.25) | data formatting | bytes 6291456 | tf_op args[12]
  149.2 2.9 fusion.29
  154.0 8.3 %convolution_convert_fusion.1 = bf16[1152,768]{1,0:T(8,128)(2,1)S(1)} fusion(bf16[2048,576]{0,1:T(8,128)(2,1)} %get-tuple-element.326, bf16[2048,576]{0,1:T(8,128)(2,1)} %get-tuple-element.325, f32[2048,768]{0,1:T(8,128)} %copy-done.7, f32[768]{0:T(1024)S(1)} %get-tuple-element.312), kind=kOutput, calls=%fused_computation.40 | convolution fusion | flops 3637346304 | bytes 12782592 | tf_op jit(solution)/shard_map/dot_general | solution.py:41
  162.6 5.0 %multiply_reduce_fusion.2 = (f32[2048]{0:T(1024)S(1)}, f32[2048]{0:T(1024)S(1)}, f32[2048,768]{0,1:T(8,128)S(1)}) fusion(f32[768]{0:T(1024)S(1)} %get-tuple-element.312, f32[2048,768]{0,1:T(8,128)} %get-tuple-element.420, bf16[2048,768]{0,1:T(8,128)(2,1)} %collective-permute-done.27, f32[2048]{0:T(1024)S(1)} %add_rsqrt_fusion, f32[2048,768]{0,1:T(8,128)S(1)} %bitcast.246, ...), kind=kLoop, calls=%fused_computation.15 | loop fusion | flops 12578816 | bytes 22055936 | tf_op jit(solution)/shard_map/reduce_sum | solution.py:436
  167.7 5.7 %collective-permute-start.30 = (bf16[2,1,2,2,48,576]{5,4,3,2,1,0:T(8,128)(2,1)S(1)}, bf16[2,1,2,2,48,576]{5,4,3,2,1,0:T(8,128)(2,1)}, u32[]{:S(2)}, u32[]{:S(2)}) collective-permute-start(bf16[2,1,2,2,48,576]{5,4,3,2,1,0:T(8,128)(2,1)S(1)} %constant_dynamic-slice_fusion.25), channel_id=1, source_target_pairs={{0,8},{2,10},{4,12},{6,14},{8,0},{10,2},{12,4},{14,6},{16,24},{18,... | collective-permute-start | bytes 1327112 | tf_op jit(solution)/shard_map/ppermute | solution.py:335
  176.4 4.2 fusion.175
  180.6 3.6 convolution_convert_fusion.2.grads
  189.4 6.8 %collective-permute-done.28 = bf16[2,2,2,1,72,384]{5,4,3,2,1,0:T(8,128)(2,1)S(1)} collective-permute-done((bf16[2,2,2,1,72,384]{5,4,3,2,1,0:T(8,128)(2,1)S(1)}, bf16[2,2,2,1,72,384]{5,4,3,2,1,0:T(8,128)(2,1)S(1)}, u32[]{:S(2)}, u32[]{:S(2)}) %collective-permute-start.28) | collective-permute-done | bytes 442400 | tf_op jit(solution)/shard_map/ppermute | solution.py:335
  199.3 5.7 %collective-permute-done.33 = bf16[2,1,2,1,48,576]{5,4,3,2,1,0:T(8,128)(2,1)S(1)} collective-permute-done((bf16[2,1,2,1,48,576]{5,4,3,2,1,0:T(8,128)(2,1)S(1)}, bf16[2,1,2,1,48,576]{5,4,3,2,1,0:T(8,128)(2,1)S(1)}, u32[]{:S(2)}, u32[]{:S(2)}) %collective-permute-start.33) | collective-permute-done | bytes 221216 | tf_op jit(solution)/shard_map/ppermute | solution.py:335
  209.7 2.5 convolution_convert_fusion.3
  220.6 35.7 %attention_backward.1 = (f32[384,2048]{1,0:T(8,128)}, f32[384,2048]{1,0:T(8,128)}, f32[384,2048]{1,0:T(8,128)}) custom-call(s32[8]{0:T(128)S(1)} %get-tuple-element.195.low, s32[8]{0:T(128)S(1)} %get-tuple-element.429.high, bf16[384,2048]{1,0:T(8,128)(2,1)S(1)} %bitcast.244, bf16[384,2048]{1,0:T(8,128)(2,1)} %bitcast.242, bf16[384,2048]{1,0:T(8,128)(2,1)} %copy-done, ...), custom_call_target="tpu_custom_call" | custom-call | tf_op jit(solution)/shard_map/attention_backward/pallas_call | solution.py:306
  259.5 2.9 subtract_convert_fusion.1
  264.7 3.9 convolution_convert_fusion
  268.6 8.0 %collective-permute-start.46 = (bf16[2,1,1,1,48,384]{5,4,3,2,1,0:T(8,128)(2,1)S(1)}, bf16[2,1,1,1,48,384]{5,4,3,2,1,0:T(8,128)(2,1)S(1)}, u32[]{:S(2)}, u32[]{:S(2)}) collective-permute-start(bf16[2,1,1,1,48,384]{5,4,3,2,1,0:T(8,128)(2,1)S(1)} %constant_dynamic-slice_fusion.13), channel_id=1, source_target_pairs={{0,4},{2,6},{4,0},{6,2},{8,12},{10,14},{12,8},{14,10},{16,20},{18,... | collective-permute-start | bytes 221192 | tf_op jit(solution)/shard_map/ppermute | solution.py:335
  277.2 5.5 %collective-permute-start.45 = (bf16[1,1,1,1,48,576]{5,4,3,2,1,0:T(8,128)(2,1)S(1)}, bf16[1,1,1,1,48,576]{5,4,3,2,1,0:T(8,128)(2,1)S(1)}, u32[]{:S(2)}, u32[]{:S(2)}) collective-permute-start(bf16[1,1,1,1,48,576]{5,4,3,2,1,0:T(8,128)(2,1)S(1)} %get-tuple-element.377), channel_id=1, source_target_pairs={{0,16},{2,18},{4,20},{6,22},{8,24},{10,26},{12,28},{14,30},{16,0},... | collective-permute-start | bytes 165896 | tf_op jit(solution)/shard_map/ppermute | solution.py:335
  282.8 2.9 collective-permute-start.43
  291.2 3.9 fusion.15
  295.2 3.4 fusion.25
  299.3 4.5 collective-permute-done.53
  310.4 4.6 collective-permute-done.49
  317.5 4.0 add_convert_fusion.1
  321.5 2.6 copy.57
  324.0 2.5 copy.56
  335.6 3.0 multiply_reduce_fusion.4
  344.0 2.5 collective-permute-done.55
  351.8 4.0 multiply_add_fusion.1
  377.8 3.7 copy.58
  385.2 3.8 select_reduce_fusion.1
  400.5 4.3 fusion.75
  421.6 3.0 multiply_add_fusion.6
  431.4 4.5 fusion.71
  450.6 3.8 select_reduce_fusion
  455.1 4.3 add_convert_fusion.4
  (573 shorter events, 206.2 us)
Async XLA Ops:
  1.7 11.4 %collective-permute-start.1 = (bf16[1,1,1,1,72,256]{5,4,3,2,1,0:T(8,128)(2,1)S(1)}, bf16[1,1,1,1,72,256]{5,4,3,2,1,0:T(8,128)(2,1)S(1)}, u32[]{:S(2)}, u32[]{:S(2)}) collective-permute-start(bf16[1,1,1,1,72,256]{5,4,3,2,1,0:T(8,128)(2,1)S(1)} %get-tuple-element.415), channel_id=1, source_target_pairs={{0,16},{2,18},{4,20},{6,22},{8,24},{10,26},{12,28},{14,30},{16,0},... | collective-permute-start | bytes 110600 | tf_op jit(solution)/shard_map/ppermute | solution.py:335
  10.5 32.1 %collective-permute-start = (bf16[1024,768]{0,1:T(8,128)(2,1)S(1)}, bf16[1024,768]{0,1:T(8,128)(2,1)}, u32[]{:S(2)}, u32[]{:S(2)}) collective-permute-start(bf16[1024,768]{0,1:T(8,128)(2,1)S(1)} %copy.49), channel_id=1, source_target_pairs={{0,1},{1,0},{2,3},{3,2},{4,5},{5,4},{6,7},{7,6},{8,9},{9,8},{10,11... | collective-permute-start | bytes 4718600 | tf_op jit(solution)/shard_map/ppermute | solution.py:335
  13.2 10.2 %collective-permute-start.8 = (bf16[1,1,1,1,72,384]{5,4,3,2,1,0:T(8,128)(2,1)S(1)}, bf16[1,1,1,1,72,384]{5,4,3,2,1,0:T(8,128)(2,1)S(1)}, u32[]{:S(2)}, u32[]{:S(2)}) collective-permute-start(bf16[1,1,1,1,72,384]{5,4,3,2,1,0:T(8,128)(2,1)S(1)} %get-tuple-element.146), channel_id=1, source_target_pairs={{0,16},{2,18},{4,20},{6,22},{8,24},{10,26},{12,28},{14,30},{16,0},... | collective-permute-start | bytes 165896 | tf_op jit(solution)/shard_map/ppermute | solution.py:335
  13.8 16.8 %collective-permute-start.9 = (bf16[1,1,1,1,48,960]{5,4,3,2,1,0:T(8,128)(2,1)S(1)}, bf16[1,1,1,1,48,960]{5,4,3,2,1,0:T(8,128)(2,1)S(1)}, u32[]{:S(2)}, u32[]{:S(2)}) collective-permute-start(bf16[1,1,1,1,48,960]{5,4,3,2,1,0:T(8,128)(2,1)S(1)} %pad_maximum_fusion.58), channel_id=1, source_target_pairs={{0,16},{2,18},{4,20},{6,22},{8,24},{10,26},{12,28},{14,30},{16,0},... | collective-permute-start | bytes 276488 | tf_op jit(solution)/shard_map/ppermute | solution.py:335
  16.3 9.9 %collective-permute-start.7 = (bf16[1,1,1,1,72,384]{5,4,3,2,1,0:T(8,128)(2,1)S(1)}, bf16[1,1,1,1,72,384]{5,4,3,2,1,0:T(8,128)(2,1)S(1)}, u32[]{:S(2)}, u32[]{:S(2)}) collective-permute-start(bf16[1,1,1,1,72,384]{5,4,3,2,1,0:T(8,128)(2,1)S(1)} %get-tuple-element.145), channel_id=1, source_target_pairs={{0,16},{2,18},{4,20},{6,22},{8,24},{10,26},{12,28},{14,30},{16,0},... | collective-permute-start | bytes 165896 | tf_op jit(solution)/shard_map/ppermute | solution.py:335
  16.8 9.5 %collective-permute-start.6 = (bf16[2,1,1,1,72,256]{5,4,3,2,1,0:T(8,128)(2,1)S(1)}, bf16[2,1,1,1,72,256]{5,4,3,2,1,0:T(8,128)(2,1)S(1)}, u32[]{:S(2)}, u32[]{:S(2)}) collective-permute-start(bf16[2,1,1,1,72,256]{5,4,3,2,1,0:T(8,128)(2,1)S(1)} %pad_maximum_fusion.61), channel_id=1, source_target_pairs={{0,4},{2,6},{4,0},{6,2},{8,12},{10,14},{12,8},{14,10},{16,20},{18,... | collective-permute-start | bytes 221192 | tf_op jit(solution)/shard_map/ppermute | solution.py:335
  30.8 11.5 %collective-permute-start.12 = (bf16[2,1,2,1,72,256]{5,4,3,2,1,0:T(8,128)(2,1)S(1)}, bf16[2,1,2,1,72,256]{5,4,3,2,1,0:T(8,128)(2,1)S(1)}, u32[]{:S(2)}, u32[]{:S(2)}) collective-permute-start(bf16[2,1,2,1,72,256]{5,4,3,2,1,0:T(8,128)(2,1)S(1)} %pad_maximum_fusion.48), channel_id=1, source_target_pairs={{0,2},{2,0},{4,6},{6,4},{8,10},{10,8},{12,14},{14,12},{16,18},{18,... | collective-permute-start | bytes 442376 | tf_op jit(solution)/shard_map/ppermute | solution.py:335
  32.4 10.0 %collective-permute-start.11 = (bf16[2,1,1,2,72,256]{5,4,3,2,1,0:T(8,128)(2,1)S(1)}, bf16[2,1,1,2,72,256]{5,4,3,2,1,0:T(8,128)(2,1)S(1)}, u32[]{:S(2)}, u32[]{:S(2)}) collective-permute-start(bf16[2,1,1,2,72,256]{5,4,3,2,1,0:T(8,128)(2,1)S(1)} %pad_maximum_fusion.47), channel_id=1, source_target_pairs={{0,8},{2,10},{4,12},{6,14},{8,0},{10,2},{12,4},{14,6},{16,24},{18,... | collective-permute-start | bytes 442376 | tf_op jit(solution)/shard_map/ppermute | solution.py:335
  34.4 8.1 %collective-permute-start.10 = (bf16[2,2,1,1,72,256]{5,4,3,2,1,0:T(8,128)(2,1)S(1)}, bf16[2,2,1,1,72,256]{5,4,3,2,1,0:T(8,128)(2,1)S(1)}, u32[]{:S(2)}, u32[]{:S(2)}) collective-permute-start(bf16[2,2,1,1,72,256]{5,4,3,2,1,0:T(8,128)(2,1)S(1)} %pad_maximum_fusion.46), channel_id=1, source_target_pairs={{0,4},{2,6},{4,0},{6,2},{8,12},{10,14},{12,8},{14,10},{16,20},{18,... | collective-permute-start | bytes 442376 | tf_op jit(solution)/shard_map/ppermute | solution.py:335
  40.7 8.4 %collective-permute-start.18 = (bf16[2,1,1,1,48,960]{5,4,3,2,1,0:T(8,128)(2,1)S(1)}, bf16[2,1,1,1,48,960]{5,4,3,2,1,0:T(8,128)(2,1)S(1)}, u32[]{:S(2)}, u32[]{:S(2)}) collective-permute-start(bf16[2,1,1,1,48,960]{5,4,3,2,1,0:T(8,128)(2,1)S(1)} %pad_maximum_fusion.45), channel_id=1, source_target_pairs={{0,4},{2,6},{4,0},{6,2},{8,12},{10,14},{12,8},{14,10},{16,20},{18,... | collective-permute-start | bytes 552968 | tf_op jit(solution)/shard_map/ppermute | solution.py:335
  61.2 11.6 %collective-permute-start.21 = (bf16[2,1,2,1,48,960]{5,4,3,2,1,0:T(8,128)(2,1)S(1)}, bf16[2,1,2,1,48,960]{5,4,3,2,1,0:T(8,128)(2,1)S(1)}, u32[]{:S(2)}, u32[]{:S(2)}) collective-permute-start(bf16[2,1,2,1,48,960]{5,4,3,2,1,0:T(8,128)(2,1)S(1)} %pad_maximum_fusion.32), channel_id=1, source_target_pairs={{0,2},{2,0},{4,6},{6,4},{8,10},{10,8},{12,14},{14,12},{16,18},{18,... | collective-permute-start | bytes 1105928 | tf_op jit(solution)/shard_map/ppermute | solution.py:335
  64.4 8.3 %collective-permute-start.19 = (bf16[2,2,1,1,72,384]{5,4,3,2,1,0:T(8,128)(2,1)S(1)}, bf16[2,2,1,1,72,384]{5,4,3,2,1,0:T(8,128)(2,1)S(1)}, u32[]{:S(2)}, u32[]{:S(2)}) collective-permute-start(bf16[2,2,1,1,72,384]{5,4,3,2,1,0:T(8,128)(2,1)S(1)} %pad_maximum_fusion.41), channel_id=1, source_target_pairs={{0,4},{2,6},{4,0},{6,2},{8,12},{10,14},{12,8},{14,10},{16,20},{18,... | collective-permute-start | bytes 663560 | tf_op jit(solution)/shard_map/ppermute | solution.py:335
  73.0 23.0 %collective-permute-start.23 = (bf16[2,2,1,2,72,384]{5,4,3,2,1,0:T(8,128)(2,1)S(1)}, bf16[2,2,1,2,72,384]{5,4,3,2,1,0:T(8,128)(2,1)S(1)}, u32[]{:S(2)}, u32[]{:S(2)}) collective-permute-start(bf16[2,2,1,2,72,384]{5,4,3,2,1,0:T(8,128)(2,1)S(1)} %pad_maximum_fusion.29), channel_id=1, source_target_pairs={{0,4},{2,6},{4,0},{6,2},{8,12},{10,14},{12,8},{14,10},{16,20},{18,... | collective-permute-start | bytes 1327112 | tf_op jit(solution)/shard_map/ppermute | solution.py:335
  74.7 21.6 %collective-permute-start.22 = (bf16[2,2,2,1,72,384]{5,4,3,2,1,0:T(8,128)(2,1)S(1)}, bf16[2,2,2,1,72,384]{5,4,3,2,1,0:T(8,128)(2,1)S(1)}, u32[]{:S(2)}, u32[]{:S(2)}) collective-permute-start(bf16[2,2,2,1,72,384]{5,4,3,2,1,0:T(8,128)(2,1)S(1)} %pad_maximum_fusion.28), channel_id=1, source_target_pairs={{0,2},{2,0},{4,6},{6,4},{8,10},{10,8},{12,14},{14,12},{16,18},{18,... | collective-permute-start | bytes 1327112 | tf_op jit(solution)/shard_map/ppermute | solution.py:335
  76.5 20.0 %collective-permute-start.24 = (bf16[2,1,2,2,48,960]{5,4,3,2,1,0:T(8,128)(2,1)S(1)}, bf16[2,1,2,2,48,960]{5,4,3,2,1,0:T(8,128)(2,1)S(1)}, u32[]{:S(2)}, u32[]{:S(2)}) collective-permute-start(bf16[2,1,2,2,48,960]{5,4,3,2,1,0:T(8,128)(2,1)S(1)} %pad_maximum_fusion.19), channel_id=1, source_target_pairs={{0,8},{2,10},{4,12},{6,14},{8,0},{10,2},{12,4},{14,6},{16,24},{18,... | collective-permute-start | bytes 2211848 | tf_op jit(solution)/shard_map/ppermute | solution.py:335
  140.7 21.8 %collective-permute-start.27 = (bf16[2048,768]{0,1:T(8,128)(2,1)}, bf16[2048,768]{0,1:T(8,128)(2,1)}, u32[]{:S(2)}, u32[]{:S(2)}) collective-permute-start(bf16[2048,768]{0,1:T(8,128)(2,1)} %get-tuple-element.419), channel_id=1, source_target_pairs={{0,1},{1,0},{2,3},{3,2},{4,5},{5,4},{6,7},{7,6},{8,9},{9,8},{10,11... | collective-permute-start | bytes 9437192 | tf_op jit(solution)/shard_map/ppermute | solution.py:335
  167.7 20.5 %collective-permute-start.30 = (bf16[2,1,2,2,48,576]{5,4,3,2,1,0:T(8,128)(2,1)S(1)}, bf16[2,1,2,2,48,576]{5,4,3,2,1,0:T(8,128)(2,1)}, u32[]{:S(2)}, u32[]{:S(2)}) collective-permute-start(bf16[2,1,2,2,48,576]{5,4,3,2,1,0:T(8,128)(2,1)S(1)} %constant_dynamic-slice_fusion.25), channel_id=1, source_target_pairs={{0,8},{2,10},{4,12},{6,14},{8,0},{10,2},{12,4},{14,6},{16,24},{18,... | collective-permute-start | bytes 1327112 | tf_op jit(solution)/shard_map/ppermute | solution.py:335
  174.2 12.8 %collective-permute-start.29 = (bf16[2,2,1,2,72,384]{5,4,3,2,1,0:T(8,128)(2,1)}, bf16[2,2,1,2,72,384]{5,4,3,2,1,0:T(8,128)(2,1)}, u32[]{:S(2)}, u32[]{:S(2)}) collective-permute-start(bf16[2,2,1,2,72,384]{5,4,3,2,1,0:T(8,128)(2,1)} %constant_dynamic-slice_fusion.26), channel_id=1, source_target_pairs={{0,4},{2,6},{4,0},{6,2},{8,12},{10,14},{12,8},{14,10},{16,20},{18,... | collective-permute-start | bytes 1327112 | tf_op jit(solution)/shard_map/ppermute | solution.py:335
  184.3 11.9 %collective-permute-start.28 = (bf16[2,2,2,1,72,384]{5,4,3,2,1,0:T(8,128)(2,1)S(1)}, bf16[2,2,2,1,72,384]{5,4,3,2,1,0:T(8,128)(2,1)S(1)}, u32[]{:S(2)}, u32[]{:S(2)}) collective-permute-start(bf16[2,2,2,1,72,384]{5,4,3,2,1,0:T(8,128)(2,1)S(1)} %constant_dynamic-slice_fusion.27), channel_id=1, source_target_pairs={{0,2},{2,0},{4,6},{6,4},{8,10},{10,8},{12,14},{14,12},{16,18},{18,... | collective-permute-start | bytes 1327112 | tf_op jit(solution)/shard_map/ppermute | solution.py:335
  205.3 9.5 %collective-permute-start.37 = (bf16[2,1,2,2,48,384]{5,4,3,2,1,0:T(8,128)(2,1)S(1)}, bf16[2,1,2,2,48,384]{5,4,3,2,1,0:T(8,128)(2,1)S(1)}, u32[]{:S(2)}, u32[]{:S(2)}) collective-permute-start(bf16[2,1,2,2,48,384]{5,4,3,2,1,0:T(8,128)(2,1)S(1)} %constant_dynamic-slice_fusion.18), channel_id=1, source_target_pairs={{0,8},{2,10},{4,12},{6,14},{8,0},{10,2},{12,4},{14,6},{16,24},{18,... | collective-permute-start | bytes 884744 | tf_op jit(solution)/shard_map/ppermute | solution.py:335
  214.9 41.6 %collective-permute-start.42 = (bf16[2,1,2,1,48,384]{5,4,3,2,1,0:T(8,128)(2,1)S(1)}, bf16[2,1,2,1,48,384]{5,4,3,2,1,0:T(8,128)(2,1)S(1)}, u32[]{:S(2)}, u32[]{:S(2)}) collective-permute-start(bf16[2,1,2,1,48,384]{5,4,3,2,1,0:T(8,128)(2,1)S(1)} %constant_dynamic-slice_fusion.14), channel_id=1, source_target_pairs={{0,2},{2,0},{4,6},{6,4},{8,10},{10,8},{12,14},{14,12},{16,18},{18,... | collective-permute-start | bytes 442376 | tf_op jit(solution)/shard_map/ppermute | solution.py:335
  216.2 40.2 %collective-permute-start.41 = (bf16[1,1,1,1,48,576]{5,4,3,2,1,0:T(8,128)(2,1)S(1)}, bf16[1,1,1,1,48,576]{5,4,3,2,1,0:T(8,128)(2,1)S(1)}, u32[]{:S(2)}, u32[]{:S(2)}) collective-permute-start(bf16[1,1,1,1,48,576]{5,4,3,2,1,0:T(8,128)(2,1)S(1)} %constant_dynamic-slice_fusion.15), channel_id=1, source_target_pairs={{0,16},{2,18},{4,20},{6,22},{8,24},{10,26},{12,28},{14,30},{16,0},... | collective-permute-start | bytes 165896 | tf_op jit(solution)/shard_map/ppermute | solution.py:335
  217.7 38.7 %collective-permute-start.40 = (bf16[1,1,1,1,72,384]{5,4,3,2,1,0:T(8,128)(2,1)S(1)}, bf16[1,1,1,1,72,384]{5,4,3,2,1,0:T(8,128)(2,1)S(1)}, u32[]{:S(2)}, u32[]{:S(2)}) collective-permute-start(bf16[1,1,1,1,72,384]{5,4,3,2,1,0:T(8,128)(2,1)S(1)} %constant_dynamic-slice_fusion.16), channel_id=1, source_target_pairs={{0,16},{2,18},{4,20},{6,22},{8,24},{10,26},{12,28},{14,30},{16,0},... | collective-permute-start | bytes 165896 | tf_op jit(solution)/shard_map/ppermute | solution.py:335
  219.1 37.4 %collective-permute-start.39 = (bf16[1,1,1,1,72,384]{5,4,3,2,1,0:T(8,128)(2,1)S(1)}, bf16[1,1,1,1,72,384]{5,4,3,2,1,0:T(8,128)(2,1)S(1)}, u32[]{:S(2)}, u32[]{:S(2)}) collective-permute-start(bf16[1,1,1,1,72,384]{5,4,3,2,1,0:T(8,128)(2,1)S(1)} %constant_dynamic-slice_fusion.17), channel_id=1, source_target_pairs={{0,16},{2,18},{4,20},{6,22},{8,24},{10,26},{12,28},{14,30},{16,0},... | collective-permute-start | bytes 165896 | tf_op jit(solution)/shard_map/ppermute | solution.py:335
  220.6 96.8 %collective-permute-start.38 = (bf16[1024,768]{0,1:T(8,128)(2,1)}, bf16[1024,768]{0,1:T(8,128)(2,1)}, u32[]{:S(2)}, u32[]{:S(2)}) collective-permute-start(bf16[1024,768]{0,1:T(8,128)(2,1)} %convolution_convert_fusion.3), channel_id=1, source_target_pairs={{0,1},{1,0},{2,3},{3,2},{4,5},{5,4},{6,7},{7,6},{8,9},{9,8},{10,11... | collective-permute-start | bytes 4718600 | tf_op jit(solution)/shard_map/ppermute | solution.py:335
  268.6 22.6 %collective-permute-start.46 = (bf16[2,1,1,1,48,384]{5,4,3,2,1,0:T(8,128)(2,1)S(1)}, bf16[2,1,1,1,48,384]{5,4,3,2,1,0:T(8,128)(2,1)S(1)}, u32[]{:S(2)}, u32[]{:S(2)}) collective-permute-start(bf16[2,1,1,1,48,384]{5,4,3,2,1,0:T(8,128)(2,1)S(1)} %constant_dynamic-slice_fusion.13), channel_id=1, source_target_pairs={{0,4},{2,6},{4,0},{6,2},{8,12},{10,14},{12,8},{14,10},{16,20},{18,... | collective-permute-start | bytes 221192 | tf_op jit(solution)/shard_map/ppermute | solution.py:335
  277.2 11.1 %collective-permute-start.45 = (bf16[1,1,1,1,48,576]{5,4,3,2,1,0:T(8,128)(2,1)S(1)}, bf16[1,1,1,1,48,576]{5,4,3,2,1,0:T(8,128)(2,1)S(1)}, u32[]{:S(2)}, u32[]{:S(2)}) collective-permute-start(bf16[1,1,1,1,48,576]{5,4,3,2,1,0:T(8,128)(2,1)S(1)} %get-tuple-element.377), channel_id=1, source_target_pairs={{0,16},{2,18},{4,20},{6,22},{8,24},{10,26},{12,28},{14,30},{16,0},... | collective-permute-start | bytes 165896 | tf_op jit(solution)/shard_map/ppermute | solution.py:335
  282.8 8.3 %collective-permute-start.43 = (bf16[1,1,1,1,72,384]{5,4,3,2,1,0:T(8,128)(2,1)S(1)}, bf16[1,1,1,1,72,384]{5,4,3,2,1,0:T(8,128)(2,1)S(1)}, u32[]{:S(2)}, u32[]{:S(2)}) collective-permute-start(bf16[1,1,1,1,72,384]{5,4,3,2,1,0:T(8,128)(2,1)S(1)} %get-tuple-element.402), channel_id=1, source_target_pairs={{0,16},{2,18},{4,20},{6,22},{8,24},{10,26},{12,28},{14,30},{16,0},... | collective-permute-start | bytes 165896 | tf_op jit(solution)/shard_map/ppermute | solution.py:335
  298.6 25.5 %collective-permute-start.54 = (bf16[1024,768]{0,1:T(8,128)(2,1)}, bf16[1024,768]{0,1:T(8,128)(2,1)}, u32[]{:S(2)}, u32[]{:S(2)}) collective-permute-start(bf16[1024,768]{0,1:T(8,128)(2,1)} %fusion.25), channel_id=1, source_target_pairs={{0,1},{1,0},{2,3},{3,2},{4,5},{5,4},{6,7},{7,6},{8,9},{9,8},{10,11... | collective-permute-start | bytes 4718600 | tf_op jit(solution)/shard_map/ppermute | solution.py:335
  299.0 8.5 %collective-permute-start.51 = (bf16[2,1,1,1,72,384]{5,4,3,2,1,0:T(8,128)(2,1)S(1)}, bf16[2,1,1,1,72,384]{5,4,3,2,1,0:T(8,128)(2,1)S(1)}, u32[]{:S(2)}, u32[]{:S(2)}) collective-permute-start(bf16[2,1,1,1,72,384]{5,4,3,2,1,0:T(8,128)(2,1)S(1)} %pad_maximum_fusion.57), channel_id=1, source_target_pairs={{0,2},{2,0},{4,6},{6,4},{8,10},{10,8},{12,14},{14,12},{16,18},{18,... | collective-permute-start | bytes 331784 | tf_op jit(solution)/shard_map/ppermute | solution.py:335
  304.4 10.6 %collective-permute-start.49 = (bf16[2,1,2,2,72,256]{5,4,3,2,1,0:T(8,128)(2,1)S(1)}, bf16[2,1,2,2,72,256]{5,4,3,2,1,0:T(8,128)(2,1)S(1)}, u32[]{:S(2)}, u32[]{:S(2)}) collective-permute-start(bf16[2,1,2,2,72,256]{5,4,3,2,1,0:T(8,128)(2,1)S(1)} %constant_dynamic-slice_fusion.10), channel_id=1, source_target_pairs={{0,8},{2,10},{4,12},{6,14},{8,0},{10,2},{12,4},{14,6},{16,24},{18,... | collective-permute-start | bytes 884744 | tf_op jit(solution)/shard_map/ppermute | solution.py:335
  307.6 8.2 %collective-permute-start.48 = (bf16[2,2,1,2,72,256]{5,4,3,2,1,0:T(8,128)(2,1)S(1)}, bf16[2,2,1,2,72,256]{5,4,3,2,1,0:T(8,128)(2,1)S(1)}, u32[]{:S(2)}, u32[]{:S(2)}) collective-permute-start(bf16[2,2,1,2,72,256]{5,4,3,2,1,0:T(8,128)(2,1)S(1)} %constant_dynamic-slice_fusion.11), channel_id=1, source_target_pairs={{0,4},{2,6},{4,0},{6,2},{8,12},{10,14},{12,8},{14,10},{16,20},{18,... | collective-permute-start | bytes 884744 | tf_op jit(solution)/shard_map/ppermute | solution.py:335
  326.6 20.0 %collective-permute-start.60 = (bf16[2,1,2,1,48,576]{5,4,3,2,1,0:T(8,128)(2,1)}, bf16[2,1,2,1,48,576]{5,4,3,2,1,0:T(8,128)(2,1)S(1)}, u32[]{:S(2)}, u32[]{:S(2)}) collective-permute-start(bf16[2,1,2,1,48,576]{5,4,3,2,1,0:T(8,128)(2,1)} %pad_maximum_fusion.40), channel_id=1, source_target_pairs={{0,2},{2,0},{4,6},{6,4},{8,10},{10,8},{12,14},{14,12},{16,18},{18,... | collective-permute-start | bytes 663560 | tf_op jit(solution)/shard_map/ppermute | solution.py:335
  327.0 19.6 %collective-permute-start.59 = (bf16[2,1,1,2,72,384]{5,4,3,2,1,0:T(8,128)(2,1)}, bf16[2,1,1,2,72,384]{5,4,3,2,1,0:T(8,128)(2,1)S(1)}, u32[]{:S(2)}, u32[]{:S(2)}) collective-permute-start(bf16[2,1,1,2,72,384]{5,4,3,2,1,0:T(8,128)(2,1)} %pad_maximum_fusion.44), channel_id=1, source_target_pairs={{0,8},{2,10},{4,12},{6,14},{8,0},{10,2},{12,4},{14,6},{16,24},{18,... | collective-permute-start | bytes 663560 | tf_op jit(solution)/shard_map/ppermute | solution.py:335
  327.5 19.2 %collective-permute-start.58 = (bf16[2,2,1,1,72,384]{5,4,3,2,1,0:T(8,128)(2,1)}, bf16[2,2,1,1,72,384]{5,4,3,2,1,0:T(8,128)(2,1)S(1)}, u32[]{:S(2)}, u32[]{:S(2)}) collective-permute-start(bf16[2,2,1,1,72,384]{5,4,3,2,1,0:T(8,128)(2,1)} %pad_maximum_fusion.43), channel_id=1, source_target_pairs={{0,4},{2,6},{4,0},{6,2},{8,12},{10,14},{12,8},{14,10},{16,20},{18,... | collective-permute-start | bytes 663560 | tf_op jit(solution)/shard_map/ppermute | solution.py:335
  329.4 11.9 %collective-permute-start.57 = (bf16[2,1,2,1,72,256]{5,4,3,2,1,0:T(8,128)(2,1)S(1)}, bf16[2,1,2,1,72,256]{5,4,3,2,1,0:T(8,128)(2,1)S(1)}, u32[]{:S(2)}, u32[]{:S(2)}) collective-permute-start(bf16[2,1,2,1,72,256]{5,4,3,2,1,0:T(8,128)(2,1)S(1)} %constant_dynamic-slice_fusion.6), channel_id=1, source_target_pairs={{0,2},{2,0},{4,6},{6,4},{8,10},{10,8},{12,14},{14,12},{16,18},{18,... | collective-permute-start | bytes 442376 | tf_op jit(solution)/shard_map/ppermute | solution.py:335
  349.2 14.4 %collective-permute-start.66 = (bf16[2,1,2,2,48,576]{5,4,3,2,1,0:T(8,128)(2,1)S(1)}, bf16[2,1,2,2,48,576]{5,4,3,2,1,0:T(8,128)(2,1)S(1)}, u32[]{:S(2)}, u32[]{:S(2)}) collective-permute-start(bf16[2,1,2,2,48,576]{5,4,3,2,1,0:T(8,128)(2,1)S(1)} %pad_maximum_fusion.27), channel_id=1, source_target_pairs={{0,8},{2,10},{4,12},{6,14},{8,0},{10,2},{12,4},{14,6},{16,24},{18,... | collective-permute-start | bytes 1327112 | tf_op jit(solution)/shard_map/ppermute | solution.py:335
  349.3 14.1 %collective-permute-start.65 = (bf16[2,2,1,2,72,384]{5,4,3,2,1,0:T(8,128)(2,1)S(1)}, bf16[2,2,1,2,72,384]{5,4,3,2,1,0:T(8,128)(2,1)S(1)}, u32[]{:S(2)}, u32[]{:S(2)}) collective-permute-start(bf16[2,2,1,2,72,384]{5,4,3,2,1,0:T(8,128)(2,1)S(1)} %pad_maximum_fusion.31), channel_id=1, source_target_pairs={{0,4},{2,6},{4,0},{6,2},{8,12},{10,14},{12,8},{14,10},{16,20},{18,... | collective-permute-start | bytes 1327112 | tf_op jit(solution)/shard_map/ppermute | solution.py:335
  350.2 13.4 %collective-permute-start.64 = (bf16[2,2,2,1,72,384]{5,4,3,2,1,0:T(8,128)(2,1)S(1)}, bf16[2,2,2,1,72,384]{5,4,3,2,1,0:T(8,128)(2,1)S(1)}, u32[]{:S(2)}, u32[]{:S(2)}) collective-permute-start(bf16[2,2,2,1,72,384]{5,4,3,2,1,0:T(8,128)(2,1)S(1)} %pad_maximum_fusion.30), channel_id=1, source_target_pairs={{0,2},{2,0},{4,6},{6,4},{8,10},{10,8},{12,14},{14,12},{16,18},{18,... | collective-permute-start | bytes 1327112 | tf_op jit(solution)/shard_map/ppermute | solution.py:335
  370.1 11.4 %collective-permute-start.69 = (bf16[1,1,1,1,72,256]{5,4,3,2,1,0:T(8,128)(2,1)}, bf16[1,1,1,1,72,256]{5,4,3,2,1,0:T(8,128)(2,1)}, u32[]{:S(2)}, u32[]{:S(2)}) collective-permute-start(bf16[1,1,1,1,72,256]{5,4,3,2,1,0:T(8,128)(2,1)} %constant_dynamic-slice_fusion), channel_id=1, source_target_pairs={{0,16},{2,18},{4,20},{6,22},{8,24},{10,26},{12,28},{14,30},{16,0},... | collective-permute-start | bytes 110600 | tf_op jit(solution)/shard_map/ppermute | solution.py:335
  372.8 9.5 %collective-permute-start.68 = (bf16[1,1,1,1,72,256]{5,4,3,2,1,0:T(8,128)(2,1)}, bf16[1,1,1,1,72,256]{5,4,3,2,1,0:T(8,128)(2,1)}, u32[]{:S(2)}, u32[]{:S(2)}) collective-permute-start(bf16[1,1,1,1,72,256]{5,4,3,2,1,0:T(8,128)(2,1)} %constant_dynamic-slice_fusion.1), channel_id=1, source_target_pairs={{0,16},{2,18},{4,20},{6,22},{8,24},{10,26},{12,28},{14,30},{16,0},... | collective-permute-start | bytes 110600 | tf_op jit(solution)/shard_map/ppermute | solution.py:335
  395.3 10.3 %collective-permute-start.76 = (f32[2,768]{1,0:T(2,128)S(1)}, f32[2,768]{1,0:T(2,128)S(1)}, u32[]{:S(2)}, u32[]{:S(2)}) collective-permute-start(f32[2,768]{1,0:T(2,128)S(1)} %fusion.166), channel_id=1, source_target_pairs={{0,2},{2,0},{4,6},{6,4},{8,10},{10,8},{12,14},{14,12},{16,18},{18,... | collective-permute-start | bytes 18440 | tf_op jit(solution)/shard_map/ppermute | solution.py:335
  395.6 10.1 %collective-permute-start.75 = (bf16[2,1,1,1,48,384]{5,4,3,2,1,0:T(8,128)(2,1)S(1)}, bf16[2,1,1,1,48,384]{5,4,3,2,1,0:T(8,128)(2,1)}, u32[]{:S(2)}, u32[]{:S(2)}) collective-permute-start(bf16[2,1,1,1,48,384]{5,4,3,2,1,0:T(8,128)(2,1)S(1)} %copy-done.54), channel_id=1, source_target_pairs={{0,4},{2,6},{4,0},{6,2},{8,12},{10,14},{12,8},{14,10},{16,20},{18,... | collective-permute-start | bytes 221192 | tf_op jit(solution)/shard_map/ppermute | solution.py:335
  396.0 9.6 %collective-permute-start.74 = (bf16[1,1,1,1,72,256]{5,4,3,2,1,0:T(8,128)(2,1)S(1)}, bf16[1,1,1,1,72,256]{5,4,3,2,1,0:T(8,128)(2,1)S(1)}, u32[]{:S(2)}, u32[]{:S(2)}) collective-permute-start(bf16[1,1,1,1,72,256]{5,4,3,2,1,0:T(8,128)(2,1)S(1)} %get-tuple-element.398), channel_id=1, source_target_pairs={{0,16},{2,18},{4,20},{6,22},{8,24},{10,26},{12,28},{14,30},{16,0},... | collective-permute-start | bytes 110600 | tf_op jit(solution)/shard_map/ppermute | solution.py:335
  397.5 8.1 %collective-permute-start.73 = (bf16[1,1,1,1,72,256]{5,4,3,2,1,0:T(8,128)(2,1)S(1)}, bf16[1,1,1,1,72,256]{5,4,3,2,1,0:T(8,128)(2,1)S(1)}, u32[]{:S(2)}, u32[]{:S(2)}) collective-permute-start(bf16[1,1,1,1,72,256]{5,4,3,2,1,0:T(8,128)(2,1)S(1)} %get-tuple-element.399), channel_id=1, source_target_pairs={{0,16},{2,18},{4,20},{6,22},{8,24},{10,26},{12,28},{14,30},{16,0},... | collective-permute-start | bytes 110600 | tf_op jit(solution)/shard_map/ppermute | solution.py:335
  424.6 11.3 %collective-permute-start.86 = (f32[2,768]{1,0:T(2,128)S(1)}, f32[2,768]{1,0:T(2,128)S(1)}, u32[]{:S(2)}, u32[]{:S(2)}) collective-permute-start(f32[2,768]{1,0:T(2,128)S(1)} %add.495), channel_id=1, source_target_pairs={{0,8},{2,10},{4,12},{6,14},{8,0},{10,2},{12,4},{14,6},{16,24},{18,... | collective-permute-start | bytes 18440 | tf_op jit(solution)/shard_map/ppermute | solution.py:335
  426.1 9.9 %collective-permute-start.85 = (bf16[2,1,2,2,48,384]{5,4,3,2,1,0:T(8,128)(2,1)S(1)}, bf16[2,1,2,2,48,384]{5,4,3,2,1,0:T(8,128)(2,1)S(1)}, u32[]{:S(2)}, u32[]{:S(2)}) collective-permute-start(bf16[2,1,2,2,48,384]{5,4,3,2,1,0:T(8,128)(2,1)S(1)} %pad_maximum_fusion.36), channel_id=1, source_target_pairs={{0,8},{2,10},{4,12},{6,14},{8,0},{10,2},{12,4},{14,6},{16,24},{18,... | collective-permute-start | bytes 884744 | tf_op jit(solution)/shard_map/ppermute | solution.py:335
  426.6 9.3 %collective-permute-start.84 = (bf16[2,1,2,1,72,256]{5,4,3,2,1,0:T(8,128)(2,1)S(1)}, bf16[2,1,2,1,72,256]{5,4,3,2,1,0:T(8,128)(2,1)S(1)}, u32[]{:S(2)}, u32[]{:S(2)}) collective-permute-start(bf16[2,1,2,1,72,256]{5,4,3,2,1,0:T(8,128)(2,1)S(1)} %pad_maximum_fusion.52), channel_id=1, source_target_pairs={{0,2},{2,0},{4,6},{6,4},{8,10},{10,8},{12,14},{14,12},{16,18},{18,... | collective-permute-start | bytes 442376 | tf_op jit(solution)/shard_map/ppermute | solution.py:335
  (122 other events, 1089.3 us)
where the time goes:
time: 479 us; the launch traced here: 470 us
  matrix products  116 us (24%)
  starting transfers between devices  114 us (24%)
  other arithmetic  78.4 us (16%)
  waiting for transfers between devices  70.7 us (15%)
  Pallas kernels  54.5 us (11%)
  local copies, waits for them, and re-layouts  30.3 us (6%)
  between operations  6.36 us (1%)
    dot_general x54, matrix products, dot(): return lax.dot_general(left, right, dims, preferred_element_type=f32)  114 us
    ppermute x91, starting transfers between devices, swap(): return lax.ppermute(value, axis, [(i, i ^ bit) for i in range(count)])  114 us
    ppermute x91, waiting for transfers between devices, swap(): return lax.ppermute(value, axis, [(i, i ^ bit) for i in range(count)])  70.7 us
    pallas_call x1, Pallas kernels, attention_backward(): pl.pallas_call(backward_kernel, out_shape=(result, result, result), grid_...  35.7 us
    unnamed x160, local copies, waits for them, and re-layouts  18.8 us
    pallas_call x1, Pallas kernels, attention_forward(): pl.pallas_call(forward_kernel, out_shape=(jax.ShapeDtypeStruct((width, ro...  18.7 us
    convert_element_type x1, other arithmetic, shards(): hidden = gated(activated, linear_part).astype(bf16)  11.4 us
  transfers between devices with their start and end apart: 91, of which 36 were waited for; matrix products, arithmetic and copies ran while one was open for 25% of the time, Pallas kernels for 12%

commit v1 on v0

--- a/solution.py
+++ b/solution.py
@@ -35,6 +35,16 @@
 TN = (((0,), (0,)), ((), ()))
 TT = (((0,), (1,)), ((), ()))
 QUARTERS = 4
+FEED_ROWS = 256
+FEED_CHUNKS = 3
+ERF_TOP = (
+    -2.72614225801306e-10, 2.77068142495902e-08, -2.10102402082508e-06, -5.69250639462346e-05,
+    -7.34990630326855e-04, -2.95459980854025e-03, -1.60960333262415e-02,
+)
+ERF_BOTTOM = (
+    -1.45660718464996e-05, -2.13374055278905e-04, -1.68282697438203e-03, -7.37332916720468e-03,
+    -1.42647390514189e-02,
+)
 
 
 def dot(left, right, dims):
@@ -81,10 +91,6 @@
     low, high = heads[:, :half], heads[:, half:]
     turned = jnp.concatenate([low * cosine - high * sine, high * cosine + low * sine], axis=1)
     return turned.reshape(values.shape)
-
-
-def unrotate(values, cosine, sine):
-    return rotate(values, cosine, -sine)
 
 
 def rows16(parts):
@@ -224,8 +230,8 @@
 
 
 def backward_kernel(
-    low, high, queries, keys, values, grads, outs, logsum, key_rows, query_rows,
-    query_grad, key_grad, value_grad, *scratch
+    low, high, queries, keys, values, grads, outs, logsum, key_rows, query_rows, cosine, sine,
+    joined_back, *scratch
 ):
     heads = queries.shape[0] // HEAD_DIM
     rows = keys.shape[1]
@@ -281,18 +287,31 @@
         return carry
 
     lax.fori_loop(low[step], high[step], block, 0)
+
+    def store(offset, columns, value):
+        half = HEAD_DIM // 2
+        upper, lower = value[:half], value[half:]
+        cos, sin = cosine[:, columns], sine[:, columns]
+        joined_back[offset : offset + half, columns] = (upper * cos + lower * sin).astype(bf16)
+        joined_back[offset + half : offset + HEAD_DIM, columns] = (lower * cos - upper * sin).astype(bf16)
+
+    width = heads * HEAD_DIM
+    columns = pl.ds(pl.multiple_of(step * TILE_Q, TILE_Q), TILE_Q)
     for h in range(heads):
-        query_grad[h * HEAD_DIM : (h + 1) * HEAD_DIM, :] = query_sum[h][...] * 0.125
+        store(h * HEAD_DIM, columns, query_sum[h][...] * 0.125)
 
     @pl.when(step == pl.num_programs(0) - 1)
     def _():
         for h in range(heads):
-            band = slice(h * HEAD_DIM, (h + 1) * HEAD_DIM)
-            key_grad[band, :] = key_sum[h][...] * (1.0 / LOG2E)
-            value_grad[band, :] = value_sum[h][...]
-
-
-def attention_backward(low, high, queries, keys, values, grads, outs, logsum, key_rows, query_rows):
+            first = width + h * HEAD_DIM
+            store(first, slice(0, rows), key_sum[h][...] * (1.0 / LOG2E))
+            first += width
+            joined_back[first : first + HEAD_DIM, :] = value_sum[h][...].astype(bf16)
+
+
+def attention_backward(
+    low, high, queries, keys, values, grads, outs, logsum, key_rows, query_rows, cosine, sine
+):
     width, rows = queries.shape
     heads = width // HEAD_DIM
 
@@ -302,18 +321,17 @@
     def tile(count):
         return pl.BlockSpec((count, TILE_Q), lambda i, low, high: (0, i))
 
-    result = jax.ShapeDtypeStruct((width, rows), f32)
     return pl.pallas_call(
         backward_kernel,
-        out_shape=(result, result, result),
+        out_shape=jax.ShapeDtypeStruct((3 * width, rows), bf16),
         grid_spec=pltpu.PrefetchScalarGridSpec(
             num_scalar_prefetch=2,
             grid=(rows // TILE_Q,),
             in_specs=[
                 tile(width), full(width), full(width), tile(width), tile(width), tile(heads),
-                full(16), tile(16),
+                full(16), tile(16), full(HEAD_DIM // 2), full(HEAD_DIM // 2),
             ],
-            out_specs=[tile(width), full(width), full(width)],
+            out_specs=full(3 * width),
             scratch_shapes=[
                 pltpu.VMEM((heads, rows, DEPTH), bf16),
                 pltpu.VMEM((heads, rows, DEPTH), bf16),
@@ -327,7 +345,187 @@
             dimension_semantics=("arbitrary",), vmem_limit_bytes=52 << 20
         ),
         name="attention_backward",
-    )(low, high, queries, keys, values, grads, outs, logsum, key_rows, query_rows)
+    )(low, high, queries, keys, values, grads, outs, logsum, key_rows, query_rows, cosine, sine)
+
+
+def layer_norm(values, gain_row):
+    centred = values - jnp.mean(values, axis=-1, keepdims=True)
+    inverse = lax.rsqrt(jnp.mean(centred * centred, axis=-1, keepdims=True) + norm_epsilon)
+    normal = centred * inverse
+    return normal * gain_row, normal, inverse
+
+
+def norm_back(upstream, gain_row, normal, inverse):
+    scaled = upstream * gain_row
+    inner_mean = jnp.mean(scaled * normal, axis=-1, keepdims=True)
+    return inverse * (scaled - jnp.mean(scaled, axis=-1, keepdims=True) - normal * inner_mean)
+
+
+def horner(square, factors):
+    total = factors[0] * square + factors[1]
+    for factor in factors[2:]:
+        total = total * square + factor
+    return total
+
+
+def error_function(value):
+    value = jnp.clip(value, -4.0, 4.0)
+    square = value * value
+    return value * horner(square, ERF_TOP) / horner(square, ERF_BOTTOM)
+
+
+def feed_kernel(
+    rows, attended, attended_other, upstream, gain, mixer, mixer_other, expand, shrink,
+    middle, hidden, second_part, shrink_grad, expand_grad, shrink_sum, expand_sum
+):
+    step = pl.program_id(0)
+    units = shrink.shape[0]
+    chunk = units // FEED_CHUNKS
+
+    @pl.when(step == 0)
+    def _():
+        shrink_sum[...] = jnp.zeros(shrink_sum.shape, f32)
+        expand_sum[...] = jnp.zeros(expand_sum.shape, f32)
+
+    total = rows[...].astype(f32) + dot(attended[...].T, mixer[...], NT)
+    total = total + dot(attended_other[...].T, mixer_other[...], NT)
+    middle[...] = total
+    normed = layer_norm(total, gain[...])[0].astype(bf16)
+    above = upstream[...]
+
+    def project(c):
+        first = slice(c * chunk, (c + 1) * chunk)
+        second = slice(units + c * chunk, units + (c + 1) * chunk)
+        return (
+            dot(expand[first, :], normed, NT),
+            dot(expand[second, :], normed, NT),
+            dot(shrink[first, :], above, NT),
+        )
+
+    waiting = project(0)
+    back = jnp.zeros(total.shape, f32)
+    for c in range(FEED_CHUNKS):
+        active, linear, grad = waiting
+        if c + 1 < FEED_CHUNKS:
+            waiting = project(c + 1)
+        first = slice(c * chunk, (c + 1) * chunk)
+        second = slice(units + c * chunk, units + (c + 1) * chunk)
+        area = 0.5 * error_function(active * math.sqrt(0.5)) + 0.5
+        gate = active * area
+        density = jnp.exp(-0.5 * active * active) * (1.0 / math.sqrt(2.0 * math.pi))
+        unit = (gate * linear).astype(bf16)
+        active_back = (grad * linear * (area + active * density)).astype(bf16)
+        linear_back = (grad * gate).astype(bf16)
+        hidden[first, :] = unit
+        shrink_sum[first, :] += dot(unit, above, NN)
+        expand_sum[first, :] += dot(active_back, normed, NN)
+        expand_sum[second, :] += dot(linear_back, normed, NN)
+        back = back + dot(active_back, expand[first, :], TN) + dot(linear_back, expand[second, :], TN)
+    second_part[...] = back.astype(bf16)
+
+    @pl.when(step == pl.num_programs(0) - 1)
+    def _():
+        shrink_grad[...] = shrink_sum[...].astype(bf16)
+        expand_grad[...] = expand_sum[...].astype(bf16)
+
+
+def feed_forward(rows, attended, attended_other, upstream, gain, mixer, mixer_other, expand, shrink):
+    count, width = rows.shape
+    mixed, units = attended.shape[0], shrink.shape[0]
+
+    def full(*shape):
+        return pl.BlockSpec(shape, lambda i: (0, 0))
+
+    def down(columns):
+        return pl.BlockSpec((FEED_ROWS, columns), lambda i: (i, 0))
+
+    def along(lines):
+        return pl.BlockSpec((lines, FEED_ROWS), lambda i: (0, i))
+
+    return pl.pallas_call(
+        feed_kernel,
+        grid=(count // FEED_ROWS,),
+        in_specs=[
+            down(width), along(mixed), along(mixed), down(width), full(1, width),
+            full(width, mixed), full(width, mixed), full(2 * units, width), full(units, width),
+        ],
+        out_specs=[
+            down(width), along(units), down(width), full(units, width), full(2 * units, width),
+        ],
+        out_shape=(
+            jax.ShapeDtypeStruct((count, width), f32),
+            jax.ShapeDtypeStruct((units, count), bf16),
+            jax.ShapeDtypeStruct((count, width), bf16),
+            jax.ShapeDtypeStruct((units, width), bf16),
+            jax.ShapeDtypeStruct((2 * units, width), bf16),
+        ),
+        scratch_shapes=[pltpu.VMEM((units, width), f32), pltpu.VMEM((2 * units, width), f32)],
+        compiler_params=pltpu.CompilerParams(
+            dimension_semantics=("arbitrary",), vmem_limit_bytes=48 << 20
+        ),
+        name="feed_forward",
+    )(rows, attended, attended_other, upstream, gain, mixer, mixer_other, expand, shrink)
+
+
+def norm_kernel(
+    middle, own, other, upstream, gain, mixer, attended,
+    middle_grad, attended_grad, mixer_grad, gain_grad, mixer_turned, mixer_sum
+):
+    step = pl.program_id(0)
+
+    @pl.when(step == 0)
+    def _():
+        mixer_turned[...] = mixer[...].T
+        mixer_sum[...] = jnp.zeros(mixer_sum.shape, f32)
+        gain_grad[...] = jnp.zeros(gain_grad.shape, f32)
+
+    unused, normal, inverse = layer_norm(middle[...], gain[...])
+    back = own[...].astype(f32) + other[...].astype(f32)
+    grad = upstream[...].astype(f32) + norm_back(back, gain[...], normal, inverse)
+    middle_grad[...] = grad
+    grad_low = grad.astype(bf16)
+    attended_grad[...] = dot(mixer_turned[...], grad_low, NT).astype(bf16)
+    mixer_sum[...] += dot(attended[...], grad_low, NN)
+    gain_grad[...] += jnp.sum(back * normal, axis=0, keepdims=True)
+
+    @pl.when(step == pl.num_programs(0) - 1)
+    def _():
+        mixer_grad[...] = mixer_sum[...].T.astype(bf16)
+
+
+def norm_backward(middle, own, other, upstream, gain, mixer, attended):
+    count, width = middle.shape
+    mixed = attended.shape[0]
+
+    def full(*shape):
+        return pl.BlockSpec(shape, lambda i: (0, 0))
+
+    def down(columns):
+        return pl.BlockSpec((FEED_ROWS, columns), lambda i: (i, 0))
+
+    def along(lines):
+        return pl.BlockSpec((lines, FEED_ROWS), lambda i: (0, i))
+
+    return pl.pallas_call(
+        norm_kernel,
+        grid=(count // FEED_ROWS,),
+        in_specs=[
+            down(width), down(width), down(width), down(width), full(1, width),
+            full(width, mixed), along(mixed),
+        ],
+        out_specs=[down(width), along(mixed), full(width, mixed), full(1, width)],
+        out_shape=(
+            jax.ShapeDtypeStruct((count, width), f32),
+            jax.ShapeDtypeStruct((mixed, count), bf16),
+            jax.ShapeDtypeStruct((width, mixed), bf16),
+            jax.ShapeDtypeStruct((1, width), f32),
+        ),
+        scratch_shapes=[pltpu.VMEM((mixed, width), bf16), pltpu.VMEM((mixed, width), f32)],
+        compiler_params=pltpu.CompilerParams(
+            dimension_semantics=("arbitrary",), vmem_limit_bytes=40 << 20
+        ),
+        name="norm_backward",
+    )(middle, own, other, upstream, gain, mixer, attended)
 
 
 def swap(value, axis, bit):
@@ -421,23 +619,6 @@
     first = jnp.where(head == 0, own, other)
     second = jnp.where(head == 0, other, own)
     return jnp.concatenate([first, second], axis=0)
-
-
-def layer_norm(values, gain_row):
-    centred = values - jnp.mean(values, axis=-1, keepdims=True)
-    inverse = lax.rsqrt(jnp.mean(centred * centred, axis=-1, keepdims=True) + norm_epsilon)
-    normal = centred * inverse
-    return normal * gain_row, normal, inverse
-
-
-def norm_back(upstream, gain_row, normal, inverse):
-    scaled = upstream * gain_row
-    inner_mean = jnp.mean(scaled * normal, axis=-1, keepdims=True)
-    return inverse * (scaled - jnp.mean(scaled, axis=-1, keepdims=True) - normal * inner_mean)
-
-
-def gated(active_in, linear_in):
-    return jax.nn.gelu(active_in, approximate=False) * linear_in
 
 
 def schulz_start(own, gathered):
@@ -486,9 +667,6 @@
     def own_half(value):
         return lax.dynamic_slice_in_dim(value, head * local_rows, local_rows, 0)
 
-    def other_half(value):
-        return lax.dynamic_slice_in_dim(value, (1 - head) * local_rows, local_rows, 0)
-
     joined_parts = [gather_start(part) for part in thirds(joined_weight[0].astype(bf16))]
     joined_parts = quarter(ordered_step, joined_parts, 0)
     others = [gather_start(part) for part in halves_of(expand_weight[0].astype(bf16))] + [
@@ -496,8 +674,8 @@
     ]
     key_rows, query_rows, cosine, sine = doc_tables(lengths[0], row_count)
     low, high = key_bounds(lengths[0], row_count)
-    residual = halves(tokens, swap(tokens, "head", 1), head).astype(f32)
-    first_normed, first_normal, first_inverse = layer_norm(residual, norm_gains[0])
+    rows_low = halves(tokens, swap(tokens, "head", 1), head)
+    first_normed, first_normal, first_inverse = layer_norm(rows_low.astype(f32), norm_gains[0])
     first_low = first_normed.astype(bf16)
 
     joined_parts, others = tie(joined_parts, others)
@@ -524,63 +702,46 @@
     attended_other = swap(attended, "head", 1)
     expand_low = jnp.concatenate([gather_rows(part) for part in others[:2]], axis=1)
     both_low = gather_rows(others[2])
-    mixer_low, shrink_low = both_low[:, :mixer_width], both_low[:, mixer_width:]
+    mixer_low, shrink_turned = both_low[:, :mixer_width], both_low[:, mixer_width:].T
     mixer_other = swap(mixer_low, "head", 1)
 
-    middle = residual + dot(attended, mixer_low, TT) + dot(attended_other, mixer_other, TT)
-    second_normed, second_normal, second_inverse = layer_norm(middle, norm_gains[1])
-    second_low = second_normed.astype(bf16)
-
-    expanded = dot(second_low, expand_low, NT)
-    hidden_width = expanded.shape[1] // 2
-    activated, linear_part = expanded[:, :hidden_width], expanded[:, hidden_width:]
-    hidden = gated(activated, linear_part).astype(bf16)
-
-    hidden_grad = dot(cotangent, shrink_low, NN)
-    unused, gate_pull = jax.vjp(gated, activated, linear_part)
-    active_grad, linear_grad = gate_pull(hidden_grad)
-    expand_back = jnp.concatenate([active_grad, linear_grad], axis=1).astype(bf16)
-    second_part = dot(expand_back, expand_low, NN)
-    second_other = swap(second_part.astype(bf16), "head", 1)
-    shrink_grad = dot(cotangent, hidden, TN).astype(bf16)
-    expand_grad = dot(expand_back, second_low, TN).astype(bf16)
+    second_gain = norm_gains[1:2]
+    middle, hidden, second_part, shrink_grad, expand_grad = feed_forward(
+        rows_low, attended, attended_other, cotangent, second_gain,
+        mixer_low, mixer_other, expand_low, shrink_turned,
+    )
+    second_other = swap(second_part, "head", 1)
 
     sums, second_other = tie(
-        [reduce_start(part) for part in halves_of(expand_grad) + [shrink_grad]], second_other
+        [reduce_start(part) for part in halves_of(expand_grad) + [shrink_grad.T]], second_other
     )
     moved = quarter(reduce_step, sums, 0)
-    second_back = second_part + second_other.astype(f32)
-    middle_grad = cotangent.astype(f32) + norm_back(
-        second_back, norm_gains[1], second_normal, second_inverse
-    )
-    middle_low = middle_grad.astype(bf16)
-    attended_grad = dot(mixer_low, middle_low, TT).astype(bf16)
-
-    sums, attended_grad, middle_low = tie(moved, attended_grad, middle_low)
+    middle_grad, attended_grad, mixer_grad, second_gain_grad = norm_backward(
+        middle, second_part, second_other, cotangent, second_gain, mixer_low, attended
+    )
+    second_gain_grad = 0.5 * second_gain_grad[0]
+
+    sums, attended_grad, shrink_now = tie(moved, attended_grad, shrink_turned)
     moved = quarter(reduce_step, sums, 1)
-    mixer_grad = lax.dot_general(
-        middle_low, attended, (((0,), (1,)), ((), ())), preferred_element_type=f32
-    ).astype(bf16)
-    second_gain_grad = jnp.sum(own_half(second_back * second_normal), axis=0)
-
-    sums, mixer_grad, second_gain_grad, shrink_now = tie(
-        moved, mixer_grad, second_gain_grad, shrink_low
-    )
+
+    def fed(columns, weight):
+        return dot(lax.dynamic_slice_in_dim(hidden, columns, local_rows, 1), weight, TN)
+
+    fed_other = fed((1 - head) * local_rows, shrink_now).astype(bf16)
+    sums, mixer_grad, fed_other, shrink_now = tie(moved, mixer_grad, fed_other, shrink_now)
     moved = quarter(reduce_step, sums, 2)
     mixer_moved = quarter(reduce_step, [reduce_start(mixer_grad)], 0, 2)
-    fed_own = dot(own_half(hidden), shrink_now, NT)
-    fed_other = dot(other_half(hidden), shrink_now, NT).astype(bf16)
-
-    sums, mixer_sum, fed_other, low = tie(moved, mixer_moved, fed_other, low)
+    fed_own = fed(head * local_rows, shrink_now)
+
+    sums, mixer_sum, fed_own, low = tie(moved, mixer_moved, fed_own, low)
     moved = quarter(reduce_step, sums, 3)
     mixer_moved = quarter(reduce_step, mixer_sum, 1, 2)
     fed_other = swap(fed_other, "head", 1)
-    query_grad, key_grad, value_grad = attention_backward(
-        low, high, queries, keys, values, attended_grad, attended, logsum, key_rows, query_rows
-    )
-    sums, mixer_sum, query_grad, key_grad, value_grad = tie(
-        moved, mixer_moved, query_grad, key_grad, value_grad
-    )
+    joined_back = attention_backward(
+        low, high, queries, keys, values, attended_grad, attended, logsum, key_rows, query_rows,
+        cosine, sine,
+    )
+    sums, mixer_sum, joined_back = tie(moved, mixer_moved, joined_back)
     expand_next = 0.5 * expand_momentum[0] + jnp.concatenate(sums[:2], axis=1)
     shrink_next = 0.5 * shrink_momentum[0] + sums[2]
     gathers = [gather_start(part) for part in halves_of(expand_next.astype(bf16))]
@@ -588,9 +749,6 @@
 
     moved = quarter(gather_step, gathers, 0)
     mixer_moved = quarter(reduce_step, mixer_sum, 2, 2)
-    joined_back = jnp.concatenate(
-        [unrotate(query_grad, cosine, sine), unrotate(key_grad, cosine, sine), value_grad], axis=0
-    ).astype(bf16)
     joined_grad = dot(joined_back, first_low, NN).astype(bf16)
 
     def first_part(start, weight):

time: 479 us -> 433 us (0.904)
  Pallas kernels: 54.5 us -> 103 us
  matrix products: 116 us -> 71.7 us
  other arithmetic: 78.4 us -> 50.6 us
  local copies, waits for them, and re-layouts: 30.3 us -> 11.7 us
    pallas_call x1 -> x3, Pallas kernels: 35.7 us -> 84 us  [the longest x1 35.5 us: feed_forward(): pl.pallas_call(feed_kernel, grid=(count // FEED_ROWS,), in_specs=[down(wi...]
    dot_general x54 -> x46, matrix products: 114 us -> 71.7 us  [dot(): return lax.dot_general(left, right, dims, preferred_element_type=f32)]
    unnamed x160 -> x122, local copies, waits for them, and re-layouts: 18.8 us -> 3.69 us
    convert_element_type x2 -> x1, other arithmetic: 15.6 us -> 1.74 us  [shards(): (own_half(middle) + fed_own + fed_other.astype(f32)).astype(bf16)]
    reduce_sum x2 -> x1, other arithmetic: 7.27 us -> 1.27 us  [norm_back(): jnp.mean(scaled, axis=-1, keepdims=True)]
    convert_element_type x21, other arithmetic: 6.74 us -> 1.33 us  [reduce_step(): return total.astype(bf16)]
    another operation x4 -> x2, other arithmetic: 6.11 us -> 0.95 us
  transfers between devices with their start and end apart: 91 -> 91, of which waited for: 36 -> 31; matrix products, arithmetic and copies ran while one was open for 25% -> 22% of each run, Pallas kernels for 12% -> 16%
where the time goes in v1:
time: 433 us; the launch traced here: 427 us
  starting transfers between devices  116 us (27%)
  Pallas kernels  103 us (24%)
  matrix products  71.7 us (17%)
  waiting for transfers between devices  67.9 us (16%)
  other arithmetic  50.6 us (12%)
  local copies, waits for them, and re-layouts  11.7 us (3%)
  between operations  6.12 us (1%)
    ppermute x91, starting transfers between devices, swap(): return lax.ppermute(value, axis, [(i, i ^ bit) for i in range(count)])  116 us
    dot_general x46, matrix products, dot(): return lax.dot_general(left, right, dims, preferred_element_type=f32)  71.7 us
    ppermute x91, waiting for transfers between devices, swap(): return lax.ppermute(value, axis, [(i, i ^ bit) for i in range(count)])  67.9 us
    pallas_call x1, Pallas kernels, feed_forward(): pl.pallas_call(feed_kernel, grid=(count // FEED_ROWS,), in_specs=[down(wi...  35.5 us
    pallas_call x1, Pallas kernels, attention_backward(): pl.pallas_call(backward_kernel, out_shape=jax.ShapeDtypeStruct((3 * width...  35.2 us
    pallas_call x1, Pallas kernels, attention_forward(): pl.pallas_call(forward_kernel, out_shape=(jax.ShapeDtypeStruct((width, ro...  19.3 us
    pallas_call x1, Pallas kernels, norm_backward(): pl.pallas_call(norm_kernel, grid=(count // FEED_ROWS,), in_specs=[down(wi...  13.3 us
  transfers between devices with their start and end apart: 91, of which 31 were waited for; matrix products, arithmetic and copies ran while one was open for 22% of the time, Pallas kernels for 16%

profile of v1, /device:TPU:0, one launch (start us, length us, event | category | flops | bytes accessed | tf_op | source)
XLA Modules:
  0.0 427.2 jit_solution(4298432150588525171)
XLA Ops:
  1.6 4.1 collective-permute-start.3
  5.8 2.8 collective-permute-start.1
  16.1 2.9 collective-permute-start.8
  25.8 2.5 collective-permute-done.6
  28.4 2.8 collective-permute-done.9
  36.3 2.4 collective-permute-start.12
  42.6 3.1 fusion.2
  45.7 3.8 fusion
  53.2 3.0 collective-permute-done.13
  60.0 3.9 fusion.150
  67.5 3.2 collective-permute-done.19
  71.6 4.3 %collective-permute-done.21 = bf16[2,1,2,1,48,960]{5,4,3,2,1,0:T(8,128)(2,1)S(1)} collective-permute-done((bf16[2,1,2,1,48,960]{5,4,3,2,1,0:T(8,128)(2,1)S(1)}, bf16[2,1,2,1,48,960]{5,4,3,2,1,0:T(8,128)(2,1)S(1)}, u32[]{:S(2)}, u32[]{:S(2)}) %collective-permute-start.21) | collective-permute-done | bytes 368672 | tf_op jit(solution)/shard_map/ppermute | solution.py:533
  78.3 2.9 collective-permute-start.24
  81.2 19.3 %attention_forward.1 = (bf16[384,2048]{1,0:T(8,128)(2,1)}, f32[6,2048]{1,0:T(8,128)S(1)}) custom-call(s32[8]{0:T(128)S(1)} %get-tuple-element.207.low, s32[8]{0:T(128)S(1)} %get-tuple-element.381.high, bf16[384,2048]{1,0:T(8,128)(2,1)S(1)} %bitcast.225, bf16[384,2048]{1,0:T(8,128)(2,1)S(1)} %bitcast.223, bf16[384,2048]{1,0:T(8,128)(2,1)S(1)} %slice.158.values, ...), custom_call_target="tpu_custom_call" | custom-call | tf_op jit(solution)/shard_map/attention_forward/pallas_call | solution.py:207
  108.4 2.8 pad_maximum_fusion.2.expand
  111.2 35.5 %feed_forward.1 = (f32[2048,768]{1,0:T(8,128)}, bf16[576,2048]{1,0:T(8,128)(2,1)}, bf16[2048,768]{1,0:T(8,128)(2,1)}, bf16[576,768]{1,0:T(8,128)(2,1)S(1)}, bf16[1152,768]{1,0:T(8,128)(2,1)}) custom-call(bf16[2048,768]{1,0:T(8,128)(2,1)} %pad_maximum_fusion.rows, bf16[384,2048]{1,0:T(8,128)(2,1)} %get-tuple-element.177.attended.outs, ...), custom_call_target="tpu_custom_call" | custom-call | tf_op jit(solution)/shard_map/feed_forward/pallas_call | solution.py:445
  147.7 2.8 pad_maximum_fusion.1
  154.7 7.2 %collective-permute-start.28 = (bf16[2,2,2,1,72,384]{5,4,3,2,1,0:T(8,128)(2,1)S(1)}, bf16[2,2,2,1,72,384]{5,4,3,2,1,0:T(8,128)(2,1)S(1)}, u32[]{:S(2)}, u32[]{:S(2)}) collective-permute-start(bf16[2,2,2,1,72,384]{5,4,3,2,1,0:T(8,128)(2,1)S(1)} %constant_dynamic-slice_fusion.27), channel_id=1, source_target_pairs={{0,2},{2,0},{4,6},{6,4},{8,10},{10,8},{12,14},{14,12},{16,18},{18,... | collective-permute-start | bytes 1327112 | tf_op jit(solution)/shard_map/ppermute | solution.py:533
  162.0 13.3 %norm_backward.1 = (f32[2048,768]{1,0:T(8,128)}, bf16[384,2048]{1,0:T(8,128)(2,1)S(1)}, bf16[768,384]{1,0:T(8,128)(2,1)S(1)}, f32[1,768]{1,0:T(1,128)S(1)}) custom-call(f32[2048,768]{1,0:T(8,128)} %get-tuple-element.181.middle, bf16[2048,768]{1,0:T(8,128)(2,1)S(1)} %copy-done.4, bf16[2048,768]{1,0:T(8,128)(2,1)} %collective-permute-done.27.other, ...), custom_call_target="tpu_custom_call" | custom-call | tf_op jit(solution)/shard_map/norm_backward/pallas_call | solution.py:509
  193.7 3.7 collective-permute-done.37
  197.6 2.9 collective-permute-start.39
  201.6 35.2 %attention_backward.1 = bf16[1152,2048]{1,0:T(8,128)(2,1)} custom-call(s32[8]{0:T(128)S(1)} %get-tuple-element.207.low, s32[8]{0:T(128)S(1)} %get-tuple-element.381.high, bf16[384,2048]{1,0:T(8,128)(2,1)} %bitcast.226, bf16[384,2048]{1,0:T(8,128)(2,1)} %bitcast.224, bf16[384,2048]{1,0:T(8,128)(2,1)} %copy-done, bf16[384,2048]{1,0:T(8,128)(2,1)} %copy-done.7, ...), custom_call_target="tpu_custom_call" | custom-call | tf_op jit(solution)/shard_map/attention_backward/pallas_call | solution.py:324
  237.1 6.3 %convolution_convert_fusion = bf16[1152,768]{1,0:T(8,128)(2,1)S(1)} fusion(bf16[1152,2048]{1,0:T(8,128)(2,1)} %attention_backward.1, bf16[2048,768]{1,0:T(8,128)(2,1)S(1)} %copy-done.14), kind=kOutput, calls=%fused_computation.6 | convolution fusion | flops 3624763392 | bytes 9633792 | tf_op jit(solution)/shard_map/dot_general | solution.py:51
  244.7 6.6 %collective-permute-start.44 = (bf16[1,1,1,1,72,384]{5,4,3,2,1,0:T(8,128)(2,1)S(1)}, bf16[1,1,1,1,72,384]{5,4,3,2,1,0:T(8,128)(2,1)S(1)}, u32[]{:S(2)}, u32[]{:S(2)}) collective-permute-start(bf16[1,1,1,1,72,384]{5,4,3,2,1,0:T(8,128)(2,1)S(1)} %get-tuple-element.354), channel_id=1, source_target_pairs={{0,16},{2,18},{4,20},{6,22},{8,24},{10,26},{12,28},{14,30},{16,0},... | collective-permute-start | bytes 165896 | tf_op jit(solution)/shard_map/ppermute | solution.py:533
  252.0 2.8 collective-permute-start.45
  255.6 2.1 collective-permute-done.45
  257.9 2.3 fusion.14
  260.3 2.3 fusion.4
  262.7 2.4 collective-permute-start.53
  265.2 4.2 collective-permute-start.50
  269.4 3.5 collective-permute-start.51
  273.1 4.6 %collective-permute-done.52 = bf16[2,1,1,1,48,576]{5,4,3,2,1,0:T(8,128)(2,1)S(1)} collective-permute-done((bf16[2,1,1,1,48,576]{5,4,3,2,1,0:T(8,128)(2,1)S(1)}, bf16[2,1,1,1,48,576]{5,4,3,2,1,0:T(8,128)(2,1)S(1)}, u32[]{:S(2)}, u32[]{:S(2)}) %collective-permute-start.52) | collective-permute-done | bytes 110624 | tf_op jit(solution)/shard_map/ppermute | solution.py:533
  280.1 4.4 %collective-permute-done.47 = bf16[2,2,2,1,72,256]{5,4,3,2,1,0:T(8,128)(2,1)S(1)} collective-permute-done((bf16[2,2,2,1,72,256]{5,4,3,2,1,0:T(8,128)(2,1)S(1)}, bf16[2,2,2,1,72,256]{5,4,3,2,1,0:T(8,128)(2,1)S(1)}, u32[]{:S(2)}, u32[]{:S(2)}) %collective-permute-start.47) | collective-permute-done | bytes 294944 | tf_op jit(solution)/shard_map/ppermute | solution.py:533
  298.5 2.1 collective-permute-done.58
  308.9 2.4 multiply_add_fusion
  314.1 6.5 %collective-permute-done.64 = bf16[2,2,2,1,72,384]{5,4,3,2,1,0:T(8,128)(2,1)S(1)} collective-permute-done((bf16[2,2,2,1,72,384]{5,4,3,2,1,0:T(8,128)(2,1)S(1)}, bf16[2,2,2,1,72,384]{5,4,3,2,1,0:T(8,128)(2,1)S(1)}, u32[]{:S(2)}, u32[]{:S(2)}) %collective-permute-start.64) | collective-permute-done | bytes 442400 | tf_op jit(solution)/shard_map/ppermute | solution.py:533
  320.8 2.2 collective-permute-done.65
  325.5 2.4 collective-permute-start.69
  328.5 2.4 collective-permute-start.67
  339.1 3.8 select_reduce_fusion.1
  354.7 4.3 %fusion.60 = f32[48,576]{1,0:T(8,128)} fusion(f32[576,576]{1,0:T(8,128)} %multiply_add_fusion.10, f32[48,576]{1,0:T(8,128)} %fusion.112, f32[48,576]{1,0:T(8,128)S(1)} %convolution_add_fusion.6), kind=kOutput, calls=%fused_computation.110 | convolution fusion | flops 415908864 | bytes 1658880 | tf_op jit(solution)/shard_map/dot_general | solution.py:51
  381.1 2.7 multiply_add_fusion.5
  383.8 4.5 %fusion.57 = f32[72,768]{1,0:T(8,128)S(1)} fusion(f32[768,768]{1,0:T(8,128)} %multiply_add_fusion.5, f32[72,768]{1,0:T(8,128)S(1)} %fusion.103, f32[72,768]{1,0:T(8,128)S(1)} %multiply_add_fusion.18), kind=kOutput, calls=%fused_computation.109 | convolution fusion | flops 994240512 | bytes 3022848 | tf_op jit(solution)/shard_map/dot_general | solution.py:51
  394.3 3.4 collective-permute-start.90
  403.7 3.1 collective-permute-done.87
  408.2 3.8 select_reduce_fusion
  412.7 4.6 %add_convert_fusion.3 = bf16[768,768]{1,0:T(8,128)(2,1)S(1)} fusion(f32[768,768]{1,0:T(8,128)} %get-tuple-element.380, f32[]{:T(128)S(6)} %mul.501), kind=kOutput, calls=%fused_computation.23 | convolution fusion | flops 910098432 | bytes 3538948 | tf_op jit(solution)/shard_map/dot_general | solution.py:51
  424.9 2.1 fusion.54
  (516 shorter events, 164.7 us)
Async XLA Ops:
  1.6 14.2 %collective-permute-start.3 = (bf16[1,1,1,1,72,256]{5,4,3,2,1,0:T(8,128)(2,1)S(1)}, bf16[1,1,1,1,72,256]{5,4,3,2,1,0:T(8,128)(2,1)S(1)}, u32[]{:S(2)}, u32[]{:S(2)}) collective-permute-start(bf16[1,1,1,1,72,256]{5,4,3,2,1,0:T(8,128)(2,1)S(1)} %get-tuple-element.366), channel_id=1, source_target_pairs={{0,16},{2,18},{4,20},{6,22},{8,24},{10,26},{12,28},{14,30},{16,0},... | collective-permute-start | bytes 110600 | tf_op jit(solution)/shard_map/ppermute | solution.py:533
  5.7 10.1 %collective-permute-start.2 = (bf16[1,1,1,1,72,256]{5,4,3,2,1,0:T(8,128)(2,1)S(1)}, bf16[1,1,1,1,72,256]{5,4,3,2,1,0:T(8,128)(2,1)S(1)}, u32[]{:S(2)}, u32[]{:S(2)}) collective-permute-start(bf16[1,1,1,1,72,256]{5,4,3,2,1,0:T(8,128)(2,1)S(1)} %get-tuple-element.367), channel_id=1, source_target_pairs={{0,16},{2,18},{4,20},{6,22},{8,24},{10,26},{12,28},{14,30},{16,0},... | collective-permute-start | bytes 110600 | tf_op jit(solution)/shard_map/ppermute | solution.py:533
  5.8 10.0 %collective-permute-start.1 = (bf16[1,1,1,1,72,256]{5,4,3,2,1,0:T(8,128)(2,1)S(1)}, bf16[1,1,1,1,72,256]{5,4,3,2,1,0:T(8,128)(2,1)S(1)}, u32[]{:S(2)}, u32[]{:S(2)}) collective-permute-start(bf16[1,1,1,1,72,256]{5,4,3,2,1,0:T(8,128)(2,1)S(1)} %get-tuple-element.368), channel_id=1, source_target_pairs={{0,16},{2,18},{4,20},{6,22},{8,24},{10,26},{12,28},{14,30},{16,0},... | collective-permute-start | bytes 110600 | tf_op jit(solution)/shard_map/ppermute | solution.py:533
  8.7 33.2 %collective-permute-start = (bf16[1024,768]{1,0:T(8,128)(2,1)}, bf16[1024,768]{1,0:T(8,128)(2,1)S(1)}, u32[]{:S(2)}, u32[]{:S(2)}) collective-permute-start(bf16[1024,768]{1,0:T(8,128)(2,1)} %param.13), channel_id=1, source_target_pairs={{0,1},{1,0},{2,3},{3,2},{4,5},{5,4},{6,7},{7,6},{8,9},{9,8},{10,11... | collective-permute-start | bytes 4718600 | tf_op jit(solution)/shard_map/ppermute | solution.py:533
  15.9 8.1 %collective-permute-start.7 = (bf16[1,1,1,1,72,384]{5,4,3,2,1,0:T(8,128)(2,1)S(1)}, bf16[1,1,1,1,72,384]{5,4,3,2,1,0:T(8,128)(2,1)S(1)}, u32[]{:S(2)}, u32[]{:S(2)}) collective-permute-start(bf16[1,1,1,1,72,384]{5,4,3,2,1,0:T(8,128)(2,1)S(1)} %get-tuple-element.149), channel_id=1, source_target_pairs={{0,16},{2,18},{4,20},{6,22},{8,24},{10,26},{12,28},{14,30},{16,0},... | collective-permute-start | bytes 165896 | tf_op jit(solution)/shard_map/ppermute | solution.py:533
  16.1 9.4 %collective-permute-start.8 = (bf16[1,1,1,1,72,384]{5,4,3,2,1,0:T(8,128)(2,1)S(1)}, bf16[1,1,1,1,72,384]{5,4,3,2,1,0:T(8,128)(2,1)S(1)}, u32[]{:S(2)}, u32[]{:S(2)}) collective-permute-start(bf16[1,1,1,1,72,384]{5,4,3,2,1,0:T(8,128)(2,1)S(1)} %get-tuple-element.150), channel_id=1, source_target_pairs={{0,16},{2,18},{4,20},{6,22},{8,24},{10,26},{12,28},{14,30},{16,0},... | collective-permute-start | bytes 165896 | tf_op jit(solution)/shard_map/ppermute | solution.py:533
  38.7 12.8 %collective-permute-start.18 = (bf16[2,1,1,1,48,960]{5,4,3,2,1,0:T(8,128)(2,1)S(1)}, bf16[2,1,1,1,48,960]{5,4,3,2,1,0:T(8,128)(2,1)S(1)}, u32[]{:S(2)}, u32[]{:S(2)}) collective-permute-start(bf16[2,1,1,1,48,960]{5,4,3,2,1,0:T(8,128)(2,1)S(1)} %pad_maximum_fusion.37), channel_id=1, source_target_pairs={{0,4},{2,6},{4,0},{6,2},{8,12},{10,14},{12,8},{14,10},{16,20},{18,... | collective-permute-start | bytes 552968 | tf_op jit(solution)/shard_map/ppermute | solution.py:533
  65.6 10.4 %collective-permute-start.21 = (bf16[2,1,2,1,48,960]{5,4,3,2,1,0:T(8,128)(2,1)S(1)}, bf16[2,1,2,1,48,960]{5,4,3,2,1,0:T(8,128)(2,1)S(1)}, u32[]{:S(2)}, u32[]{:S(2)}) collective-permute-start(bf16[2,1,2,1,48,960]{5,4,3,2,1,0:T(8,128)(2,1)S(1)} %pad_maximum_fusion.24), channel_id=1, source_target_pairs={{0,2},{2,0},{4,6},{6,4},{8,10},{10,8},{12,14},{14,12},{16,18},{18,... | collective-permute-start | bytes 1105928 | tf_op jit(solution)/shard_map/ppermute | solution.py:533
  76.1 24.4 %collective-permute-start.22 = (bf16[2,2,2,1,72,384]{5,4,3,2,1,0:T(8,128)(2,1)S(1)}, bf16[2,2,2,1,72,384]{5,4,3,2,1,0:T(8,128)(2,1)S(1)}, u32[]{:S(2)}, u32[]{:S(2)}) collective-permute-start(bf16[2,2,2,1,72,384]{5,4,3,2,1,0:T(8,128)(2,1)S(1)} %pad_maximum_fusion.20), channel_id=1, source_target_pairs={{0,2},{2,0},{4,6},{6,4},{8,10},{10,8},{12,14},{14,12},{16,18},{18,... | collective-permute-start | bytes 1327112 | tf_op jit(solution)/shard_map/ppermute | solution.py:533
  76.7 24.9 %collective-permute-start.23 = (bf16[2,2,1,2,72,384]{5,4,3,2,1,0:T(8,128)(2,1)S(1)}, bf16[2,2,1,2,72,384]{5,4,3,2,1,0:T(8,128)(2,1)S(1)}, u32[]{:S(2)}, u32[]{:S(2)}) collective-permute-start(bf16[2,2,1,2,72,384]{5,4,3,2,1,0:T(8,128)(2,1)S(1)} %pad_maximum_fusion.21), channel_id=1, source_target_pairs={{0,4},{2,6},{4,0},{6,2},{8,12},{10,14},{12,8},{14,10},{16,20},{18,... | collective-permute-start | bytes 1327112 | tf_op jit(solution)/shard_map/ppermute | solution.py:533
  78.3 24.5 %collective-permute-start.24 = (bf16[2,1,2,2,48,960]{5,4,3,2,1,0:T(8,128)(2,1)S(1)}, bf16[2,1,2,2,48,960]{5,4,3,2,1,0:T(8,128)(2,1)S(1)}, u32[]{:S(2)}, u32[]{:S(2)}) collective-permute-start(bf16[2,1,2,2,48,960]{5,4,3,2,1,0:T(8,128)(2,1)S(1)} %pad_maximum_fusion.11), channel_id=1, source_target_pairs={{0,8},{2,10},{4,12},{6,14},{8,0},{10,2},{12,4},{14,6},{16,24},{18,... | collective-permute-start | bytes 2211848 | tf_op jit(solution)/shard_map/ppermute | solution.py:533
  103.1 8.1 %collective-permute-start.25 = (bf16[384,2048]{1,0:T(8,128)(2,1)}, bf16[384,2048]{1,0:T(8,128)(2,1)S(1)}, u32[]{:S(2)}, u32[]{:S(2)}) collective-permute-start(bf16[384,2048]{1,0:T(8,128)(2,1)} %get-tuple-element.177.attended.outs), channel_id=1, source_target_pairs={{0,1},{1,0},{2,3},{3,2},{4,5},{5,4},{6,7},{7,6},{8,9},{9,8},{10,11... | collective-permute-start | bytes 4718600 | tf_op jit(solution)/shard_map/ppermute | solution.py:533
  153.7 21.6 %collective-permute-start.29 = (bf16[2,2,1,2,72,384]{5,4,3,2,1,0:T(8,128)(2,1)S(1)}, bf16[2,2,1,2,72,384]{5,4,3,2,1,0:T(8,128)(2,1)S(1)}, u32[]{:S(2)}, u32[]{:S(2)}) collective-permute-start(bf16[2,2,1,2,72,384]{5,4,3,2,1,0:T(8,128)(2,1)S(1)} %constant_dynamic-slice_fusion.26), channel_id=1, source_target_pairs={{0,4},{2,6},{4,0},{6,2},{8,12},{10,14},{12,8},{14,10},{16,20},{18,... | collective-permute-start | bytes 1327112 | tf_op jit(solution)/shard_map/ppermute | solution.py:533
  154.7 20.8 %collective-permute-start.28 = (bf16[2,2,2,1,72,384]{5,4,3,2,1,0:T(8,128)(2,1)S(1)}, bf16[2,2,2,1,72,384]{5,4,3,2,1,0:T(8,128)(2,1)S(1)}, u32[]{:S(2)}, u32[]{:S(2)}) collective-permute-start(bf16[2,2,2,1,72,384]{5,4,3,2,1,0:T(8,128)(2,1)S(1)} %constant_dynamic-slice_fusion.27), channel_id=1, source_target_pairs={{0,2},{2,0},{4,6},{6,4},{8,10},{10,8},{12,14},{14,12},{16,18},{18,... | collective-permute-start | bytes 1327112 | tf_op jit(solution)/shard_map/ppermute | solution.py:533
  161.9 13.7 %collective-permute-start.30 = (bf16[2,1,2,2,48,576]{5,4,3,2,1,0:T(8,128)(2,1)S(1)}, bf16[2,1,2,2,48,576]{5,4,3,2,1,0:T(8,128)(2,1)S(1)}, u32[]{:S(2)}, u32[]{:S(2)}) collective-permute-start(bf16[2,1,2,2,48,576]{5,4,3,2,1,0:T(8,128)(2,1)S(1)} %constant_dynamic-slice_fusion.25), channel_id=1, source_target_pairs={{0,8},{2,10},{4,12},{6,14},{8,0},{10,2},{12,4},{14,6},{16,24},{18,... | collective-permute-start | bytes 1327112 | tf_op jit(solution)/shard_map/ppermute | solution.py:533
  189.1 8.3 %collective-permute-start.37 = (bf16[2,1,2,2,48,384]{5,4,3,2,1,0:T(8,128)(2,1)S(1)}, bf16[2,1,2,2,48,384]{5,4,3,2,1,0:T(8,128)(2,1)S(1)}, u32[]{:S(2)}, u32[]{:S(2)}) collective-permute-start(bf16[2,1,2,2,48,384]{5,4,3,2,1,0:T(8,128)(2,1)S(1)} %constant_dynamic-slice_fusion.18), channel_id=1, source_target_pairs={{0,8},{2,10},{4,12},{6,14},{8,0},{10,2},{12,4},{14,6},{16,24},{18,... | collective-permute-start | bytes 884744 | tf_op jit(solution)/shard_map/ppermute | solution.py:533
  191.7 95.2 %collective-permute-start.38 = (bf16[1024,768]{1,0:T(8,128)(2,1)S(1)}, bf16[1024,768]{1,0:T(8,128)(2,1)S(1)}, u32[]{:S(2)}, u32[]{:S(2)}) collective-permute-start(bf16[1024,768]{1,0:T(8,128)(2,1)S(1)} %convolution_convert_fusion.1), channel_id=1, source_target_pairs={{0,1},{1,0},{2,3},{3,2},{4,5},{5,4},{6,7},{7,6},{8,9},{9,8},{10,11... | collective-permute-start | bytes 4718600 | tf_op jit(solution)/shard_map/ppermute | solution.py:533
  197.6 39.3 %collective-permute-start.40 = (bf16[1,1,1,1,72,384]{5,4,3,2,1,0:T(8,128)(2,1)S(1)}, bf16[1,1,1,1,72,384]{5,4,3,2,1,0:T(8,128)(2,1)S(1)}, u32[]{:S(2)}, u32[]{:S(2)}) collective-permute-start(bf16[1,1,1,1,72,384]{5,4,3,2,1,0:T(8,128)(2,1)S(1)} %constant_dynamic-slice_fusion.16), channel_id=1, source_target_pairs={{0,16},{2,18},{4,20},{6,22},{8,24},{10,26},{12,28},{14,30},{16,0},... | collective-permute-start | bytes 165896 | tf_op jit(solution)/shard_map/ppermute | solution.py:533
  197.6 39.3 %collective-permute-start.39 = (bf16[1,1,1,1,72,384]{5,4,3,2,1,0:T(8,128)(2,1)S(1)}, bf16[1,1,1,1,72,384]{5,4,3,2,1,0:T(8,128)(2,1)S(1)}, u32[]{:S(2)}, u32[]{:S(2)}) collective-permute-start(bf16[1,1,1,1,72,384]{5,4,3,2,1,0:T(8,128)(2,1)S(1)} %constant_dynamic-slice_fusion.17), channel_id=1, source_target_pairs={{0,16},{2,18},{4,20},{6,22},{8,24},{10,26},{12,28},{14,30},{16,0},... | collective-permute-start | bytes 165896 | tf_op jit(solution)/shard_map/ppermute | solution.py:533
  200.6 36.2 %collective-permute-start.41 = (bf16[1,1,1,1,48,576]{5,4,3,2,1,0:T(8,128)(2,1)S(1)}, bf16[1,1,1,1,48,576]{5,4,3,2,1,0:T(8,128)(2,1)S(1)}, u32[]{:S(2)}, u32[]{:S(2)}) collective-permute-start(bf16[1,1,1,1,48,576]{5,4,3,2,1,0:T(8,128)(2,1)S(1)} %constant_dynamic-slice_fusion.15), channel_id=1, source_target_pairs={{0,16},{2,18},{4,20},{6,22},{8,24},{10,26},{12,28},{14,30},{16,0},... | collective-permute-start | bytes 165896 | tf_op jit(solution)/shard_map/ppermute | solution.py:533
  200.7 36.3 %collective-permute-start.42 = (bf16[2,1,2,1,48,384]{5,4,3,2,1,0:T(8,128)(2,1)S(1)}, bf16[2,1,2,1,48,384]{5,4,3,2,1,0:T(8,128)(2,1)S(1)}, u32[]{:S(2)}, u32[]{:S(2)}) collective-permute-start(bf16[2,1,2,1,48,384]{5,4,3,2,1,0:T(8,128)(2,1)S(1)} %constant_dynamic-slice_fusion.14), channel_id=1, source_target_pairs={{0,2},{2,0},{4,6},{6,4},{8,10},{10,8},{12,14},{14,12},{16,18},{18,... | collective-permute-start | bytes 442376 | tf_op jit(solution)/shard_map/ppermute | solution.py:533
  243.4 14.4 %collective-permute-start.46 = (bf16[2,1,1,1,48,384]{5,4,3,2,1,0:T(8,128)(2,1)S(1)}, bf16[2,1,1,1,48,384]{5,4,3,2,1,0:T(8,128)(2,1)S(1)}, u32[]{:S(2)}, u32[]{:S(2)}) collective-permute-start(bf16[2,1,1,1,48,384]{5,4,3,2,1,0:T(8,128)(2,1)S(1)} %constant_dynamic-slice_fusion.13), channel_id=1, source_target_pairs={{0,4},{2,6},{4,0},{6,2},{8,12},{10,14},{12,8},{14,10},{16,20},{18,... | collective-permute-start | bytes 221192 | tf_op jit(solution)/shard_map/ppermute | solution.py:533
  244.7 13.0 %collective-permute-start.44 = (bf16[1,1,1,1,72,384]{5,4,3,2,1,0:T(8,128)(2,1)S(1)}, bf16[1,1,1,1,72,384]{5,4,3,2,1,0:T(8,128)(2,1)S(1)}, u32[]{:S(2)}, u32[]{:S(2)}) collective-permute-start(bf16[1,1,1,1,72,384]{5,4,3,2,1,0:T(8,128)(2,1)S(1)} %get-tuple-element.354), channel_id=1, source_target_pairs={{0,16},{2,18},{4,20},{6,22},{8,24},{10,26},{12,28},{14,30},{16,0},... | collective-permute-start | bytes 165896 | tf_op jit(solution)/shard_map/ppermute | solution.py:533
  262.7 10.2 %collective-permute-start.53 = (bf16[1,1,1,1,48,384]{5,4,3,2,1,0:T(8,128)(2,1)S(1)}, bf16[1,1,1,1,48,384]{5,4,3,2,1,0:T(8,128)(2,1)S(1)}, u32[]{:S(2)}, u32[]{:S(2)}) collective-permute-start(bf16[1,1,1,1,48,384]{5,4,3,2,1,0:T(8,128)(2,1)S(1)} %constant_dynamic-slice_fusion.9), channel_id=1, source_target_pairs={{0,16},{2,18},{4,20},{6,22},{8,24},{10,26},{12,28},{14,30},{16,0},... | collective-permute-start | bytes 110600 | tf_op jit(solution)/shard_map/ppermute | solution.py:533
  265.2 12.6 %collective-permute-start.50 = (bf16[2,1,1,1,72,384]{5,4,3,2,1,0:T(8,128)(2,1)S(1)}, bf16[2,1,1,1,72,384]{5,4,3,2,1,0:T(8,128)(2,1)S(1)}, u32[]{:S(2)}, u32[]{:S(2)}) collective-permute-start(bf16[2,1,1,1,72,384]{5,4,3,2,1,0:T(8,128)(2,1)S(1)} %pad_maximum_fusion.48), channel_id=1, source_target_pairs={{0,8},{2,10},{4,12},{6,14},{8,0},{10,2},{12,4},{14,6},{16,24},{18,... | collective-permute-start | bytes 331784 | tf_op jit(solution)/shard_map/ppermute | solution.py:533
  269.4 10.5 %collective-permute-start.51 = (bf16[2,1,1,1,72,384]{5,4,3,2,1,0:T(8,128)(2,1)S(1)}, bf16[2,1,1,1,72,384]{5,4,3,2,1,0:T(8,128)(2,1)S(1)}, u32[]{:S(2)}, u32[]{:S(2)}) collective-permute-start(bf16[2,1,1,1,72,384]{5,4,3,2,1,0:T(8,128)(2,1)S(1)} %pad_maximum_fusion.49), channel_id=1, source_target_pairs={{0,2},{2,0},{4,6},{6,4},{8,10},{10,8},{12,14},{14,12},{16,18},{18,... | collective-permute-start | bytes 331784 | tf_op jit(solution)/shard_map/ppermute | solution.py:533
  273.0 15.6 %collective-permute-start.54 = (bf16[1024,768]{1,0:T(8,128)(2,1)S(1)}, bf16[1024,768]{1,0:T(8,128)(2,1)S(1)}, u32[]{:S(2)}, u32[]{:S(2)}) collective-permute-start(bf16[1024,768]{1,0:T(8,128)(2,1)S(1)} %fusion.14), channel_id=1, source_target_pairs={{0,1},{1,0},{2,3},{3,2},{4,5},{5,4},{6,7},{7,6},{8,9},{9,8},{10,11... | collective-permute-start | bytes 4718600 | tf_op jit(solution)/shard_map/ppermute | solution.py:533
  307.8 12.9 %collective-permute-start.64 = (bf16[2,2,2,1,72,384]{5,4,3,2,1,0:T(8,128)(2,1)S(1)}, bf16[2,2,2,1,72,384]{5,4,3,2,1,0:T(8,128)(2,1)S(1)}, u32[]{:S(2)}, u32[]{:S(2)}) collective-permute-start(bf16[2,2,2,1,72,384]{5,4,3,2,1,0:T(8,128)(2,1)S(1)} %pad_maximum_fusion.22), channel_id=1, source_target_pairs={{0,2},{2,0},{4,6},{6,4},{8,10},{10,8},{12,14},{14,12},{16,18},{18,... | collective-permute-start | bytes 1327112 | tf_op jit(solution)/shard_map/ppermute | solution.py:533
  311.3 11.7 %collective-permute-start.65 = (bf16[2,2,1,2,72,384]{5,4,3,2,1,0:T(8,128)(2,1)S(1)}, bf16[2,2,1,2,72,384]{5,4,3,2,1,0:T(8,128)(2,1)S(1)}, u32[]{:S(2)}, u32[]{:S(2)}) collective-permute-start(bf16[2,2,1,2,72,384]{5,4,3,2,1,0:T(8,128)(2,1)S(1)} %pad_maximum_fusion.23), channel_id=1, source_target_pairs={{0,4},{2,6},{4,0},{6,2},{8,12},{10,14},{12,8},{14,10},{16,20},{18,... | collective-permute-start | bytes 1327112 | tf_op jit(solution)/shard_map/ppermute | solution.py:533
  312.2 12.5 %collective-permute-start.66 = (bf16[2,1,2,2,48,576]{5,4,3,2,1,0:T(8,128)(2,1)S(1)}, bf16[2,1,2,2,48,576]{5,4,3,2,1,0:T(8,128)(2,1)S(1)}, u32[]{:S(2)}, u32[]{:S(2)}) collective-permute-start(bf16[2,1,2,2,48,576]{5,4,3,2,1,0:T(8,128)(2,1)S(1)} %pad_maximum_fusion.19), channel_id=1, source_target_pairs={{0,8},{2,10},{4,12},{6,14},{8,0},{10,2},{12,4},{14,6},{16,24},{18,... | collective-permute-start | bytes 1327112 | tf_op jit(solution)/shard_map/ppermute | solution.py:533
  325.5 11.1 %collective-permute-start.69 = (bf16[1,1,1,1,72,256]{5,4,3,2,1,0:T(8,128)(2,1)}, bf16[1,1,1,1,72,256]{5,4,3,2,1,0:T(8,128)(2,1)}, u32[]{:S(2)}, u32[]{:S(2)}) collective-permute-start(bf16[1,1,1,1,72,256]{5,4,3,2,1,0:T(8,128)(2,1)} %constant_dynamic-slice_fusion), channel_id=1, source_target_pairs={{0,16},{2,18},{4,20},{6,22},{8,24},{10,26},{12,28},{14,30},{16,0},... | collective-permute-start | bytes 110600 | tf_op jit(solution)/shard_map/ppermute | solution.py:533
  327.9 9.6 %collective-permute-start.68 = (bf16[1,1,1,1,72,256]{5,4,3,2,1,0:T(8,128)(2,1)S(1)}, bf16[1,1,1,1,72,256]{5,4,3,2,1,0:T(8,128)(2,1)}, u32[]{:S(2)}, u32[]{:S(2)}) collective-permute-start(bf16[1,1,1,1,72,256]{5,4,3,2,1,0:T(8,128)(2,1)S(1)} %constant_dynamic-slice_fusion.1), channel_id=1, source_target_pairs={{0,16},{2,18},{4,20},{6,22},{8,24},{10,26},{12,28},{14,30},{16,0},... | collective-permute-start | bytes 110600 | tf_op jit(solution)/shard_map/ppermute | solution.py:533
  328.5 9.8 %collective-permute-start.67 = (bf16[1,1,1,1,72,256]{5,4,3,2,1,0:T(8,128)(2,1)S(1)}, bf16[1,1,1,1,72,256]{5,4,3,2,1,0:T(8,128)(2,1)}, u32[]{:S(2)}, u32[]{:S(2)}) collective-permute-start(bf16[1,1,1,1,72,256]{5,4,3,2,1,0:T(8,128)(2,1)S(1)} %constant_dynamic-slice_fusion.2), channel_id=1, source_target_pairs={{0,16},{2,18},{4,20},{6,22},{8,24},{10,26},{12,28},{14,30},{16,0},... | collective-permute-start | bytes 110600 | tf_op jit(solution)/shard_map/ppermute | solution.py:533
  343.7 16.0 %collective-permute-start.76 = (f32[2,768]{1,0:T(2,128)}, f32[2,768]{1,0:T(2,128)S(1)}, u32[]{:S(2)}, u32[]{:S(2)}) collective-permute-start(f32[2,768]{1,0:T(2,128)} %fusion.147), channel_id=1, source_target_pairs={{0,2},{2,0},{4,6},{6,4},{8,10},{10,8},{12,14},{14,12},{16,18},{18,... | collective-permute-start | bytes 18440 | tf_op jit(solution)/shard_map/ppermute | solution.py:533
  345.1 17.6 %collective-permute-start.75 = (bf16[2,1,1,1,48,384]{5,4,3,2,1,0:T(8,128)(2,1)S(1)}, bf16[2,1,1,1,48,384]{5,4,3,2,1,0:T(8,128)(2,1)S(1)}, u32[]{:S(2)}, u32[]{:S(2)}) collective-permute-start(bf16[2,1,1,1,48,384]{5,4,3,2,1,0:T(8,128)(2,1)S(1)} %copy-done.40), channel_id=1, source_target_pairs={{0,4},{2,6},{4,0},{6,2},{8,12},{10,14},{12,8},{14,10},{16,20},{18,... | collective-permute-start | bytes 221192 | tf_op jit(solution)/shard_map/ppermute | solution.py:533
  345.6 14.8 %collective-permute-start.74 = (bf16[1,1,1,1,72,256]{5,4,3,2,1,0:T(8,128)(2,1)S(1)}, bf16[1,1,1,1,72,256]{5,4,3,2,1,0:T(8,128)(2,1)}, u32[]{:S(2)}, u32[]{:S(2)}) collective-permute-start(bf16[1,1,1,1,72,256]{5,4,3,2,1,0:T(8,128)(2,1)S(1)} %get-tuple-element.351), channel_id=1, source_target_pairs={{0,16},{2,18},{4,20},{6,22},{8,24},{10,26},{12,28},{14,30},{16,0},... | collective-permute-start | bytes 110600 | tf_op jit(solution)/shard_map/ppermute | solution.py:533
  347.0 14.1 %collective-permute-start.73 = (bf16[1,1,1,1,72,256]{5,4,3,2,1,0:T(8,128)(2,1)S(1)}, bf16[1,1,1,1,72,256]{5,4,3,2,1,0:T(8,128)(2,1)}, u32[]{:S(2)}, u32[]{:S(2)}) collective-permute-start(bf16[1,1,1,1,72,256]{5,4,3,2,1,0:T(8,128)(2,1)S(1)} %get-tuple-element.352), channel_id=1, source_target_pairs={{0,16},{2,18},{4,20},{6,22},{8,24},{10,26},{12,28},{14,30},{16,0},... | collective-permute-start | bytes 110600 | tf_op jit(solution)/shard_map/ppermute | solution.py:533
  348.6 13.4 %collective-permute-start.72 = (bf16[1,1,1,1,72,256]{5,4,3,2,1,0:T(8,128)(2,1)S(1)}, bf16[1,1,1,1,72,256]{5,4,3,2,1,0:T(8,128)(2,1)}, u32[]{:S(2)}, u32[]{:S(2)}) collective-permute-start(bf16[1,1,1,1,72,256]{5,4,3,2,1,0:T(8,128)(2,1)S(1)} %get-tuple-element.353), channel_id=1, source_target_pairs={{0,16},{2,18},{4,20},{6,22},{8,24},{10,26},{12,28},{14,30},{16,0},... | collective-permute-start | bytes 110600 | tf_op jit(solution)/shard_map/ppermute | solution.py:533
  362.8 11.6 %collective-permute-start.81 = (f32[2,768]{1,0:T(2,128)S(1)}, f32[2,768]{1,0:T(2,128)S(1)}, u32[]{:S(2)}, u32[]{:S(2)}) collective-permute-start(f32[2,768]{1,0:T(2,128)S(1)} %add.457), channel_id=1, source_target_pairs={{0,4},{2,6},{4,0},{6,2},{8,12},{10,14},{12,8},{14,10},{16,20},{18,... | collective-permute-start | bytes 18440 | tf_op jit(solution)/shard_map/ppermute | solution.py:533
  363.6 10.7 %collective-permute-start.77 = (bf16[2,1,1,1,72,256]{5,4,3,2,1,0:T(8,128)(2,1)S(1)}, bf16[2,1,1,1,72,256]{5,4,3,2,1,0:T(8,128)(2,1)S(1)}, u32[]{:S(2)}, u32[]{:S(2)}) collective-permute-start(bf16[2,1,1,1,72,256]{5,4,3,2,1,0:T(8,128)(2,1)S(1)} %pad_maximum_fusion.55), channel_id=1, source_target_pairs={{0,8},{2,10},{4,12},{6,14},{8,0},{10,2},{12,4},{14,6},{16,24},{18,... | collective-permute-start | bytes 221192 | tf_op jit(solution)/shard_map/ppermute | solution.py:533
  364.9 9.5 %collective-permute-start.78 = (bf16[2,1,1,1,72,256]{5,4,3,2,1,0:T(8,128)(2,1)S(1)}, bf16[2,1,1,1,72,256]{5,4,3,2,1,0:T(8,128)(2,1)S(1)}, u32[]{:S(2)}, u32[]{:S(2)}) collective-permute-start(bf16[2,1,1,1,72,256]{5,4,3,2,1,0:T(8,128)(2,1)S(1)} %pad_maximum_fusion.56), channel_id=1, source_target_pairs={{0,2},{2,0},{4,6},{6,4},{8,10},{10,8},{12,14},{14,12},{16,18},{18,... | collective-permute-start | bytes 221192 | tf_op jit(solution)/shard_map/ppermute | solution.py:533
  366.0 8.4 %collective-permute-start.79 = (bf16[2,1,1,1,72,256]{5,4,3,2,1,0:T(8,128)(2,1)S(1)}, bf16[2,1,1,1,72,256]{5,4,3,2,1,0:T(8,128)(2,1)S(1)}, u32[]{:S(2)}, u32[]{:S(2)}) collective-permute-start(bf16[2,1,1,1,72,256]{5,4,3,2,1,0:T(8,128)(2,1)S(1)} %pad_maximum_fusion.57), channel_id=1, source_target_pairs={{0,4},{2,6},{4,0},{6,2},{8,12},{10,14},{12,8},{14,10},{16,20},{18,... | collective-permute-start | bytes 221192 | tf_op jit(solution)/shard_map/ppermute | solution.py:533
  375.3 13.1 %collective-permute-start.86 = (f32[2,768]{1,0:T(2,128)S(1)}, f32[2,768]{1,0:T(2,128)S(1)}, u32[]{:S(2)}, u32[]{:S(2)}) collective-permute-start(f32[2,768]{1,0:T(2,128)S(1)} %add.465), channel_id=1, source_target_pairs={{0,8},{2,10},{4,12},{6,14},{8,0},{10,2},{12,4},{14,6},{16,24},{18,... | collective-permute-start | bytes 18440 | tf_op jit(solution)/shard_map/ppermute | solution.py:533
  375.4 13.0 %collective-permute-start.82 = (bf16[2,2,1,1,72,256]{5,4,3,2,1,0:T(8,128)(2,1)S(1)}, bf16[2,2,1,1,72,256]{5,4,3,2,1,0:T(8,128)(2,1)S(1)}, u32[]{:S(2)}, u32[]{:S(2)}) collective-permute-start(bf16[2,2,1,1,72,256]{5,4,3,2,1,0:T(8,128)(2,1)S(1)} %pad_maximum_fusion.42), channel_id=1, source_target_pairs={{0,4},{2,6},{4,0},{6,2},{8,12},{10,14},{12,8},{14,10},{16,20},{18,... | collective-permute-start | bytes 442376 | tf_op jit(solution)/shard_map/ppermute | solution.py:533
  375.6 12.7 %collective-permute-start.83 = (bf16[2,1,1,2,72,256]{5,4,3,2,1,0:T(8,128)(2,1)S(1)}, bf16[2,1,1,2,72,256]{5,4,3,2,1,0:T(8,128)(2,1)S(1)}, u32[]{:S(2)}, u32[]{:S(2)}) collective-permute-start(bf16[2,1,1,2,72,256]{5,4,3,2,1,0:T(8,128)(2,1)S(1)} %pad_maximum_fusion.43), channel_id=1, source_target_pairs={{0,8},{2,10},{4,12},{6,14},{8,0},{10,2},{12,4},{14,6},{16,24},{18,... | collective-permute-start | bytes 442376 | tf_op jit(solution)/shard_map/ppermute | solution.py:533
  377.3 11.1 %collective-permute-start.84 = (bf16[2,1,2,1,72,256]{5,4,3,2,1,0:T(8,128)(2,1)S(1)}, bf16[2,1,2,1,72,256]{5,4,3,2,1,0:T(8,128)(2,1)S(1)}, u32[]{:S(2)}, u32[]{:S(2)}) collective-permute-start(bf16[2,1,2,1,72,256]{5,4,3,2,1,0:T(8,128)(2,1)S(1)} %pad_maximum_fusion.44), channel_id=1, source_target_pairs={{0,2},{2,0},{4,6},{6,4},{8,10},{10,8},{12,14},{14,12},{16,18},{18,... | collective-permute-start | bytes 442376 | tf_op jit(solution)/shard_map/ppermute | solution.py:533
  378.2 10.3 %collective-permute-start.85 = (bf16[2,1,2,2,48,384]{5,4,3,2,1,0:T(8,128)(2,1)S(1)}, bf16[2,1,2,2,48,384]{5,4,3,2,1,0:T(8,128)(2,1)S(1)}, u32[]{:S(2)}, u32[]{:S(2)}) collective-permute-start(bf16[2,1,2,2,48,384]{5,4,3,2,1,0:T(8,128)(2,1)S(1)} %pad_maximum_fusion.28), channel_id=1, source_target_pairs={{0,8},{2,10},{4,12},{6,14},{8,0},{10,2},{12,4},{14,6},{16,24},{18,... | collective-permute-start | bytes 884744 | tf_op jit(solution)/shard_map/ppermute | solution.py:533
  394.3 8.6 %collective-permute-start.90 = (f32[2,768]{1,0:T(2,128)S(1)}, f32[2,768]{1,0:T(2,128)S(1)}, u32[]{:S(2)}, u32[]{:S(2)}) collective-permute-start(f32[2,768]{1,0:T(2,128)S(1)} %add.470), channel_id=1, source_target_pairs={{0,16},{2,18},{4,20},{6,22},{8,24},{10,26},{12,28},{14,30},{16,0},... | collective-permute-start | bytes 18440 | tf_op jit(solution)/shard_map/ppermute | solution.py:533
  (105 other events, 932.1 us)

commit v2 on v1

--- a/solution.py
+++ b/solution.py
@@ -621,27 +621,71 @@
     return jnp.concatenate([first, second], axis=0)
 
 
-def schulz_start(own, gathered):
-    gram = dot(gathered, gathered, TN)
-    norm_value = jnp.sqrt(jnp.trace(gram)) + 1e-07
-    return own / norm_value, gram / (norm_value * norm_value)
-
-
-def schulz_step(state, last=False):
-    rows, gram = state
-    low_gram = gram.astype(bf16)
-    change = (ns_second * gram + ns_third * dot(low_gram, low_gram, NN)).astype(bf16)
-    rows = ns_first * rows + dot(rows.astype(bf16), change, NN)
-    if last:
-        return rows
-    once = ns_first * gram + dot(low_gram, change, NN)
-    return rows, ns_first * once + dot(once.astype(bf16), change, NN)
-
-
-def schulz_rest(state):
+def schulz_kernel(*refs, count, offset, scale):
+    parts = refs[:count]
+    own, weight, updated, gram, low, change = refs[count:]
+    columns = gram.shape[0]
+    lines = 256 if columns % 256 == 0 else columns
+    if offset is None:
+        held = [part[...] for part in parts]
+    else:
+        held = [parts[0][:, offset : offset + columns]]
+    down = 0
+    for left in held:
+        along = 0
+        for right in held:
+            gram[down : down + left.shape[1], along : along + right.shape[1]] = dot(left, right, TN)
+            along += right.shape[1]
+        down += left.shape[1]
+    shape = (columns, columns)
+    diagonal = lax.broadcasted_iota(jnp.int32, shape, 0) == lax.broadcasted_iota(jnp.int32, shape, 1)
+    trace = jnp.sum(jnp.where(diagonal, gram[...], 0.0), axis=0, keepdims=True)
+    norm_value = jnp.sqrt(jnp.sum(trace, axis=1, keepdims=True)) + 1e-07
+    rows = own[...] / norm_value
+    shrunk = 1.0 / (norm_value * norm_value)
+    gram[...] = gram[...] * shrunk
+    low[...] = gram[...].astype(bf16)
+
+    def per_block(body):
+        def run(index, carry):
+            body(pl.ds(pl.multiple_of(index * lines, lines), lines))
+            return carry
+
+        lax.fori_loop(0, columns // lines, run, 0)
+
+    def form_change(block):
+        squared = dot(low[block, :], low[...], NN)
+        change[block, :] = (ns_second * gram[block, :] + ns_third * squared).astype(bf16)
+
+    def next_gram(block):
+        once = ns_first * gram[block, :] + dot(low[block, :], change[...], NN)
+        twice = ns_first * once + dot(once.astype(bf16), change[...], NN)
+        gram[block, :] = twice
+        low[block, :] = twice.astype(bf16)
+
     for iteration in range(NS_ITERS):
-        state = schulz_step(state, iteration + 1 == NS_ITERS)
-    return state
+        per_block(form_change)
+        rows = ns_first * rows + dot(rows.astype(bf16), change[...], NN)
+        if iteration + 1 < NS_ITERS:
+            per_block(next_gram)
+    updated[...] = weight[...] - scale * rows
+
+
+def schulz(parts, offset, own, weight, name):
+    columns = own.shape[1]
+    shape_scale = muon_rate * math.sqrt(parts[0].shape[0] / columns)
+    kernel = functools.partial(schulz_kernel, count=len(parts), offset=offset, scale=shape_scale)
+    return pl.pallas_call(
+        kernel,
+        out_shape=jax.ShapeDtypeStruct(own.shape, f32),
+        scratch_shapes=[
+            pltpu.VMEM((columns, columns), f32),
+            pltpu.VMEM((columns, columns), bf16),
+            pltpu.VMEM((columns, columns), bf16),
+        ],
+        compiler_params=pltpu.CompilerParams(vmem_limit_bytes=40 << 20),
+        name=name,
+    )(*parts, own, weight)
 
 
 def shards(
@@ -683,12 +727,11 @@
     others = quarter(ordered_step, others, 0)
     joined_parts, others = tie(joined_parts, others)
     joined_parts = quarter(ordered_step, joined_parts, 2)
-    moved = quarter(ordered_step, others, 1)
-    joined_parts, first_low = tie(joined_parts, first_low)
+    others = quarter(ordered_step, others, 1)
+    joined_parts, others, first_low = tie(joined_parts, others, first_low)
     joined_parts = quarter(ordered_step, joined_parts, 3)
-    joined_parts, others = tie(joined_parts, moved)
-
     moved = quarter(ordered_step, others, 2)
+
     joined_low = jnp.concatenate([gather_rows(part) for part in joined_parts], axis=1)
     joined = dot(joined_low, first_low, NT)
     width = joined.shape[0] // 3
@@ -712,136 +755,117 @@
     )
     second_other = swap(second_part, "head", 1)
 
-    sums, second_other = tie(
-        [reduce_start(part) for part in halves_of(expand_grad) + [shrink_grad.T]], second_other
-    )
+    sums, second_other = tie([reduce_start(part) for part in halves_of(expand_grad)], second_other)
     moved = quarter(reduce_step, sums, 0)
     middle_grad, attended_grad, mixer_grad, second_gain_grad = norm_backward(
         middle, second_part, second_other, cotangent, second_gain, mixer_low, attended
     )
     second_gain_grad = 0.5 * second_gain_grad[0]
+    both_sum = [reduce_start(jnp.concatenate([mixer_grad, shrink_grad.T], axis=1))]
 
     sums, attended_grad, shrink_now = tie(moved, attended_grad, shrink_turned)
     moved = quarter(reduce_step, sums, 1)
 
-    def fed(columns, weight):
-        return dot(lax.dynamic_slice_in_dim(hidden, columns, local_rows, 1), weight, TN)
-
-    fed_other = fed((1 - head) * local_rows, shrink_now).astype(bf16)
-    sums, mixer_grad, fed_other, shrink_now = tie(moved, mixer_grad, fed_other, shrink_now)
+    def fed(columns):
+        return dot(lax.dynamic_slice_in_dim(hidden, columns, local_rows, 1), shrink_now, TN)
+
+    fed_other = fed((1 - head) * local_rows).astype(bf16)
+    fed_own = fed(head * local_rows)
+
+    sums, both_sum, fed_other, fed_own, low = tie(moved, both_sum, fed_other, fed_own, low)
     moved = quarter(reduce_step, sums, 2)
-    mixer_moved = quarter(reduce_step, [reduce_start(mixer_grad)], 0, 2)
-    fed_own = fed(head * local_rows, shrink_now)
-
-    sums, mixer_sum, fed_own, low = tie(moved, mixer_moved, fed_own, low)
-    moved = quarter(reduce_step, sums, 3)
-    mixer_moved = quarter(reduce_step, mixer_sum, 1, 2)
+    both_moved = quarter(reduce_step, both_sum, 0, 2)
     fed_other = swap(fed_other, "head", 1)
     joined_back = attention_backward(
         low, high, queries, keys, values, attended_grad, attended, logsum, key_rows, query_rows,
         cosine, sine,
     )
-    sums, mixer_sum, joined_back = tie(moved, mixer_moved, joined_back)
-    expand_next = 0.5 * expand_momentum[0] + jnp.concatenate(sums[:2], axis=1)
-    shrink_next = 0.5 * shrink_momentum[0] + sums[2]
-    gathers = [gather_start(part) for part in halves_of(expand_next.astype(bf16))]
-    gathers.append(gather_start(shrink_next.astype(bf16)))
-
-    moved = quarter(gather_step, gathers, 0)
-    mixer_moved = quarter(reduce_step, mixer_sum, 2, 2)
+    sums, both_sum, joined_back = tie(moved, both_moved, joined_back)
+    moved = quarter(reduce_step, sums, 3)
+    both_moved = quarter(reduce_step, both_sum, 1, 2)
     joined_grad = dot(joined_back, first_low, NN).astype(bf16)
 
     def first_part(start, weight):
         columns = lax.dynamic_slice_in_dim(joined_back, start, local_rows, 1)
         return dot(columns, weight, TN)
 
-    gathers, mixer_sum, joined_grad, joined_now = tie(moved, mixer_moved, joined_grad, joined_low)
+    sums, both_sum, joined_grad, joined_now = tie(moved, both_moved, joined_grad, joined_low)
+    expand_next = 0.5 * expand_momentum[0] + jnp.concatenate(sums, axis=1)
+    gathers = [gather_start(part) for part in halves_of(expand_next.astype(bf16))]
     sums = quarter(reduce_step, [reduce_start(part) for part in thirds(joined_grad)], 0)
-    moved = quarter(gather_step, gathers, 1)
-    mixer_moved = quarter(reduce_step, mixer_sum, 3, 2)
+    moved = quarter(gather_step, gathers, 0)
+    both_moved = quarter(reduce_step, both_sum, 2, 2)
     first_other = swap(
         first_part((1 - head) * local_rows, joined_now).astype(bf16), "head", 1
     )
     first_mine = first_part(head * local_rows, joined_now)
-    layer_output = (own_half(middle) + fed_own + fed_other.astype(f32)).astype(bf16)
-
-    sums, gathers, mixer_sum, first_other, first_mine = tie(
-        sums, moved, mixer_moved, first_other, first_mine
-    )
-    mixer_next = 0.5 * mixer_momentum[0] + mixer_sum[0]
+
+    sums, gathers, both_sum, first_other, first_mine = tie(
+        sums, moved, both_moved, first_other, first_mine
+    )
     moved = quarter(reduce_step, sums, 1)
-    gathers_moved = quarter(gather_step, gathers, 2)
+    gathers_moved = quarter(gather_step, gathers, 1)
+    both_moved = quarter(reduce_step, both_sum, 3, 2)
     first_back = first_mine + first_other.astype(f32)
     own_normal = own_half(first_normal)
     first_gain_grad = jnp.sum(first_back * own_normal, axis=0)
 
-    sums, gathers, first_gain_grad, first_gain = tie(
-        moved, gathers_moved, first_gain_grad, norm_gains[0]
-    )
+    sums, gathers, both_sum, first_gain_grad, first_gain = tie(
+        moved, gathers_moved, both_moved, first_gain_grad, norm_gains[0]
+    )
+    mixer_next = 0.5 * mixer_momentum[0] + both_sum[0][:, :mixer_width]
+    shrink_next = 0.5 * shrink_momentum[0] + both_sum[0][:, mixer_width:]
+    both_gather = [gather_start(jnp.concatenate([mixer_next, shrink_next], axis=1).astype(bf16))]
+    gain_totals = jnp.stack([first_gain_grad, second_gain_grad])
     moved = quarter(reduce_step, sums, 2)
-    gathers_moved = quarter(gather_step, gathers, 3)
+    gathers_moved = quarter(gather_step, gathers, 2)
+    both_moved = quarter(gather_step, both_gather, 0, 2)
+    gain_moved = total_step(gain_totals, 0)
     input_gradient = own_half(middle_grad) + norm_back(
         first_back, first_gain, own_normal, own_half(first_inverse)
     )
 
-    sums, gathers, input_gradient = tie(moved, gathers_moved, input_gradient)
-    mixer_gather = [gather_start(mixer_next.astype(bf16))]
-    gain_totals = jnp.stack([first_gain_grad, second_gain_grad])
-    expand_full = jnp.concatenate([gather_rows(state) for state in gathers[:2]], axis=1)
-    shrink_full = gather_rows(gathers[2])
-
+    sums, gathers, both_gather, gain_totals, input_gradient, fed_own = tie(
+        moved, gathers_moved, both_moved, gain_moved, input_gradient, fed_own
+    )
     moved = quarter(reduce_step, sums, 3)
-    mixer_moved = quarter(gather_step, mixer_gather, 0, 2)
-    gain_moved = total_step(gain_totals, 0)
-    shrink_state = schulz_step(schulz_start(shrink_next, shrink_full))
-    sums, mixer_gather, gain_totals, shrink_state, expand_full = tie(
-        moved, mixer_moved, gain_moved, shrink_state, expand_full
+    gathers_moved = quarter(gather_step, gathers, 3)
+    both_moved = quarter(gather_step, both_gather, 1, 2)
+    gain_moved = total_step(gain_totals, 1)
+    layer_output = (own_half(middle) + fed_own + fed_other.astype(f32)).astype(bf16)
+
+    sums, gathers, both_gather, gain_totals, layer_output = tie(
+        moved, gathers_moved, both_moved, gain_moved, layer_output
     )
     joined_next = 0.5 * joined_momentum[0] + jnp.concatenate(sums, axis=1)
     joined_gather = [gather_start(part) for part in thirds(joined_next.astype(bf16))]
-
     moved = quarter(gather_step, joined_gather, 0)
-    mixer_moved = quarter(gather_step, mixer_gather, 1, 2)
-    gain_moved = total_step(gain_totals, 1)
-    shrink_rows = schulz_step(schulz_step(shrink_state), True)
-    expand_state = schulz_start(expand_next, expand_full)
-    joined_gather, mixer_gather, gain_totals, shrink_rows, expand_state = tie(
-        moved, mixer_moved, gain_moved, shrink_rows, expand_state
-    )
-
+    both_moved = quarter(gather_step, both_gather, 2, 2)
+    gain_moved = total_step(gain_totals, 2)
+    updated_expand = schulz(
+        [gather_rows(part) for part in gathers], None, expand_next, expand_weight[0], "schulz_expand"
+    )
+    joined_gather, both_gather, gain_totals, updated_expand = tie(
+        moved, both_moved, gain_moved, updated_expand
+    )
     moved = quarter(gather_step, joined_gather, 1)
-    mixer_moved = quarter(gather_step, mixer_gather, 2, 2)
-    gain_moved = total_step(gain_totals, 2)
-    expand_state = schulz_step(expand_state)
-    joined_gather, mixer_gather, gain_totals, expand_state = tie(
-        moved, mixer_moved, gain_moved, expand_state
-    )
-
+    both_moved = quarter(gather_step, both_gather, 3, 2)
+    gain_moved = total_step(gain_totals, 3)
+    joined_gather, both_gather, gain_totals = tie(moved, both_moved, gain_moved)
+    both_full = [gather_rows(both_gather[0])]
     moved = quarter(gather_step, joined_gather, 2)
-    mixer_moved = quarter(gather_step, mixer_gather, 3, 2)
-    gain_moved = total_step(gain_totals, 3)
-    expand_rows = schulz_step(schulz_step(expand_state), True)
-    joined_gather, mixer_gather, gain_totals, expand_rows = tie(
-        moved, mixer_moved, gain_moved, expand_rows
-    )
-
+    gain_totals = total_step(gain_totals, 4)
+    updated_shrink = schulz(
+        both_full, mixer_width, shrink_next, shrink_weight[0], "schulz_shrink"
+    )
+    joined_gather, both_full, updated_shrink = tie(moved, both_full, updated_shrink)
     moved = quarter(gather_step, joined_gather, 3)
-    gain_totals = total_step(gain_totals, 4)
-    mixer_rows = schulz_rest(schulz_start(mixer_next, gather_rows(mixer_gather[0])))
-    joined_gather, mixer_rows = tie(moved, mixer_rows)
-    joined_full = jnp.concatenate([gather_rows(state) for state in joined_gather], axis=1)
-    joined_rows = schulz_rest(schulz_start(joined_next, joined_full))
-
-    dp_count = lax.axis_size("dp")
-    updated = []
-    for weight, rows in (
-        (joined_weight, joined_rows),
-        (mixer_weight, mixer_rows),
-        (expand_weight, expand_rows),
-        (shrink_weight, shrink_rows),
-    ):
-        shape_scale = math.sqrt(rows.shape[0] * dp_count / rows.shape[1])
-        updated.append((weight[0] - muon_rate * shape_scale * rows)[None])
+    updated_mixer = schulz(both_full, 0, mixer_next, mixer_weight[0], "schulz_mixer")
+    joined_gather, updated_mixer = tie(moved, updated_mixer)
+    updated_joined = schulz(
+        [gather_rows(part) for part in joined_gather],
+        None, joined_next, joined_weight[0], "schulz_joined",
+    )
 
     momentum_gains = 0.5 * gain_momentum + gain_totals
     updated_gains = norm_gains - gain_rate * momentum_gains * lax.rsqrt(
@@ -854,10 +878,10 @@
         mixer_next[None],
         expand_next[None],
         shrink_next[None],
-        updated[0],
-        updated[1],
-        updated[2],
-        updated[3],
+        updated_joined[None],
+        updated_mixer[None],
+        updated_expand[None],
+        updated_shrink[None],
         momentum_gains,
         updated_gains,
     )

time: 433 us -> 410 us (0.947)
  matrix products: 71.7 us -> 19 us
  Pallas kernels: 103 us -> 149 us
  starting transfers between devices: 116 us -> 99.3 us
  waiting for transfers between devices: 67.9 us -> 80.9 us
  other arithmetic: 50.6 us -> 40.8 us
    dot_general x46 -> x6, matrix products: 71.7 us -> 19 us  [dot(): return lax.dot_general(left, right, dims, preferred_element_type=f32)]
    pallas_call x0 -> x4, Pallas kernels: none -> 39.6 us  [schulz(): pl.pallas_call(kernel, out_shape=jax.ShapeDtypeStruct(own.shape, f32), sc...]
    ppermute x91 -> x83, starting transfers between devices: 116 us -> 99.3 us  [swap(): return lax.ppermute(value, axis, [(i, i ^ bit) for i in range(count)])]
    ppermute x91 -> x83, waiting for transfers between devices: 67.9 us -> 80.9 us  [swap(): return lax.ppermute(value, axis, [(i, i ^ bit) for i in range(count)])]
  transfers between devices with their start and end apart: 91 -> 83, of which waited for: 31 -> 30; matrix products, arithmetic and copies ran while one was open for 22% -> 14% of each run, Pallas kernels for 16% -> 25%
where the time goes in v2:
time: 410 us; the launch traced here: 405 us
  Pallas kernels  149 us (36%)
  starting transfers between devices  99.3 us (24%)
  waiting for transfers between devices  80.9 us (20%)
  other arithmetic  40.8 us (10%)
  matrix products  19 us (5%)
  local copies, waits for them, and re-layouts  12.7 us (3%)
    ppermute x83, starting transfers between devices, swap(): return lax.ppermute(value, axis, [(i, i ^ bit) for i in range(count)])  99.3 us
    ppermute x83, waiting for transfers between devices, swap(): return lax.ppermute(value, axis, [(i, i ^ bit) for i in range(count)])  80.9 us
    pallas_call x4, Pallas kernels, schulz(): pl.pallas_call(kernel, out_shape=jax.ShapeDtypeStruct(own.shape, f32), sc...  39.6 us
    pallas_call x1, Pallas kernels, attention_backward(): pl.pallas_call(backward_kernel, out_shape=jax.ShapeDtypeStruct((3 * width...  38.9 us
    pallas_call x1, Pallas kernels, feed_forward(): pl.pallas_call(feed_kernel, grid=(count // FEED_ROWS,), in_specs=[down(wi...  35.5 us
    pallas_call x1, Pallas kernels, attention_forward(): pl.pallas_call(forward_kernel, out_shape=(jax.ShapeDtypeStruct((width, ro...  21.7 us
    dot_general x6, matrix products, dot(): return lax.dot_general(left, right, dims, preferred_element_type=f32)  19 us
    pallas_call x1, Pallas kernels, norm_backward(): pl.pallas_call(norm_kernel, grid=(count // FEED_ROWS,), in_specs=[down(wi...  13 us
  transfers between devices with their start and end apart: 83, of which 30 were waited for; matrix products, arithmetic and copies ran while one was open for 14% of the time, Pallas kernels for 25%

profile of v2, /device:TPU:0, one launch (start us, length us, event | category | flops | bytes accessed | tf_op | source)
XLA Modules:
  0.0 404.5 jit_solution(13648195426792499831)
XLA Ops:
  1.6 4.1 %collective-permute-start.3 = (bf16[1,1,1,1,72,256]{5,4,3,2,1,0:T(8,128)(2,1)S(1)}, bf16[1,1,1,1,72,256]{5,4,3,2,1,0:T(8,128)(2,1)S(1)}, u32[]{:S(2)}, u32[]{:S(2)}) collective-permute-start(bf16[1,1,1,1,72,256]{5,4,3,2,1,0:T(8,128)(2,1)S(1)} %get-tuple-element.336), channel_id=1, source_target_pairs={{0,16},{2,18},{4,20},{6,22},{8,24},{10,26},{12,28},{14,30},{16,0},... | collective-permute-start | bytes 110600 | tf_op jit(solution)/shard_map/ppermute | solution.py:533
  5.8 2.8 collective-permute-start.1
  16.1 2.9 collective-permute-start.8
  25.7 2.5 collective-permute-done.6
  28.3 2.8 collective-permute-done.9
  36.3 2.1 collective-permute-start.12
  41.6 2.6 collective-permute-done.15
  45.1 3.2 fusion.2
  48.3 3.8 fusion
  56.6 3.2 collective-permute-done.16
  60.8 3.0 collective-permute-done.19
  65.3 3.9 fusion.21
  74.7 21.7 %attention_forward.1 = (bf16[384,2048]{1,0:T(8,128)(2,1)}, f32[6,2048]{1,0:T(8,128)S(1)}) custom-call(s32[8]{0:T(128)S(1)} %get-tuple-element.177.low, s32[8]{0:T(128)S(1)} %get-tuple-element.343.high, bf16[384,2048]{1,0:T(8,128)(2,1)S(1)} %bitcast.128, bf16[384,2048]{1,0:T(8,128)(2,1)S(1)} %bitcast.126, bf16[384,2048]{1,0:T(8,128)(2,1)S(1)} %slice.168.values, ...), custom_call_target="tpu_custom_call" | custom-call | tf_op jit(solution)/shard_map/attention_forward/pallas_call | solution.py:207
  104.2 2.8 pad_maximum_fusion.2.expand
  106.9 35.5 %feed_forward.1 = (f32[2048,768]{1,0:T(8,128)}, bf16[576,2048]{1,0:T(8,128)(2,1)}, bf16[2048,768]{1,0:T(8,128)(2,1)}, bf16[576,768]{1,0:T(8,128)(2,1)S(1)}, bf16[1152,768]{1,0:T(8,128)(2,1)}) custom-call(bf16[2048,768]{1,0:T(8,128)(2,1)} %pad_maximum_fusion.rows, bf16[384,2048]{1,0:T(8,128)(2,1)} %get-tuple-element.157.attended.outs, ...), custom_call_target="tpu_custom_call" | custom-call | tf_op jit(solution)/shard_map/feed_forward/pallas_call | solution.py:445
  145.2 4.2 %collective-permute-done.27.other = bf16[2048,768]{1,0:T(8,128)(2,1)} collective-permute-done((bf16[2048,768]{1,0:T(8,128)(2,1)}, bf16[2048,768]{1,0:T(8,128)(2,1)}, u32[]{:S(2)}, u32[]{:S(2)}) %collective-permute-start.27) | collective-permute-done | bytes 3145760 | tf_op jit(solution)/shard_map/ppermute | solution.py:533
  150.2 3.2 collective-permute-start.29
  155.5 13.0 %norm_backward.1 = (f32[2048,768]{1,0:T(8,128)}, bf16[384,2048]{1,0:T(8,128)(2,1)S(1)}, bf16[768,384]{1,0:T(8,128)(2,1)S(1)}, f32[1,768]{1,0:T(1,128)S(1)}) custom-call(f32[2048,768]{1,0:T(8,128)} %get-tuple-element.165.middle, bf16[2048,768]{1,0:T(8,128)(2,1)S(1)} %copy-done.4, bf16[2048,768]{1,0:T(8,128)(2,1)} %collective-permute-done.27.other, ...), custom_call_target="tpu_custom_call" | custom-call | tf_op jit(solution)/shard_map/norm_backward/pallas_call | solution.py:509
  173.6 4.7 %collective-permute-start.31 = (bf16[2,1,1,2,72,384]{5,4,3,2,1,0:T(8,128)(2,1)S(1)}, bf16[2,1,1,2,72,384]{5,4,3,2,1,0:T(8,128)(2,1)S(1)}, u32[]{:S(2)}, u32[]{:S(2)}) collective-permute-start(bf16[2,1,1,2,72,384]{5,4,3,2,1,0:T(8,128)(2,1)S(1)} %constant_dynamic-slice_fusion.20), channel_id=1, source_target_pairs={{0,8},{2,10},{4,12},{6,14},{8,0},{10,2},{12,4},{14,6},{16,24},{18,... | collective-permute-start | bytes 663560 | tf_op jit(solution)/shard_map/ppermute | solution.py:533
  179.8 2.6 convolution_convert_fusion.1
  182.4 2.5 collective-permute-done.30
  188.3 38.9 %attention_backward.1 = bf16[1152,2048]{1,0:T(8,128)(2,1)} custom-call(s32[8]{0:T(128)S(1)} %get-tuple-element.177.low, s32[8]{0:T(128)S(1)} %get-tuple-element.343.high, bf16[384,2048]{1,0:T(8,128)(2,1)} %bitcast.129, bf16[384,2048]{1,0:T(8,128)(2,1)} %bitcast.127, bf16[384,2048]{1,0:T(8,128)(2,1)} %copy-done.1, bf16[384,2048]{1,0:T(8,128)(2,1)} %copy-done.7, ...), custom_call_target="tpu_custom_call" | custom-call | tf_op jit(solution)/shard_map/attention_backward/pallas_call | solution.py:324
  228.6 6.3 %convolution_convert_fusion = bf16[1152,768]{1,0:T(8,128)(2,1)S(1)} fusion(bf16[1152,2048]{1,0:T(8,128)(2,1)} %attention_backward.1, bf16[2048,768]{1,0:T(8,128)(2,1)S(1)} %copy-done.22), kind=kOutput, calls=%fused_computation.6 | convolution fusion | flops 3624763392 | bytes 9633792 | tf_op jit(solution)/shard_map/dot_general | solution.py:51
  234.9 4.0 collective-permute-start.36
  241.5 2.5 collective-permute-done.35
  244.0 6.3 %collective-permute-done.37 = bf16[2,1,2,1,48,960]{5,4,3,2,1,0:T(8,128)(2,1)S(1)} collective-permute-done((bf16[2,1,2,1,48,960]{5,4,3,2,1,0:T(8,128)(2,1)S(1)}, bf16[2,1,2,1,48,960]{5,4,3,2,1,0:T(8,128)(2,1)S(1)}, u32[]{:S(2)}, u32[]{:S(2)}) %collective-permute-start.37) | collective-permute-done | bytes 368672 | tf_op jit(solution)/shard_map/ppermute | solution.py:533
  250.6 2.4 fusion.8
  253.0 2.4 fusion.4
  255.5 3.7 collective-permute-start.43
  259.7 2.6 collective-permute-start.41
  262.3 2.6 collective-permute-done.42
  265.7 4.2 %collective-permute-start.40 = (bf16[2,1,2,2,72,256]{5,4,3,2,1,0:T(8,128)(2,1)S(1)}, bf16[2,1,2,2,72,256]{5,4,3,2,1,0:T(8,128)(2,1)S(1)}, u32[]{:S(2)}, u32[]{:S(2)}) collective-permute-start(bf16[2,1,2,2,72,256]{5,4,3,2,1,0:T(8,128)(2,1)S(1)} %constant_dynamic-slice_fusion.11), channel_id=1, source_target_pairs={{0,8},{2,10},{4,12},{6,14},{8,0},{10,2},{12,4},{14,6},{16,24},{18,... | collective-permute-start | bytes 884744 | tf_op jit(solution)/shard_map/ppermute | solution.py:533
  270.6 2.4 collective-permute-done.38
  273.1 2.8 collective-permute-done.40
  286.2 3.0 collective-permute-done.46
  295.0 2.4 multiply_add_fusion
  299.3 2.1 collective-permute-start.55
  301.5 3.5 collective-permute-done.56
  305.0 3.0 collective-permute-done.55
  317.5 3.2 collective-permute-done.63
  320.8 4.5 %collective-permute-done.61 = bf16[2,2,2,1,72,384]{5,4,3,2,1,0:T(8,128)(2,1)S(1)} collective-permute-done((bf16[2,2,2,1,72,384]{5,4,3,2,1,0:T(8,128)(2,1)S(1)}, bf16[2,2,2,1,72,384]{5,4,3,2,1,0:T(8,128)(2,1)S(1)}, u32[]{:S(2)}, u32[]{:S(2)}) %collective-permute-start.61) | collective-permute-done | bytes 442400 | tf_op jit(solution)/shard_map/ppermute | solution.py:533
  325.4 2.4 collective-permute-done.62
  327.9 2.2 collective-permute-start.68
  334.7 14.3 %schulz_expand.1 = f32[72,768]{1,0:T(8,128)} custom-call(bf16[1152,384]{1,0:T(8,128)(2,1)S(1)} %bitcast.130, bf16[1152,384]{1,0:T(8,128)(2,1)S(1)} %bitcast.131, f32[72,768]{1,0:T(8,128)S(1)} %get-tuple-element.259.refs_2_, f32[72,768]{1,0:T(8,128)S(1)} %bitcast.135), custom_call_target="tpu_custom_call" | custom-call | tf_op jit(solution)/shard_map/schulz_expand/pallas_call | solution.py:678
  354.8 10.9 %collective-permute-done.75 = f32[2,768]{1,0:T(2,128)S(1)} collective-permute-done((f32[2,768]{1,0:T(2,128)S(1)}, f32[2,768]{1,0:T(2,128)S(1)}, u32[]{:S(2)}, u32[]{:S(2)}) %collective-permute-start.75) | collective-permute-done | bytes 6176 | tf_op jit(solution)/shard_map/ppermute | solution.py:533
  373.2 7.6 %schulz_shrink.1 = f32[48,576]{1,0:T(8,128)} custom-call(bf16[768,960]{1,0:T(8,128)(2,1)S(1)} %bitcast.124, f32[48,576]{1,0:T(8,128)S(1)} %get-tuple-element.257.refs_1_, f32[48,576]{1,0:T(8,128)S(1)} %bitcast.138), custom_call_target="tpu_custom_call" | custom-call | tf_op jit(solution)/shard_map/schulz_shrink/pallas_call | solution.py:678
  384.3 3.8 schulz_mixer.1
  390.1 13.9 %schulz_joined.1 = f32[72,768]{1,0:T(8,128)} custom-call(bf16[1152,256]{1,0:T(8,128)(2,1)S(1)} %bitcast.132, bf16[1152,256]{1,0:T(8,128)(2,1)S(1)} %bitcast.133, bf16[1152,256]{1,0:T(8,128)(2,1)S(1)} %bitcast.134, f32[72,768]{1,0:T(8,128)S(1)} %get-tuple-element.253.refs_3_, f32[72,768]{1,0:T(8,128)S(1)} %bitcast.136), custom_call_target="tpu_custom_call" | custom-call | tf_op jit(solution)/shard_map/schulz_joined/pallas_call | solution.py:678
  (429 shorter events, 116.6 us)
Async XLA Ops:
  1.6 14.1 %collective-permute-start.3 = (bf16[1,1,1,1,72,256]{5,4,3,2,1,0:T(8,128)(2,1)S(1)}, bf16[1,1,1,1,72,256]{5,4,3,2,1,0:T(8,128)(2,1)S(1)}, u32[]{:S(2)}, u32[]{:S(2)}) collective-permute-start(bf16[1,1,1,1,72,256]{5,4,3,2,1,0:T(8,128)(2,1)S(1)} %get-tuple-element.336), channel_id=1, source_target_pairs={{0,16},{2,18},{4,20},{6,22},{8,24},{10,26},{12,28},{14,30},{16,0},... | collective-permute-start | bytes 110600 | tf_op jit(solution)/shard_map/ppermute | solution.py:533
  5.7 10.0 %collective-permute-start.2 = (bf16[1,1,1,1,72,256]{5,4,3,2,1,0:T(8,128)(2,1)S(1)}, bf16[1,1,1,1,72,256]{5,4,3,2,1,0:T(8,128)(2,1)S(1)}, u32[]{:S(2)}, u32[]{:S(2)}) collective-permute-start(bf16[1,1,1,1,72,256]{5,4,3,2,1,0:T(8,128)(2,1)S(1)} %get-tuple-element.337), channel_id=1, source_target_pairs={{0,16},{2,18},{4,20},{6,22},{8,24},{10,26},{12,28},{14,30},{16,0},... | collective-permute-start | bytes 110600 | tf_op jit(solution)/shard_map/ppermute | solution.py:533
  5.8 9.9 %collective-permute-start.1 = (bf16[1,1,1,1,72,256]{5,4,3,2,1,0:T(8,128)(2,1)S(1)}, bf16[1,1,1,1,72,256]{5,4,3,2,1,0:T(8,128)(2,1)S(1)}, u32[]{:S(2)}, u32[]{:S(2)}) collective-permute-start(bf16[1,1,1,1,72,256]{5,4,3,2,1,0:T(8,128)(2,1)S(1)} %get-tuple-element.338), channel_id=1, source_target_pairs={{0,16},{2,18},{4,20},{6,22},{8,24},{10,26},{12,28},{14,30},{16,0},... | collective-permute-start | bytes 110600 | tf_op jit(solution)/shard_map/ppermute | solution.py:533
  8.7 35.5 %collective-permute-start = (bf16[1024,768]{1,0:T(8,128)(2,1)}, bf16[1024,768]{1,0:T(8,128)(2,1)S(1)}, u32[]{:S(2)}, u32[]{:S(2)}) collective-permute-start(bf16[1024,768]{1,0:T(8,128)(2,1)} %param.13), channel_id=1, source_target_pairs={{0,1},{1,0},{2,3},{3,2},{4,5},{5,4},{6,7},{7,6},{8,9},{9,8},{10,11... | collective-permute-start | bytes 4718600 | tf_op jit(solution)/shard_map/ppermute | solution.py:533
  15.8 8.1 %collective-permute-start.7 = (bf16[1,1,1,1,72,384]{5,4,3,2,1,0:T(8,128)(2,1)S(1)}, bf16[1,1,1,1,72,384]{5,4,3,2,1,0:T(8,128)(2,1)S(1)}, u32[]{:S(2)}, u32[]{:S(2)}) collective-permute-start(bf16[1,1,1,1,72,384]{5,4,3,2,1,0:T(8,128)(2,1)S(1)} %get-tuple-element.132), channel_id=1, source_target_pairs={{0,16},{2,18},{4,20},{6,22},{8,24},{10,26},{12,28},{14,30},{16,0},... | collective-permute-start | bytes 165896 | tf_op jit(solution)/shard_map/ppermute | solution.py:533
  16.1 9.4 %collective-permute-start.8 = (bf16[1,1,1,1,72,384]{5,4,3,2,1,0:T(8,128)(2,1)S(1)}, bf16[1,1,1,1,72,384]{5,4,3,2,1,0:T(8,128)(2,1)S(1)}, u32[]{:S(2)}, u32[]{:S(2)}) collective-permute-start(bf16[1,1,1,1,72,384]{5,4,3,2,1,0:T(8,128)(2,1)S(1)} %get-tuple-element.133), channel_id=1, source_target_pairs={{0,16},{2,18},{4,20},{6,22},{8,24},{10,26},{12,28},{14,30},{16,0},... | collective-permute-start | bytes 165896 | tf_op jit(solution)/shard_map/ppermute | solution.py:533
  52.1 7.6 %collective-permute-start.16 = (bf16[2,2,1,1,72,384]{5,4,3,2,1,0:T(8,128)(2,1)S(1)}, bf16[2,2,1,1,72,384]{5,4,3,2,1,0:T(8,128)(2,1)S(1)}, u32[]{:S(2)}, u32[]{:S(2)}) collective-permute-start(bf16[2,2,1,1,72,384]{5,4,3,2,1,0:T(8,128)(2,1)S(1)} %pad_maximum_fusion.31), channel_id=1, source_target_pairs={{0,4},{2,6},{4,0},{6,2},{8,12},{10,14},{12,8},{14,10},{16,20},{18,... | collective-permute-start | bytes 663560 | tf_op jit(solution)/shard_map/ppermute | solution.py:533
  53.9 9.9 %collective-permute-start.19 = (bf16[2,2,2,1,72,256]{5,4,3,2,1,0:T(8,128)(2,1)S(1)}, bf16[2,2,2,1,72,256]{5,4,3,2,1,0:T(8,128)(2,1)S(1)}, u32[]{:S(2)}, u32[]{:S(2)}) collective-permute-start(bf16[2,2,2,1,72,256]{5,4,3,2,1,0:T(8,128)(2,1)S(1)} %pad_maximum_fusion.25), channel_id=1, source_target_pairs={{0,2},{2,0},{4,6},{6,4},{8,10},{10,8},{12,14},{14,12},{16,18},{18,... | collective-permute-start | bytes 884744 | tf_op jit(solution)/shard_map/ppermute | solution.py:533
  54.9 9.0 %collective-permute-start.20 = (bf16[2,2,1,2,72,256]{5,4,3,2,1,0:T(8,128)(2,1)S(1)}, bf16[2,2,1,2,72,256]{5,4,3,2,1,0:T(8,128)(2,1)S(1)}, u32[]{:S(2)}, u32[]{:S(2)}) collective-permute-start(bf16[2,2,1,2,72,256]{5,4,3,2,1,0:T(8,128)(2,1)S(1)} %pad_maximum_fusion.26), channel_id=1, source_target_pairs={{0,4},{2,6},{4,0},{6,2},{8,12},{10,14},{12,8},{14,10},{16,20},{18,... | collective-permute-start | bytes 884744 | tf_op jit(solution)/shard_map/ppermute | solution.py:533
  56.5 7.7 %collective-permute-start.21 = (bf16[2,1,2,2,72,256]{5,4,3,2,1,0:T(8,128)(2,1)S(1)}, bf16[2,1,2,2,72,256]{5,4,3,2,1,0:T(8,128)(2,1)S(1)}, u32[]{:S(2)}, u32[]{:S(2)}) collective-permute-start(bf16[2,1,2,2,72,256]{5,4,3,2,1,0:T(8,128)(2,1)S(1)} %pad_maximum_fusion.27), channel_id=1, source_target_pairs={{0,8},{2,10},{4,12},{6,14},{8,0},{10,2},{12,4},{14,6},{16,24},{18,... | collective-permute-start | bytes 884744 | tf_op jit(solution)/shard_map/ppermute | solution.py:533
  59.7 11.9 %collective-permute-start.18 = (bf16[2,1,2,1,48,960]{5,4,3,2,1,0:T(8,128)(2,1)S(1)}, bf16[2,1,2,1,48,960]{5,4,3,2,1,0:T(8,128)(2,1)S(1)}, u32[]{:S(2)}, u32[]{:S(2)}) collective-permute-start(bf16[2,1,2,1,48,960]{5,4,3,2,1,0:T(8,128)(2,1)S(1)} %pad_maximum_fusion.23), channel_id=1, source_target_pairs={{0,2},{2,0},{4,6},{6,4},{8,10},{10,8},{12,14},{14,12},{16,18},{18,... | collective-permute-start | bytes 1105928 | tf_op jit(solution)/shard_map/ppermute | solution.py:533
  71.8 24.6 %collective-permute-start.22 = (bf16[2,2,2,1,72,384]{5,4,3,2,1,0:T(8,128)(2,1)S(1)}, bf16[2,2,2,1,72,384]{5,4,3,2,1,0:T(8,128)(2,1)S(1)}, u32[]{:S(2)}, u32[]{:S(2)}) collective-permute-start(bf16[2,2,2,1,72,384]{5,4,3,2,1,0:T(8,128)(2,1)S(1)} %pad_maximum_fusion.19), channel_id=1, source_target_pairs={{0,2},{2,0},{4,6},{6,4},{8,10},{10,8},{12,14},{14,12},{16,18},{18,... | collective-permute-start | bytes 1327112 | tf_op jit(solution)/shard_map/ppermute | solution.py:533
  72.8 24.8 %collective-permute-start.23 = (bf16[2,2,1,2,72,384]{5,4,3,2,1,0:T(8,128)(2,1)S(1)}, bf16[2,2,1,2,72,384]{5,4,3,2,1,0:T(8,128)(2,1)S(1)}, u32[]{:S(2)}, u32[]{:S(2)}) collective-permute-start(bf16[2,2,1,2,72,384]{5,4,3,2,1,0:T(8,128)(2,1)S(1)} %pad_maximum_fusion.20), channel_id=1, source_target_pairs={{0,4},{2,6},{4,0},{6,2},{8,12},{10,14},{12,8},{14,10},{16,20},{18,... | collective-permute-start | bytes 1327112 | tf_op jit(solution)/shard_map/ppermute | solution.py:533
  73.7 25.0 %collective-permute-start.24 = (bf16[2,1,2,2,48,960]{5,4,3,2,1,0:T(8,128)(2,1)S(1)}, bf16[2,1,2,2,48,960]{5,4,3,2,1,0:T(8,128)(2,1)S(1)}, u32[]{:S(2)}, u32[]{:S(2)}) collective-permute-start(bf16[2,1,2,2,48,960]{5,4,3,2,1,0:T(8,128)(2,1)S(1)} %pad_maximum_fusion.11), channel_id=1, source_target_pairs={{0,8},{2,10},{4,12},{6,14},{8,0},{10,2},{12,4},{14,6},{16,24},{18,... | collective-permute-start | bytes 2211848 | tf_op jit(solution)/shard_map/ppermute | solution.py:533
  99.0 8.0 %collective-permute-start.25 = (bf16[384,2048]{1,0:T(8,128)(2,1)}, bf16[384,2048]{1,0:T(8,128)(2,1)S(1)}, u32[]{:S(2)}, u32[]{:S(2)}) collective-permute-start(bf16[384,2048]{1,0:T(8,128)(2,1)} %get-tuple-element.157.attended.outs), channel_id=1, source_target_pairs={{0,1},{1,0},{2,3},{3,2},{4,5},{5,4},{6,7},{7,6},{8,9},{9,8},{10,11... | collective-permute-start | bytes 4718600 | tf_op jit(solution)/shard_map/ppermute | solution.py:533
  99.1 7.8 %collective-permute-start.26 = (bf16[768,384]{1,0:T(8,128)(2,1)S(1)}, bf16[768,384]{1,0:T(8,128)(2,1)}, u32[]{:S(2)}, u32[]{:S(2)}) collective-permute-start(bf16[768,384]{1,0:T(8,128)(2,1)S(1)} %slice.126.mixer), channel_id=1, source_target_pairs={{0,1},{1,0},{2,3},{3,2},{4,5},{5,4},{6,7},{7,6},{8,9},{9,8},{10,11... | collective-permute-start | bytes 1769480 | tf_op jit(solution)/shard_map/ppermute | solution.py:533
  150.2 20.6 %collective-permute-start.29 = (bf16[2,2,1,2,72,384]{5,4,3,2,1,0:T(8,128)(2,1)}, bf16[2,2,1,2,72,384]{5,4,3,2,1,0:T(8,128)(2,1)}, u32[]{:S(2)}, u32[]{:S(2)}) collective-permute-start(bf16[2,2,1,2,72,384]{5,4,3,2,1,0:T(8,128)(2,1)} %constant_dynamic-slice_fusion.22), channel_id=1, source_target_pairs={{0,4},{2,6},{4,0},{6,2},{8,12},{10,14},{12,8},{14,10},{16,20},{18,... | collective-permute-start | bytes 1327112 | tf_op jit(solution)/shard_map/ppermute | solution.py:533
  154.2 18.1 %collective-permute-start.28 = (bf16[2,2,2,1,72,384]{5,4,3,2,1,0:T(8,128)(2,1)}, bf16[2,2,2,1,72,384]{5,4,3,2,1,0:T(8,128)(2,1)}, u32[]{:S(2)}, u32[]{:S(2)}) collective-permute-start(bf16[2,2,2,1,72,384]{5,4,3,2,1,0:T(8,128)(2,1)} %constant_dynamic-slice_fusion.23), channel_id=1, source_target_pairs={{0,2},{2,0},{4,6},{6,4},{8,10},{10,8},{12,14},{14,12},{16,18},{18,... | collective-permute-start | bytes 1327112 | tf_op jit(solution)/shard_map/ppermute | solution.py:533
  173.6 11.4 %collective-permute-start.31 = (bf16[2,1,1,2,72,384]{5,4,3,2,1,0:T(8,128)(2,1)S(1)}, bf16[2,1,1,2,72,384]{5,4,3,2,1,0:T(8,128)(2,1)S(1)}, u32[]{:S(2)}, u32[]{:S(2)}) collective-permute-start(bf16[2,1,1,2,72,384]{5,4,3,2,1,0:T(8,128)(2,1)S(1)} %constant_dynamic-slice_fusion.20), channel_id=1, source_target_pairs={{0,8},{2,10},{4,12},{6,14},{8,0},{10,2},{12,4},{14,6},{16,24},{18,... | collective-permute-start | bytes 663560 | tf_op jit(solution)/shard_map/ppermute | solution.py:533
  185.2 43.0 %collective-permute-start.34 = (bf16[2,1,2,2,48,960]{5,4,3,2,1,0:T(8,128)(2,1)S(1)}, bf16[2,1,2,2,48,960]{5,4,3,2,1,0:T(8,128)(2,1)S(1)}, u32[]{:S(2)}, u32[]{:S(2)}) collective-permute-start(bf16[2,1,2,2,48,960]{5,4,3,2,1,0:T(8,128)(2,1)S(1)} %constant_dynamic-slice_fusion.17), channel_id=1, source_target_pairs={{0,8},{2,10},{4,12},{6,14},{8,0},{10,2},{12,4},{14,6},{16,24},{18,... | collective-permute-start | bytes 2211848 | tf_op jit(solution)/shard_map/ppermute | solution.py:533
  186.2 41.0 %collective-permute-start.33 = (bf16[2,1,1,1,72,384]{5,4,3,2,1,0:T(8,128)(2,1)S(1)}, bf16[2,1,1,1,72,384]{5,4,3,2,1,0:T(8,128)(2,1)}, u32[]{:S(2)}, u32[]{:S(2)}) collective-permute-start(bf16[2,1,1,1,72,384]{5,4,3,2,1,0:T(8,128)(2,1)S(1)} %constant_dynamic-slice_fusion.18), channel_id=1, source_target_pairs={{0,2},{2,0},{4,6},{6,4},{8,10},{10,8},{12,14},{14,12},{16,18},{18,... | collective-permute-start | bytes 331784 | tf_op jit(solution)/shard_map/ppermute | solution.py:533
  186.6 41.6 %collective-permute-start.32 = (bf16[2,1,1,1,72,384]{5,4,3,2,1,0:T(8,128)(2,1)S(1)}, bf16[2,1,1,1,72,384]{5,4,3,2,1,0:T(8,128)(2,1)S(1)}, u32[]{:S(2)}, u32[]{:S(2)}) collective-permute-start(bf16[2,1,1,1,72,384]{5,4,3,2,1,0:T(8,128)(2,1)S(1)} %constant_dynamic-slice_fusion.19), channel_id=1, source_target_pairs={{0,8},{2,10},{4,12},{6,14},{8,0},{10,2},{12,4},{14,6},{16,24},{18,... | collective-permute-start | bytes 331784 | tf_op jit(solution)/shard_map/ppermute | solution.py:533
  188.3 124.6 %collective-permute-start.65 = (bf16[1024,768]{1,0:T(8,128)(2,1)}, bf16[1024,768]{1,0:T(8,128)(2,1)S(1)}, u32[]{:S(2)}, u32[]{:S(2)}) collective-permute-start(bf16[1024,768]{1,0:T(8,128)(2,1)} %convolution_convert_fusion.1), channel_id=1, source_target_pairs={{0,1},{1,0},{2,3},{3,2},{4,5},{5,4},{6,7},{7,6},{8,9},{9,8},{10,11... | collective-permute-start | bytes 4718600 | tf_op jit(solution)/shard_map/ppermute | solution.py:533
  239.1 11.3 %collective-permute-start.37 = (bf16[2,1,2,1,48,960]{5,4,3,2,1,0:T(8,128)(2,1)S(1)}, bf16[2,1,2,1,48,960]{5,4,3,2,1,0:T(8,128)(2,1)S(1)}, u32[]{:S(2)}, u32[]{:S(2)}) collective-permute-start(bf16[2,1,2,1,48,960]{5,4,3,2,1,0:T(8,128)(2,1)S(1)} %constant_dynamic-slice_fusion.14), channel_id=1, source_target_pairs={{0,2},{2,0},{4,6},{6,4},{8,10},{10,8},{12,14},{14,12},{16,18},{18,... | collective-permute-start | bytes 1105928 | tf_op jit(solution)/shard_map/ppermute | solution.py:533
  255.5 14.4 %collective-permute-start.43 = (bf16[2,1,1,1,48,960]{5,4,3,2,1,0:T(8,128)(2,1)S(1)}, bf16[2,1,1,1,48,960]{5,4,3,2,1,0:T(8,128)(2,1)S(1)}, u32[]{:S(2)}, u32[]{:S(2)}) collective-permute-start(bf16[2,1,1,1,48,960]{5,4,3,2,1,0:T(8,128)(2,1)S(1)} %constant_dynamic-slice_fusion.10), channel_id=1, source_target_pairs={{0,4},{2,6},{4,0},{6,2},{8,12},{10,14},{12,8},{14,10},{16,20},{18,... | collective-permute-start | bytes 552968 | tf_op jit(solution)/shard_map/ppermute | solution.py:533
  259.2 18.4 %collective-permute-start.44 = (bf16[1024,768]{1,0:T(8,128)(2,1)S(1)}, bf16[1024,768]{1,0:T(8,128)(2,1)S(1)}, u32[]{:S(2)}, u32[]{:S(2)}) collective-permute-start(bf16[1024,768]{1,0:T(8,128)(2,1)S(1)} %fusion.8), channel_id=1, source_target_pairs={{0,1},{1,0},{2,3},{3,2},{4,5},{5,4},{6,7},{7,6},{8,9},{9,8},{10,11... | collective-permute-start | bytes 4718600 | tf_op jit(solution)/shard_map/ppermute | solution.py:533
  264.9 8.1 %collective-permute-start.38 = (bf16[2,2,2,1,72,256]{5,4,3,2,1,0:T(8,128)(2,1)S(1)}, bf16[2,2,2,1,72,256]{5,4,3,2,1,0:T(8,128)(2,1)S(1)}, u32[]{:S(2)}, u32[]{:S(2)}) collective-permute-start(bf16[2,2,2,1,72,256]{5,4,3,2,1,0:T(8,128)(2,1)S(1)} %constant_dynamic-slice_fusion.13), channel_id=1, source_target_pairs={{0,2},{2,0},{4,6},{6,4},{8,10},{10,8},{12,14},{14,12},{16,18},{18,... | collective-permute-start | bytes 884744 | tf_op jit(solution)/shard_map/ppermute | solution.py:533
  265.7 10.3 %collective-permute-start.40 = (bf16[2,1,2,2,72,256]{5,4,3,2,1,0:T(8,128)(2,1)S(1)}, bf16[2,1,2,2,72,256]{5,4,3,2,1,0:T(8,128)(2,1)S(1)}, u32[]{:S(2)}, u32[]{:S(2)}) collective-permute-start(bf16[2,1,2,2,72,256]{5,4,3,2,1,0:T(8,128)(2,1)S(1)} %constant_dynamic-slice_fusion.11), channel_id=1, source_target_pairs={{0,8},{2,10},{4,12},{6,14},{8,0},{10,2},{12,4},{14,6},{16,24},{18,... | collective-permute-start | bytes 884744 | tf_op jit(solution)/shard_map/ppermute | solution.py:533
  293.4 8.0 %collective-permute-start.51 = (bf16[2,1,1,1,72,256]{5,4,3,2,1,0:T(8,128)(2,1)S(1)}, bf16[2,1,1,1,72,256]{5,4,3,2,1,0:T(8,128)(2,1)S(1)}, u32[]{:S(2)}, u32[]{:S(2)}) collective-permute-start(bf16[2,1,1,1,72,256]{5,4,3,2,1,0:T(8,128)(2,1)S(1)} %constant_dynamic-slice_fusion.5), channel_id=1, source_target_pairs={{0,8},{2,10},{4,12},{6,14},{8,0},{10,2},{12,4},{14,6},{16,24},{18,... | collective-permute-start | bytes 221192 | tf_op jit(solution)/shard_map/ppermute | solution.py:533
  299.3 8.7 %collective-permute-start.55 = (bf16[2,1,1,2,72,384]{5,4,3,2,1,0:T(8,128)(2,1)S(1)}, bf16[2,1,1,2,72,384]{5,4,3,2,1,0:T(8,128)(2,1)S(1)}, u32[]{:S(2)}, u32[]{:S(2)}) collective-permute-start(bf16[2,1,1,2,72,384]{5,4,3,2,1,0:T(8,128)(2,1)S(1)} %pad_maximum_fusion.34), channel_id=1, source_target_pairs={{0,8},{2,10},{4,12},{6,14},{8,0},{10,2},{12,4},{14,6},{16,24},{18,... | collective-permute-start | bytes 663560 | tf_op jit(solution)/shard_map/ppermute | solution.py:533
  308.1 7.8 %collective-permute-start.64 = (f32[2,768]{1,0:T(2,128)S(1)}, f32[2,768]{1,0:T(2,128)S(1)}, u32[]{:S(2)}, u32[]{:S(2)}) collective-permute-start(f32[2,768]{1,0:T(2,128)S(1)} %fusion.20), channel_id=1, source_target_pairs={{0,2},{2,0},{4,6},{6,4},{8,10},{10,8},{12,14},{14,12},{16,18},{18,... | collective-permute-start | bytes 18440 | tf_op jit(solution)/shard_map/ppermute | solution.py:533
  312.9 7.8 %collective-permute-start.63 = (bf16[2,1,1,1,48,960]{5,4,3,2,1,0:T(8,128)(2,1)S(1)}, bf16[2,1,1,1,48,960]{5,4,3,2,1,0:T(8,128)(2,1)S(1)}, u32[]{:S(2)}, u32[]{:S(2)}) collective-permute-start(bf16[2,1,1,1,48,960]{5,4,3,2,1,0:T(8,128)(2,1)S(1)} %pad_maximum_fusion.36), channel_id=1, source_target_pairs={{0,4},{2,6},{4,0},{6,2},{8,12},{10,14},{12,8},{14,10},{16,20},{18,... | collective-permute-start | bytes 552968 | tf_op jit(solution)/shard_map/ppermute | solution.py:533
  315.8 9.4 %collective-permute-start.61 = (bf16[2,2,2,1,72,384]{5,4,3,2,1,0:T(8,128)(2,1)S(1)}, bf16[2,2,2,1,72,384]{5,4,3,2,1,0:T(8,128)(2,1)S(1)}, u32[]{:S(2)}, u32[]{:S(2)}) collective-permute-start(bf16[2,2,2,1,72,384]{5,4,3,2,1,0:T(8,128)(2,1)S(1)} %pad_maximum_fusion.21), channel_id=1, source_target_pairs={{0,2},{2,0},{4,6},{6,4},{8,10},{10,8},{12,14},{14,12},{16,18},{18,... | collective-permute-start | bytes 1327112 | tf_op jit(solution)/shard_map/ppermute | solution.py:533
  316.4 11.3 %collective-permute-start.62 = (bf16[2,2,1,2,72,384]{5,4,3,2,1,0:T(8,128)(2,1)S(1)}, bf16[2,2,1,2,72,384]{5,4,3,2,1,0:T(8,128)(2,1)S(1)}, u32[]{:S(2)}, u32[]{:S(2)}) collective-permute-start(bf16[2,2,1,2,72,384]{5,4,3,2,1,0:T(8,128)(2,1)S(1)} %pad_maximum_fusion.22), channel_id=1, source_target_pairs={{0,4},{2,6},{4,0},{6,2},{8,12},{10,14},{12,8},{14,10},{16,20},{18,... | collective-permute-start | bytes 1327112 | tf_op jit(solution)/shard_map/ppermute | solution.py:533
  327.9 21.1 %collective-permute-start.68 = (bf16[1,1,1,1,72,256]{5,4,3,2,1,0:T(8,128)(2,1)S(1)}, bf16[1,1,1,1,72,256]{5,4,3,2,1,0:T(8,128)(2,1)S(1)}, u32[]{:S(2)}, u32[]{:S(2)}) collective-permute-start(bf16[1,1,1,1,72,256]{5,4,3,2,1,0:T(8,128)(2,1)S(1)} %get-tuple-element.321), channel_id=1, source_target_pairs={{0,16},{2,18},{4,20},{6,22},{8,24},{10,26},{12,28},{14,30},{16,0},... | collective-permute-start | bytes 110600 | tf_op jit(solution)/shard_map/ppermute | solution.py:533
  330.1 19.0 %collective-permute-start.69 = (bf16[2,1,2,1,48,960]{5,4,3,2,1,0:T(8,128)(2,1)S(1)}, bf16[2,1,2,1,48,960]{5,4,3,2,1,0:T(8,128)(2,1)S(1)}, u32[]{:S(2)}, u32[]{:S(2)}) collective-permute-start(bf16[2,1,2,1,48,960]{5,4,3,2,1,0:T(8,128)(2,1)S(1)} %pad_maximum_fusion.24), channel_id=1, source_target_pairs={{0,2},{2,0},{4,6},{6,4},{8,10},{10,8},{12,14},{14,12},{16,18},{18,... | collective-permute-start | bytes 1105928 | tf_op jit(solution)/shard_map/ppermute | solution.py:533
  330.8 18.1 %collective-permute-start.70 = (f32[2,768]{1,0:T(2,128)S(1)}, f32[2,768]{1,0:T(2,128)S(1)}, u32[]{:S(2)}, u32[]{:S(2)}) collective-permute-start(f32[2,768]{1,0:T(2,128)S(1)} %add.289), channel_id=1, source_target_pairs={{0,4},{2,6},{4,0},{6,2},{8,12},{10,14},{12,8},{14,10},{16,20},{18,... | collective-permute-start | bytes 18440 | tf_op jit(solution)/shard_map/ppermute | solution.py:533
  331.8 17.3 %collective-permute-start.67 = (bf16[1,1,1,1,72,256]{5,4,3,2,1,0:T(8,128)(2,1)S(1)}, bf16[1,1,1,1,72,256]{5,4,3,2,1,0:T(8,128)(2,1)S(1)}, u32[]{:S(2)}, u32[]{:S(2)}) collective-permute-start(bf16[1,1,1,1,72,256]{5,4,3,2,1,0:T(8,128)(2,1)S(1)} %get-tuple-element.322), channel_id=1, source_target_pairs={{0,16},{2,18},{4,20},{6,22},{8,24},{10,26},{12,28},{14,30},{16,0},... | collective-permute-start | bytes 110600 | tf_op jit(solution)/shard_map/ppermute | solution.py:533
  333.0 16.0 %collective-permute-start.66 = (bf16[1,1,1,1,72,256]{5,4,3,2,1,0:T(8,128)(2,1)S(1)}, bf16[1,1,1,1,72,256]{5,4,3,2,1,0:T(8,128)(2,1)S(1)}, u32[]{:S(2)}, u32[]{:S(2)}) collective-permute-start(bf16[1,1,1,1,72,256]{5,4,3,2,1,0:T(8,128)(2,1)S(1)} %get-tuple-element.323), channel_id=1, source_target_pairs={{0,16},{2,18},{4,20},{6,22},{8,24},{10,26},{12,28},{14,30},{16,0},... | collective-permute-start | bytes 110600 | tf_op jit(solution)/shard_map/ppermute | solution.py:533
  349.2 17.5 %collective-permute-start.74 = (bf16[2,1,2,2,48,960]{5,4,3,2,1,0:T(8,128)(2,1)S(1)}, bf16[2,1,2,2,48,960]{5,4,3,2,1,0:T(8,128)(2,1)S(1)}, u32[]{:S(2)}, u32[]{:S(2)}) collective-permute-start(bf16[2,1,2,2,48,960]{5,4,3,2,1,0:T(8,128)(2,1)S(1)} %pad_maximum_fusion.12), channel_id=1, source_target_pairs={{0,8},{2,10},{4,12},{6,14},{8,0},{10,2},{12,4},{14,6},{16,24},{18,... | collective-permute-start | bytes 2211848 | tf_op jit(solution)/shard_map/ppermute | solution.py:533
  349.7 16.0 %collective-permute-start.75 = (f32[2,768]{1,0:T(2,128)S(1)}, f32[2,768]{1,0:T(2,128)S(1)}, u32[]{:S(2)}, u32[]{:S(2)}) collective-permute-start(f32[2,768]{1,0:T(2,128)S(1)} %add.295), channel_id=1, source_target_pairs={{0,8},{2,10},{4,12},{6,14},{8,0},{10,2},{12,4},{14,6},{16,24},{18,... | collective-permute-start | bytes 18440 | tf_op jit(solution)/shard_map/ppermute | solution.py:533
  351.3 15.3 %collective-permute-start.71 = (bf16[2,1,1,1,72,256]{5,4,3,2,1,0:T(8,128)(2,1)S(1)}, bf16[2,1,1,1,72,256]{5,4,3,2,1,0:T(8,128)(2,1)S(1)}, u32[]{:S(2)}, u32[]{:S(2)}) collective-permute-start(bf16[2,1,1,1,72,256]{5,4,3,2,1,0:T(8,128)(2,1)S(1)} %pad_maximum_fusion.52), channel_id=1, source_target_pairs={{0,8},{2,10},{4,12},{6,14},{8,0},{10,2},{12,4},{14,6},{16,24},{18,... | collective-permute-start | bytes 221192 | tf_op jit(solution)/shard_map/ppermute | solution.py:533
  352.5 14.2 %collective-permute-start.72 = (bf16[2,1,1,1,72,256]{5,4,3,2,1,0:T(8,128)(2,1)S(1)}, bf16[2,1,1,1,72,256]{5,4,3,2,1,0:T(8,128)(2,1)S(1)}, u32[]{:S(2)}, u32[]{:S(2)}) collective-permute-start(bf16[2,1,1,1,72,256]{5,4,3,2,1,0:T(8,128)(2,1)S(1)} %pad_maximum_fusion.53), channel_id=1, source_target_pairs={{0,2},{2,0},{4,6},{6,4},{8,10},{10,8},{12,14},{14,12},{16,18},{18,... | collective-permute-start | bytes 221192 | tf_op jit(solution)/shard_map/ppermute | solution.py:533
  353.5 13.2 %collective-permute-start.73 = (bf16[2,1,1,1,72,256]{5,4,3,2,1,0:T(8,128)(2,1)S(1)}, bf16[2,1,1,1,72,256]{5,4,3,2,1,0:T(8,128)(2,1)S(1)}, u32[]{:S(2)}, u32[]{:S(2)}) collective-permute-start(bf16[2,1,1,1,72,256]{5,4,3,2,1,0:T(8,128)(2,1)S(1)} %pad_maximum_fusion.54), channel_id=1, source_target_pairs={{0,4},{2,6},{4,0},{6,2},{8,12},{10,14},{12,8},{14,10},{16,20},{18,... | collective-permute-start | bytes 221192 | tf_op jit(solution)/shard_map/ppermute | solution.py:533
  366.9 13.9 %collective-permute-start.82 = (f32[2,768]{1,0:T(2,128)S(1)}, f32[2,768]{1,0:T(2,128)S(1)}, u32[]{:S(2)}, u32[]{:S(2)}) collective-permute-start(f32[2,768]{1,0:T(2,128)S(1)} %add.296), channel_id=1, source_target_pairs={{0,16},{2,18},{4,20},{6,22},{8,24},{10,26},{12,28},{14,30},{16,0},... | collective-permute-start | bytes 18440 | tf_op jit(solution)/shard_map/ppermute | solution.py:533
  369.6 11.4 %collective-permute-start.76 = (bf16[2,2,1,1,72,256]{5,4,3,2,1,0:T(8,128)(2,1)S(1)}, bf16[2,2,1,1,72,256]{5,4,3,2,1,0:T(8,128)(2,1)S(1)}, u32[]{:S(2)}, u32[]{:S(2)}) collective-permute-start(bf16[2,2,1,1,72,256]{5,4,3,2,1,0:T(8,128)(2,1)S(1)} %pad_maximum_fusion.40), channel_id=1, source_target_pairs={{0,4},{2,6},{4,0},{6,2},{8,12},{10,14},{12,8},{14,10},{16,20},{18,... | collective-permute-start | bytes 442376 | tf_op jit(solution)/shard_map/ppermute | solution.py:533
  371.2 9.8 %collective-permute-start.77 = (bf16[2,1,1,2,72,256]{5,4,3,2,1,0:T(8,128)(2,1)S(1)}, bf16[2,1,1,2,72,256]{5,4,3,2,1,0:T(8,128)(2,1)S(1)}, u32[]{:S(2)}, u32[]{:S(2)}) collective-permute-start(bf16[2,1,1,2,72,256]{5,4,3,2,1,0:T(8,128)(2,1)S(1)} %pad_maximum_fusion.41), channel_id=1, source_target_pairs={{0,8},{2,10},{4,12},{6,14},{8,0},{10,2},{12,4},{14,6},{16,24},{18,... | collective-permute-start | bytes 442376 | tf_op jit(solution)/shard_map/ppermute | solution.py:533
  373.0 8.1 %collective-permute-start.78 = (bf16[2,1,2,1,72,256]{5,4,3,2,1,0:T(8,128)(2,1)S(1)}, bf16[2,1,2,1,72,256]{5,4,3,2,1,0:T(8,128)(2,1)S(1)}, u32[]{:S(2)}, u32[]{:S(2)}) collective-permute-start(bf16[2,1,2,1,72,256]{5,4,3,2,1,0:T(8,128)(2,1)S(1)} %pad_maximum_fusion.42), channel_id=1, source_target_pairs={{0,2},{2,0},{4,6},{6,4},{8,10},{10,8},{12,14},{14,12},{16,18},{18,... | collective-permute-start | bytes 442376 | tf_op jit(solution)/shard_map/ppermute | solution.py:533
  (87 other events, 1122.6 us)

commit v3 on v2

--- a/solution.py
+++ b/solution.py
@@ -374,20 +374,181 @@
     return value * horner(square, ERF_TOP) / horner(square, ERF_BOTTOM)
 
 
+def turn(value):
+    columns = value.shape[1]
+    rest = jnp.zeros((value.shape[0], -columns % 128), value.dtype)
+    return jnp.concatenate([value, rest], axis=1).T[:columns, :]
+
+
+def turn_back(value):
+    lines = value.shape[0]
+    rest = jnp.zeros((-lines % 128, value.shape[1]), value.dtype)
+    return jnp.concatenate([value, rest], axis=0).T[:, :lines]
+
+
+def first_kernel(head, own, other, gain, rows, normed):
+    tiles = pl.num_programs(0) // 2
+    mine = pl.program_id(0) // tiles == head[0]
+    value = jnp.where(mine, own[...].astype(f32), other[...].astype(f32))
+    rows[...] = value.astype(bf16)
+    normed[...] = layer_norm(value, gain[...])[0].astype(bf16)
+
+
+def first_norm(head, own, other, gain):
+    half, width = own.shape
+    tiles = half // FEED_ROWS
+    result = jax.ShapeDtypeStruct((2 * half, width), bf16)
+    spec = pl.BlockSpec((FEED_ROWS, width), lambda i, head: (i, 0))
+    return pl.pallas_call(
+        first_kernel,
+        out_shape=(result, result),
+        grid_spec=pltpu.PrefetchScalarGridSpec(
+            num_scalar_prefetch=1,
+            grid=(2 * tiles,),
+            in_specs=[
+                pl.BlockSpec(
+                    (FEED_ROWS, width),
+                    lambda i, head: (jnp.clip(i - head[0] * tiles, 0, tiles - 1), 0),
+                ),
+                pl.BlockSpec(
+                    (FEED_ROWS, width),
+                    lambda i, head: (jnp.clip(i - (1 - head[0]) * tiles, 0, tiles - 1), 0),
+                ),
+                pl.BlockSpec((1, width), lambda i, head: (0, 0)),
+            ],
+            out_specs=[spec, spec],
+        ),
+        compiler_params=pltpu.CompilerParams(dimension_semantics=("arbitrary",)),
+        name="first_norm",
+    )(head, own, other, gain)
+
+
+def gradient_kernel(back, normed, grad, total):
+    step = pl.program_id(0)
+
+    @pl.when(step == 0)
+    def _():
+        total[...] = dot(back[...], normed[...], NN)
+
+    @pl.when(step > 0)
+    def _():
+        total[...] += dot(back[...], normed[...], NN)
+
+    @pl.when(step == pl.num_programs(0) - 1)
+    def _():
+        grad[...] = total[...].astype(bf16)
+
+
+def joined_gradient(back, normed):
+    lines, count = back.shape
+    width = normed.shape[1]
+    tile = 2 * FEED_ROWS
+    return pl.pallas_call(
+        gradient_kernel,
+        grid=(count // tile,),
+        in_specs=[
+            pl.BlockSpec((lines, tile), lambda i: (0, i)),
+            pl.BlockSpec((tile, width), lambda i: (i, 0)),
+        ],
+        out_specs=pl.BlockSpec((lines, width), lambda i: (0, 0)),
+        out_shape=jax.ShapeDtypeStruct((lines, width), bf16),
+        scratch_shapes=[pltpu.VMEM((lines, width), f32)],
+        compiler_params=pltpu.CompilerParams(
+            dimension_semantics=("arbitrary",), vmem_limit_bytes=32 << 20
+        ),
+        name="joined_gradient",
+    )(back, normed)
+
+
+def pull_kernel(head, back, weight, out):
+    out[...] = dot(back[...].T, weight[...], NN).astype(bf16)
+
+
+def pull_other(head, back, weight):
+    lines, count = back.shape
+    width = weight.shape[1]
+    tiles = count // 2 // FEED_ROWS
+    return pl.pallas_call(
+        pull_kernel,
+        out_shape=jax.ShapeDtypeStruct((count // 2, width), bf16),
+        grid_spec=pltpu.PrefetchScalarGridSpec(
+            num_scalar_prefetch=1,
+            grid=(tiles,),
+            in_specs=[
+                pl.BlockSpec((lines, FEED_ROWS), lambda i, head: (0, (1 - head[0]) * tiles + i)),
+                pl.BlockSpec((lines, width), lambda i, head: (0, 0)),
+            ],
+            out_specs=pl.BlockSpec((FEED_ROWS, width), lambda i, head: (i, 0)),
+        ),
+        compiler_params=pltpu.CompilerParams(
+            dimension_semantics=("arbitrary",), vmem_limit_bytes=24 << 20
+        ),
+        name="pull_other",
+    )(head, back, weight)
+
+
+def input_kernel(head, back, weight, other, rows, middle_grad, gain, input_grad, gain_grad):
+    @pl.when(pl.program_id(0) == 0)
+    def _():
+        gain_grad[...] = jnp.zeros(gain_grad.shape, f32)
+
+    pulled = dot(back[...].T, weight[...], NN) + other[...].astype(f32)
+    unused, normal, inverse = layer_norm(rows[...].astype(f32), gain[...])
+    input_grad[...] = middle_grad[...] + norm_back(pulled, gain[...], normal, inverse)
+    gain_grad[...] += jnp.sum(pulled * normal, axis=0, keepdims=True)
+
+
+def input_backward(head, back, weight, other, rows, middle_grad, gain):
+    lines, count = back.shape
+    width = weight.shape[1]
+    tiles = count // 2 // FEED_ROWS
+
+    def down():
+        return pl.BlockSpec((FEED_ROWS, width), lambda i, head: (i, 0))
+
+    return pl.pallas_call(
+        input_kernel,
+        out_shape=(
+            jax.ShapeDtypeStruct((count // 2, width), f32),
+            jax.ShapeDtypeStruct((1, width), f32),
+        ),
+        grid_spec=pltpu.PrefetchScalarGridSpec(
+            num_scalar_prefetch=1,
+            grid=(tiles,),
+            in_specs=[
+                pl.BlockSpec((lines, FEED_ROWS), lambda i, head: (0, head[0] * tiles + i)),
+                pl.BlockSpec((lines, width), lambda i, head: (0, 0)),
+                down(),
+                down(),
+                pl.BlockSpec((FEED_ROWS, width), lambda i, head: (head[0] * tiles + i, 0)),
+                pl.BlockSpec((1, width), lambda i, head: (0, 0)),
+            ],
+            out_specs=[down(), pl.BlockSpec((1, width), lambda i, head: (0, 0))],
+        ),
+        compiler_params=pltpu.CompilerParams(
+            dimension_semantics=("arbitrary",), vmem_limit_bytes=24 << 20
+        ),
+        name="input_backward",
+    )(head, back, weight, other, rows, middle_grad, gain)
+
+
 def feed_kernel(
-    rows, attended, attended_other, upstream, gain, mixer, mixer_other, expand, shrink,
-    middle, hidden, second_part, shrink_grad, expand_grad, shrink_sum, expand_sum
+    rows, attended, attended_other, upstream, gain, both, mixer_other, expand_left, expand_right,
+    middle, hidden, second_part, shrink_grad, expand_grad, shrink_sum, expand_sum, expand, shrink
 ):
     step = pl.program_id(0)
-    units = shrink.shape[0]
+    mixed, units = attended.shape[0], shrink.shape[0]
     chunk = units // FEED_CHUNKS
 
     @pl.when(step == 0)
     def _():
+        expand[:, : expand_left.shape[1]] = expand_left[...]
+        expand[:, expand_left.shape[1] :] = expand_right[...]
+        shrink[...] = turn(both[:, mixed:])
         shrink_sum[...] = jnp.zeros(shrink_sum.shape, f32)
         expand_sum[...] = jnp.zeros(expand_sum.shape, f32)
 
-    total = rows[...].astype(f32) + dot(attended[...].T, mixer[...], NT)
+    total = rows[...].astype(f32) + dot(attended[...].T, both[:, :mixed], NT)
     total = total + dot(attended_other[...].T, mixer_other[...], NT)
     middle[...] = total
     normed = layer_norm(total, gain[...])[0].astype(bf16)
@@ -429,9 +590,9 @@
         expand_grad[...] = expand_sum[...].astype(bf16)
 
 
-def feed_forward(rows, attended, attended_other, upstream, gain, mixer, mixer_other, expand, shrink):
+def feed_forward(rows, attended, attended_other, upstream, gain, both, mixer_other, expand):
     count, width = rows.shape
-    mixed, units = attended.shape[0], shrink.shape[0]
+    mixed, units = attended.shape[0], expand[0].shape[0] // 2
 
     def full(*shape):
         return pl.BlockSpec(shape, lambda i: (0, 0))
@@ -447,7 +608,7 @@
         grid=(count // FEED_ROWS,),
         in_specs=[
             down(width), along(mixed), along(mixed), down(width), full(1, width),
-            full(width, mixed), full(width, mixed), full(2 * units, width), full(units, width),
+            full(*both.shape), full(width, mixed), full(*expand[0].shape), full(*expand[1].shape),
         ],
         out_specs=[
             down(width), along(units), down(width), full(units, width), full(2 * units, width),
@@ -459,23 +620,28 @@
             jax.ShapeDtypeStruct((units, width), bf16),
             jax.ShapeDtypeStruct((2 * units, width), bf16),
         ),
-        scratch_shapes=[pltpu.VMEM((units, width), f32), pltpu.VMEM((2 * units, width), f32)],
+        scratch_shapes=[
+            pltpu.VMEM((units, width), f32),
+            pltpu.VMEM((2 * units, width), f32),
+            pltpu.VMEM((2 * units, width), bf16),
+            pltpu.VMEM((units, width), bf16),
+        ],
         compiler_params=pltpu.CompilerParams(
             dimension_semantics=("arbitrary",), vmem_limit_bytes=48 << 20
         ),
         name="feed_forward",
-    )(rows, attended, attended_other, upstream, gain, mixer, mixer_other, expand, shrink)
+    )(rows, attended, attended_other, upstream, gain, both, mixer_other, *expand)
 
 
 def norm_kernel(
-    middle, own, other, upstream, gain, mixer, attended,
-    middle_grad, attended_grad, mixer_grad, gain_grad, mixer_turned, mixer_sum
+    middle, own, other, upstream, gain, both, attended, shrink_grad,
+    middle_grad, attended_grad, both_grad, gain_grad, mixer_turned, mixer_sum
 ):
     step = pl.program_id(0)
 
     @pl.when(step == 0)
     def _():
-        mixer_turned[...] = mixer[...].T
+        mixer_turned[...] = both[:, : attended.shape[0]].T
         mixer_sum[...] = jnp.zeros(mixer_sum.shape, f32)
         gain_grad[...] = jnp.zeros(gain_grad.shape, f32)
 
@@ -490,10 +656,12 @@
 
     @pl.when(step == pl.num_programs(0) - 1)
     def _():
-        mixer_grad[...] = mixer_sum[...].T.astype(bf16)
-
-
-def norm_backward(middle, own, other, upstream, gain, mixer, attended):
+        mixed = attended.shape[0]
+        both_grad[:, :mixed] = mixer_sum[...].T.astype(bf16)
+        both_grad[:, mixed:] = turn_back(shrink_grad[...])
+
+
+def norm_backward(middle, own, other, upstream, gain, both, attended, shrink_grad):
     count, width = middle.shape
     mixed = attended.shape[0]
 
@@ -511,13 +679,13 @@
         grid=(count // FEED_ROWS,),
         in_specs=[
             down(width), down(width), down(width), down(width), full(1, width),
-            full(width, mixed), along(mixed),
+            full(*both.shape), along(mixed), full(*shrink_grad.shape),
         ],
-        out_specs=[down(width), along(mixed), full(width, mixed), full(1, width)],
+        out_specs=[down(width), along(mixed), full(*both.shape), full(1, width)],
         out_shape=(
             jax.ShapeDtypeStruct((count, width), f32),
             jax.ShapeDtypeStruct((mixed, count), bf16),
-            jax.ShapeDtypeStruct((width, mixed), bf16),
+            jax.ShapeDtypeStruct(both.shape, bf16),
             jax.ShapeDtypeStruct((1, width), f32),
         ),
         scratch_shapes=[pltpu.VMEM((mixed, width), bf16), pltpu.VMEM((mixed, width), f32)],
@@ -525,7 +693,7 @@
             dimension_semantics=("arbitrary",), vmem_limit_bytes=40 << 20
         ),
         name="norm_backward",
-    )(middle, own, other, upstream, gain, mixer, attended)
+    )(middle, own, other, upstream, gain, both, attended, shrink_grad)
 
 
 def swap(value, axis, bit):
@@ -615,21 +783,7 @@
     return value
 
 
-def halves(own, other, head):
-    first = jnp.where(head == 0, own, other)
-    second = jnp.where(head == 0, other, own)
-    return jnp.concatenate([first, second], axis=0)
-
-
-def schulz_kernel(*refs, count, offset, scale):
-    parts = refs[:count]
-    own, weight, updated, gram, low, change = refs[count:]
-    columns = gram.shape[0]
-    lines = 256 if columns % 256 == 0 else columns
-    if offset is None:
-        held = [part[...] for part in parts]
-    else:
-        held = [parts[0][:, offset : offset + columns]]
+def schulz_start(held, own, gram, low):
     down = 0
     for left in held:
         along = 0
@@ -637,14 +791,18 @@
             gram[down : down + left.shape[1], along : along + right.shape[1]] = dot(left, right, TN)
             along += right.shape[1]
         down += left.shape[1]
-    shape = (columns, columns)
+    shape = gram.shape
     diagonal = lax.broadcasted_iota(jnp.int32, shape, 0) == lax.broadcasted_iota(jnp.int32, shape, 1)
     trace = jnp.sum(jnp.where(diagonal, gram[...], 0.0), axis=0, keepdims=True)
     norm_value = jnp.sqrt(jnp.sum(trace, axis=1, keepdims=True)) + 1e-07
-    rows = own[...] / norm_value
-    shrunk = 1.0 / (norm_value * norm_value)
-    gram[...] = gram[...] * shrunk
+    gram[...] = gram[...] * (1.0 / (norm_value * norm_value))
     low[...] = gram[...].astype(bf16)
+    return own[...] / norm_value
+
+
+def schulz_steps(rows, gram, low, change, first, stop):
+    columns = gram.shape[0]
+    lines = 256 if columns % 256 == 0 else columns
 
     def per_block(body):
         def run(index, carry):
@@ -663,29 +821,89 @@
         gram[block, :] = twice
         low[block, :] = twice.astype(bf16)
 
-    for iteration in range(NS_ITERS):
+    for iteration in range(first, stop):
         per_block(form_change)
         rows = ns_first * rows + dot(rows.astype(bf16), change[...], NN)
         if iteration + 1 < NS_ITERS:
             per_block(next_gram)
-    updated[...] = weight[...] - scale * rows
+    return rows
+
+
+def whole_kernel(*refs, count, offset, scale):
+    parts = refs[:count]
+    own, weight, updated, gram, low, change = refs[count:]
+    if offset is None:
+        held = [part[...] for part in parts]
+    else:
+        held = [parts[0][:, offset : offset + gram.shape[0]]]
+    rows = schulz_start(held, own, gram, low)
+    updated[...] = weight[...] - scale * schulz_steps(rows, gram, low, change, 0, NS_ITERS)
+
+
+def early_kernel(*refs, count):
+    own, rows, gram_out, low_out, gram, low, change = refs[count:]
+    start = schulz_start([part[...] for part in refs[:count]], own, gram, low)
+    rows[...] = start
+    gram_out[...] = gram[...]
+    low_out[...] = low[...]
+
+
+def late_kernel(rows, gram_in, low_in, weight, updated, gram, low, change, *, scale):
+    gram[...] = gram_in[...]
+    low[...] = low_in[...]
+    done = schulz_steps(rows[...], gram, low, change, 0, NS_ITERS)
+    updated[...] = weight[...] - scale * done
+
+
+def square_scratch(columns):
+    return [
+        pltpu.VMEM((columns, columns), f32),
+        pltpu.VMEM((columns, columns), bf16),
+        pltpu.VMEM((columns, columns), bf16),
+    ]
+
+
+def shape_scale(rows, columns):
+    return muon_rate * math.sqrt(rows / columns)
 
 
 def schulz(parts, offset, own, weight, name):
     columns = own.shape[1]
-    shape_scale = muon_rate * math.sqrt(parts[0].shape[0] / columns)
-    kernel = functools.partial(schulz_kernel, count=len(parts), offset=offset, scale=shape_scale)
     return pl.pallas_call(
-        kernel,
+        functools.partial(
+            whole_kernel, count=len(parts), offset=offset, scale=shape_scale(parts[0].shape[0], columns)
+        ),
         out_shape=jax.ShapeDtypeStruct(own.shape, f32),
-        scratch_shapes=[
-            pltpu.VMEM((columns, columns), f32),
-            pltpu.VMEM((columns, columns), bf16),
-            pltpu.VMEM((columns, columns), bf16),
-        ],
+        scratch_shapes=square_scratch(columns),
         compiler_params=pltpu.CompilerParams(vmem_limit_bytes=40 << 20),
         name=name,
     )(*parts, own, weight)
+
+
+def schulz_early(parts, own):
+    columns = own.shape[1]
+    return pl.pallas_call(
+        functools.partial(early_kernel, count=len(parts)),
+        out_shape=(
+            jax.ShapeDtypeStruct(own.shape, f32),
+            jax.ShapeDtypeStruct((columns, columns), f32),
+            jax.ShapeDtypeStruct((columns, columns), bf16),
+        ),
+        scratch_shapes=square_scratch(columns),
+        compiler_params=pltpu.CompilerParams(vmem_limit_bytes=40 << 20),
+        name="schulz_early",
+    )(*parts, own)
+
+
+def schulz_late(state, weight, rows):
+    columns = weight.shape[1]
+    return pl.pallas_call(
+        functools.partial(late_kernel, scale=shape_scale(rows, columns)),
+        out_shape=jax.ShapeDtypeStruct(weight.shape, f32),
+        scratch_shapes=square_scratch(columns),
+        compiler_params=pltpu.CompilerParams(vmem_limit_bytes=40 << 20),
+        name="schulz_late",
+    )(*state, weight)
 
 
 def shards(
@@ -718,9 +936,8 @@
     ]
     key_rows, query_rows, cosine, sine = doc_tables(lengths[0], row_count)
     low, high = key_bounds(lengths[0], row_count)
-    rows_low = halves(tokens, swap(tokens, "head", 1), head)
-    first_normed, first_normal, first_inverse = layer_norm(rows_low.astype(f32), norm_gains[0])
-    first_low = first_normed.astype(bf16)
+    head_place = head[None]
+    rows_low, first_low = first_norm(head_place, tokens, swap(tokens, "head", 1), norm_gains[0:1])
 
     joined_parts, others = tie(joined_parts, others)
     joined_parts = quarter(ordered_step, joined_parts, 1)
@@ -743,31 +960,28 @@
     attended, logsum = attention_forward(low, high, queries, keys, values, key_rows, query_rows)
     others, attended, logsum = tie(moved, attended, logsum)
     attended_other = swap(attended, "head", 1)
-    expand_low = jnp.concatenate([gather_rows(part) for part in others[:2]], axis=1)
     both_low = gather_rows(others[2])
-    mixer_low, shrink_turned = both_low[:, :mixer_width], both_low[:, mixer_width:].T
-    mixer_other = swap(mixer_low, "head", 1)
+    mixer_other = swap(both_low[:, :mixer_width], "head", 1)
 
     second_gain = norm_gains[1:2]
     middle, hidden, second_part, shrink_grad, expand_grad = feed_forward(
         rows_low, attended, attended_other, cotangent, second_gain,
-        mixer_low, mixer_other, expand_low, shrink_turned,
+        both_low, mixer_other, [gather_rows(part) for part in others[:2]],
     )
     second_other = swap(second_part, "head", 1)
 
-    sums, second_other = tie([reduce_start(part) for part in halves_of(expand_grad)], second_other)
-    moved = quarter(reduce_step, sums, 0)
-    middle_grad, attended_grad, mixer_grad, second_gain_grad = norm_backward(
-        middle, second_part, second_other, cotangent, second_gain, mixer_low, attended
-    )
-    second_gain_grad = 0.5 * second_gain_grad[0]
-    both_sum = [reduce_start(jnp.concatenate([mixer_grad, shrink_grad.T], axis=1))]
-
-    sums, attended_grad, shrink_now = tie(moved, attended_grad, shrink_turned)
+    moved = quarter(reduce_step, [reduce_start(part) for part in halves_of(expand_grad)], 0)
+    middle_grad, attended_grad, both_grad, second_gain_grad = norm_backward(
+        middle, second_part, second_other, cotangent, second_gain, both_low, attended, shrink_grad
+    )
+    both_sum = [reduce_start(both_grad)]
+
+    sums, attended_grad, both_now = tie(moved, attended_grad, both_low)
     moved = quarter(reduce_step, sums, 1)
 
     def fed(columns):
-        return dot(lax.dynamic_slice_in_dim(hidden, columns, local_rows, 1), shrink_now, TN)
+        units = lax.dynamic_slice_in_dim(hidden, columns, local_rows, 1)
+        return dot(units, both_now[:, mixer_width:], TT)
 
     fed_other = fed((1 - head) * local_rows).astype(bf16)
     fed_own = fed(head * local_rows)
@@ -783,11 +997,7 @@
     sums, both_sum, joined_back = tie(moved, both_moved, joined_back)
     moved = quarter(reduce_step, sums, 3)
     both_moved = quarter(reduce_step, both_sum, 1, 2)
-    joined_grad = dot(joined_back, first_low, NN).astype(bf16)
-
-    def first_part(start, weight):
-        columns = lax.dynamic_slice_in_dim(joined_back, start, local_rows, 1)
-        return dot(columns, weight, TN)
+    joined_grad = joined_gradient(joined_back, first_low)
 
     sums, both_sum, joined_grad, joined_now = tie(moved, both_moved, joined_grad, joined_low)
     expand_next = 0.5 * expand_momentum[0] + jnp.concatenate(sums, axis=1)
@@ -795,71 +1005,65 @@
     sums = quarter(reduce_step, [reduce_start(part) for part in thirds(joined_grad)], 0)
     moved = quarter(gather_step, gathers, 0)
     both_moved = quarter(reduce_step, both_sum, 2, 2)
-    first_other = swap(
-        first_part((1 - head) * local_rows, joined_now).astype(bf16), "head", 1
-    )
-    first_mine = first_part(head * local_rows, joined_now)
-
-    sums, gathers, both_sum, first_other, first_mine = tie(
-        sums, moved, both_moved, first_other, first_mine
-    )
+    first_other = pull_other(head_place, joined_back, joined_now)
+
+    sums, gathers, both_sum, first_other, fed_own = tie(sums, moved, both_moved, first_other, fed_own)
+    first_other = swap(first_other, "head", 1)
     moved = quarter(reduce_step, sums, 1)
     gathers_moved = quarter(gather_step, gathers, 1)
     both_moved = quarter(reduce_step, both_sum, 3, 2)
-    first_back = first_mine + first_other.astype(f32)
-    own_normal = own_half(first_normal)
-    first_gain_grad = jnp.sum(first_back * own_normal, axis=0)
-
-    sums, gathers, both_sum, first_gain_grad, first_gain = tie(
-        moved, gathers_moved, both_moved, first_gain_grad, norm_gains[0]
+    layer_output = (own_half(middle) + fed_own + fed_other.astype(f32)).astype(bf16)
+
+    sums, gathers, both_sum, first_other, layer_output = tie(
+        moved, gathers_moved, both_moved, first_other, layer_output
     )
     mixer_next = 0.5 * mixer_momentum[0] + both_sum[0][:, :mixer_width]
     shrink_next = 0.5 * shrink_momentum[0] + both_sum[0][:, mixer_width:]
     both_gather = [gather_start(jnp.concatenate([mixer_next, shrink_next], axis=1).astype(bf16))]
-    gain_totals = jnp.stack([first_gain_grad, second_gain_grad])
     moved = quarter(reduce_step, sums, 2)
     gathers_moved = quarter(gather_step, gathers, 2)
     both_moved = quarter(gather_step, both_gather, 0, 2)
-    gain_moved = total_step(gain_totals, 0)
-    input_gradient = own_half(middle_grad) + norm_back(
-        first_back, first_gain, own_normal, own_half(first_inverse)
-    )
-
-    sums, gathers, both_gather, gain_totals, input_gradient, fed_own = tie(
-        moved, gathers_moved, both_moved, gain_moved, input_gradient, fed_own
-    )
+    input_gradient, first_gain_grad = input_backward(
+        head_place, joined_back, joined_now, first_other, tokens, middle_grad, norm_gains[0:1]
+    )
+
+    sums, gathers, both_gather, first_gain_grad = tie(
+        moved, gathers_moved, both_moved, first_gain_grad
+    )
+    gain_totals = jnp.concatenate([first_gain_grad, 0.5 * second_gain_grad], axis=0)
     moved = quarter(reduce_step, sums, 3)
     gathers_moved = quarter(gather_step, gathers, 3)
     both_moved = quarter(gather_step, both_gather, 1, 2)
-    gain_moved = total_step(gain_totals, 1)
-    layer_output = (own_half(middle) + fed_own + fed_other.astype(f32)).astype(bf16)
-
-    sums, gathers, both_gather, gain_totals, layer_output = tie(
-        moved, gathers_moved, both_moved, gain_moved, layer_output
-    )
+    gain_moved = total_step(gain_totals, 0)
+
+    sums, gathers, both_gather, gain_totals = tie(moved, gathers_moved, both_moved, gain_moved)
     joined_next = 0.5 * joined_momentum[0] + jnp.concatenate(sums, axis=1)
     joined_gather = [gather_start(part) for part in thirds(joined_next.astype(bf16))]
     moved = quarter(gather_step, joined_gather, 0)
     both_moved = quarter(gather_step, both_gather, 2, 2)
+    gain_moved = total_step(gain_totals, 1)
+    expand_state = schulz_early([gather_rows(part) for part in gathers], expand_next)
+    joined_gather, both_gather, gain_totals, expand_state = tie(
+        moved, both_moved, gain_moved, expand_state
+    )
+    moved = quarter(gather_step, joined_gather, 1)
+    both_moved = quarter(gather_step, both_gather, 3, 2)
     gain_moved = total_step(gain_totals, 2)
-    updated_expand = schulz(
-        [gather_rows(part) for part in gathers], None, expand_next, expand_weight[0], "schulz_expand"
-    )
+    updated_expand = schulz_late(expand_state, expand_weight[0], expand_grad.shape[0])
     joined_gather, both_gather, gain_totals, updated_expand = tie(
         moved, both_moved, gain_moved, updated_expand
     )
-    moved = quarter(gather_step, joined_gather, 1)
-    both_moved = quarter(gather_step, both_gather, 3, 2)
-    gain_moved = total_step(gain_totals, 3)
-    joined_gather, both_gather, gain_totals = tie(moved, both_moved, gain_moved)
     both_full = [gather_rows(both_gather[0])]
     moved = quarter(gather_step, joined_gather, 2)
-    gain_totals = total_step(gain_totals, 4)
+    gain_moved = total_step(gain_totals, 3)
     updated_shrink = schulz(
         both_full, mixer_width, shrink_next, shrink_weight[0], "schulz_shrink"
     )
-    joined_gather, both_full, updated_shrink = tie(moved, both_full, updated_shrink)
+    joined_gather, both_full, gain_totals, updated_shrink = tie(
+        moved, both_full, gain_moved, updated_shrink
+    )
     moved = quarter(gather_step, joined_gather, 3)
+    gain_totals = total_step(gain_totals, 4)
     updated_mixer = schulz(both_full, 0, mixer_next, mixer_weight[0], "schulz_mixer")
     joined_gather, updated_mixer = tie(moved, updated_mixer)
     updated_joined = schulz(

time: 410 us -> 414 us (level)
  Pallas kernels: 149 us -> 170 us
  other arithmetic: 40.8 us -> 27.1 us
  matrix products: 19 us -> 7.95 us
  starting transfers between devices: 99.3 us -> 105 us
  local copies, waits for them, and re-layouts: 12.7 us -> 17.2 us
    pallas_call x4 -> x9, Pallas kernels: 39.6 us -> 61.6 us  [the longest x3 25.2 us: schulz(): pl.pallas_call(functools.partial(whole_kernel, count=len(parts), offset=o...]
    dot_general x6 -> x3, matrix products: 19 us -> 7.95 us  [dot(): return lax.dot_general(left, right, dims, preferred_element_type=f32)]
    unnamed x102 -> x92, local copies, waits for them, and re-layouts: 3.27 us -> 9.65 us
    ppermute x83, starting transfers between devices: 99.3 us -> 105 us  [swap(): return lax.ppermute(value, axis, [(i, i ^ bit) for i in range(count)])]
    reduce_sum x4 -> x0, other arithmetic: 5.07 us -> none  [the longest x1 3.16 us: layer_norm(): jnp.mean(centred * centred, axis=-1, keepdims=True) + norm_epsilon]
    concatenate x3 -> x1, other arithmetic: 4.74 us -> 0.01 us  [shards(): jnp.concatenate([first_gain_grad, 0.5 * second_gain_grad], axis=0)]
    mul x2 -> x1, other arithmetic: 4.35 us -> 0.01 us  [shards(): 0.5 * second_gain_grad]
  transfers between devices with their start and end apart: 83 -> 83, of which waited for: 30 -> 27; matrix products, arithmetic and copies ran while one was open for 14% -> 10% of each run, Pallas kernels for 25% -> 24%
where the time goes in v3:
time: 414 us; the launch traced here: 410 us
  Pallas kernels  170 us (41%)
  starting transfers between devices  105 us (25%)
  waiting for transfers between devices  79.7 us (19%)
  other arithmetic  27.1 us (7%)
  local copies, waits for them, and re-layouts  17.2 us (4%)
  matrix products  7.95 us (2%)
    ppermute x83, starting transfers between devices, swap(): return lax.ppermute(value, axis, [(i, i ^ bit) for i in range(count)])  105 us
    ppermute x83, waiting for transfers between devices, swap(): return lax.ppermute(value, axis, [(i, i ^ bit) for i in range(count)])  79.7 us
    pallas_call x1, Pallas kernels, attention_backward(): pl.pallas_call(backward_kernel, out_shape=jax.ShapeDtypeStruct((3 * width...  39.1 us
    pallas_call x1, Pallas kernels, feed_forward(): pl.pallas_call(feed_kernel, grid=(count // FEED_ROWS,), in_specs=[down(wi...  35.7 us
    pallas_call x3, Pallas kernels, schulz(): pl.pallas_call(functools.partial(whole_kernel, count=len(parts), offset=o...  25.2 us
    pallas_call x1, Pallas kernels, attention_forward(): pl.pallas_call(forward_kernel, out_shape=(jax.ShapeDtypeStruct((width, ro...  20.7 us
    pallas_call x1, Pallas kernels, norm_backward(): pl.pallas_call(norm_kernel, grid=(count // FEED_ROWS,), in_specs=[down(wi...  13.2 us
    pallas_call x1, Pallas kernels, schulz_late(): pl.pallas_call(functools.partial(late_kernel, scale=shape_scale(rows, col...  11.9 us
  transfers between devices with their start and end apart: 83, of which 27 were waited for; matrix products, arithmetic and copies ran while one was open for 10% of the time, Pallas kernels for 24%

profile of v3, /device:TPU:0, one launch (start us, length us, event | category | flops | bytes accessed | tf_op | source)
XLA Modules:
  0.0 410.0 jit_solution(1281333306474878491)
XLA Ops:
  2.2 3.7 collective-permute-start.3
  5.9 2.8 collective-permute-start.1
  21.9 2.3 collective-permute-start.8
  24.3 2.7 collective-permute-done.8
  26.9 2.3 collective-permute-start.9
  29.5 4.1 %collective-permute-done.9 = bf16[1,1,1,1,48,960]{5,4,3,2,1,0:T(8,128)(2,1)S(1)} collective-permute-done((bf16[1,1,1,1,48,960]{5,4,3,2,1,0:T(8,128)(2,1)S(1)}, bf16[1,1,1,1,48,960]{5,4,3,2,1,0:T(8,128)(2,1)S(1)}, u32[]{:S(2)}, u32[]{:S(2)}) %collective-permute-start.9) | collective-permute-done | bytes 92192 | tf_op jit(solution)/shard_map/ppermute | solution.py:701
  34.1 2.4 collective-permute-start.10
  39.4 3.8 collective-permute-done.14
  46.6 2.2 collective-permute-done.15
  50.1 7.8 %first_norm.1 = (bf16[2048,768]{1,0:T(8,128)(2,1)}, bf16[2048,768]{1,0:T(8,128)(2,1)}) custom-call(s32[1]{0:T(128)} %bitcast.head, bf16[1024,768]{1,0:T(8,128)(2,1)} %rows.1, bf16[1024,768]{1,0:T(8,128)(2,1)} %copy-done.30, f32[1,768]{1,0:T(1,128)} %get-tuple-element.346.gain), custom_call_target="tpu_custom_call" | custom-call | tf_op jit(solution)/shard_map/first_norm/pallas_call | solution.py:402
  65.4 3.9 collective-permute-done.21
  74.2 3.9 fusion.11
  84.6 20.7 %attention_forward.1 = (bf16[384,2048]{1,0:T(8,128)(2,1)S(1)}, f32[6,2048]{1,0:T(8,128)S(1)}) custom-call(s32[8]{0:T(128)S(1)} %get-tuple-element.181.low, s32[8]{0:T(128)S(1)} %get-tuple-element.347.high, bf16[384,2048]{1,0:T(8,128)(2,1)S(1)} %bitcast.127, bf16[384,2048]{1,0:T(8,128)(2,1)S(1)} %bitcast.125, bf16[384,2048]{1,0:T(8,128)(2,1)S(1)} %slice.170.values, ...), custom_call_target="tpu_custom_call" | custom-call | tf_op jit(solution)/shard_map/attention_forward/pallas_call | solution.py:207
  107.1 3.6 collective-permute-done.26.mixer_other
  111.9 35.7 %feed_forward.1 = (f32[2048,768]{1,0:T(8,128)}, bf16[576,2048]{1,0:T(8,128)(2,1)}, bf16[2048,768]{1,0:T(8,128)(2,1)}, bf16[576,768]{1,0:T(8,128)(2,1)S(1)}, bf16[1152,768]{1,0:T(8,128)(2,1)}) custom-call(bf16[2048,768]{1,0:T(8,128)(2,1)} %get-tuple-element.134.rows, bf16[384,2048]{1,0:T(8,128)(2,1)S(1)} %get-tuple-element.164.attended.outs, ...), custom_call_target="tpu_custom_call" | custom-call | tf_op jit(solution)/shard_map/feed_forward/pallas_call | solution.py:606
  148.7 2.5 fusion.16
  154.1 3.4 collective-permute-start.28
  159.2 6.5 %collective-permute-done.27 = bf16[2,2,2,1,72,384]{5,4,3,2,1,0:T(8,128)(2,1)} collective-permute-done((bf16[2,2,2,1,72,384]{5,4,3,2,1,0:T(8,128)(2,1)}, bf16[2,2,2,1,72,384]{5,4,3,2,1,0:T(8,128)(2,1)}, u32[]{:S(2)}, u32[]{:S(2)}) %collective-permute-start.27) | collective-permute-done | bytes 442400 | tf_op jit(solution)/shard_map/ppermute | solution.py:701
  170.3 13.2 %norm_backward.1 = (f32[2048,768]{1,0:T(8,128)}, bf16[384,2048]{1,0:T(8,128)(2,1)S(1)}, bf16[768,960]{1,0:T(8,128)(2,1)S(1)}, f32[1,768]{1,0:T(1,128)S(1)}) custom-call(f32[2048,768]{1,0:T(8,128)} %get-tuple-element.169.middle, bf16[2048,768]{1,0:T(8,128)(2,1)S(1)} %copy-done.11, bf16[2048,768]{1,0:T(8,128)(2,1)S(1)} %collective-permute-done.29.other, ...), custom_call_target="tpu_custom_call" | custom-call | tf_op jit(solution)/shard_map/norm_backward/pallas_call | solution.py:677
  185.3 3.1 collective-permute-start.31
  189.9 2.6 convolution_convert_fusion
  196.8 39.1 %attention_backward.1.back = bf16[1152,2048]{1,0:T(8,128)(2,1)} custom-call(s32[8]{0:T(128)S(1)} %get-tuple-element.181.low, s32[8]{0:T(128)S(1)} %get-tuple-element.347.high, bf16[384,2048]{1,0:T(8,128)(2,1)} %bitcast.128, bf16[384,2048]{1,0:T(8,128)(2,1)} %bitcast.126, bf16[384,2048]{1,0:T(8,128)(2,1)} %copy-done.3, bf16[384,2048]{1,0:T(8,128)(2,1)} %copy-done.14, ...), custom_call_target="tpu_custom_call" | custom-call | tf_op jit(solution)/shard_map/attention_backward/pallas_call | solution.py:324
  236.4 2.9 collective-permute-start.36
  239.4 2.3 copy-done
  241.8 5.0 %joined_gradient.1 = bf16[1152,768]{1,0:T(8,128)(2,1)S(1)} custom-call(bf16[1152,2048]{1,0:T(8,128)(2,1)S(1)} %copy-done, bf16[2048,768]{1,0:T(8,128)(2,1)S(1)} %copy-done.10), custom_call_target="tpu_custom_call" | custom-call | tf_op jit(solution)/shard_map/joined_gradient/pallas_call | solution.py:446
  246.8 3.6 collective-permute-done.37
  251.1 4.5 %collective-permute-start.39 = (bf16[2,2,1,2,72,256]{5,4,3,2,1,0:T(8,128)(2,1)S(1)}, bf16[2,2,1,2,72,256]{5,4,3,2,1,0:T(8,128)(2,1)S(1)}, u32[]{:S(2)}, u32[]{:S(2)}) collective-permute-start(bf16[2,2,1,2,72,256]{5,4,3,2,1,0:T(8,128)(2,1)S(1)} %constant_dynamic-slice_fusion.11), channel_id=1, source_target_pairs={{0,4},{2,6},{4,0},{6,2},{8,12},{10,14},{12,8},{14,10},{16,20},{18,... | collective-permute-start | bytes 884744 | tf_op jit(solution)/shard_map/ppermute | solution.py:701
  255.7 2.0 collective-permute-start.41
  258.7 3.3 pull_other.1
  262.8 5.6 %collective-permute-start.40 = (bf16[2,1,2,2,72,256]{5,4,3,2,1,0:T(8,128)(2,1)S(1)}, bf16[2,1,2,2,72,256]{5,4,3,2,1,0:T(8,128)(2,1)S(1)}, u32[]{:S(2)}, u32[]{:S(2)}) collective-permute-start(bf16[2,1,2,2,72,256]{5,4,3,2,1,0:T(8,128)(2,1)S(1)} %constant_dynamic-slice_fusion.10), channel_id=1, source_target_pairs={{0,8},{2,10},{4,12},{6,14},{8,0},{10,2},{12,4},{14,6},{16,24},{18,... | collective-permute-start | bytes 884744 | tf_op jit(solution)/shard_map/ppermute | solution.py:701
  268.6 4.6 %collective-permute-done.40 = bf16[2,1,2,2,72,256]{5,4,3,2,1,0:T(8,128)(2,1)S(1)} collective-permute-done((bf16[2,1,2,2,72,256]{5,4,3,2,1,0:T(8,128)(2,1)S(1)}, bf16[2,1,2,2,72,256]{5,4,3,2,1,0:T(8,128)(2,1)S(1)}, u32[]{:S(2)}, u32[]{:S(2)}) %collective-permute-start.40) | collective-permute-done | bytes 294944 | tf_op jit(solution)/shard_map/ppermute | solution.py:701
  276.6 2.3 collective-permute-start.49
  279.0 4.4 %collective-permute-done.49 = bf16[1,1,1,1,48,960]{5,4,3,2,1,0:T(8,128)(2,1)S(1)} collective-permute-done((bf16[1,1,1,1,48,960]{5,4,3,2,1,0:T(8,128)(2,1)S(1)}, bf16[1,1,1,1,48,960]{5,4,3,2,1,0:T(8,128)(2,1)S(1)}, u32[]{:S(2)}, u32[]{:S(2)}) %collective-permute-start.49) | collective-permute-done | bytes 92192 | tf_op jit(solution)/shard_map/ppermute | solution.py:701
  283.4 4.7 %collective-permute-done.47 = bf16[2,1,1,1,72,384]{5,4,3,2,1,0:T(8,128)(2,1)S(1)} collective-permute-done((bf16[2,1,1,1,72,384]{5,4,3,2,1,0:T(8,128)(2,1)S(1)}, bf16[2,1,1,1,72,384]{5,4,3,2,1,0:T(8,128)(2,1)S(1)}, u32[]{:S(2)}, u32[]{:S(2)}) %collective-permute-start.47) | collective-permute-done | bytes 110624 | tf_op jit(solution)/shard_map/ppermute | solution.py:701
  289.3 3.7 collective-permute-done.48
  294.2 4.4 %collective-permute-done.46 = bf16[2,1,2,1,72,256]{5,4,3,2,1,0:T(8,128)(2,1)S(1)} collective-permute-done((bf16[2,1,2,1,72,256]{5,4,3,2,1,0:T(8,128)(2,1)S(1)}, bf16[2,1,2,1,72,256]{5,4,3,2,1,0:T(8,128)(2,1)S(1)}, u32[]{:S(2)}, u32[]{:S(2)}) %collective-permute-start.46) | collective-permute-done | bytes 147488 | tf_op jit(solution)/shard_map/ppermute | solution.py:701
  298.8 2.0 add_convert_fusion
  306.4 5.9 %input_backward.1 = (f32[1024,768]{1,0:T(8,128)}, f32[1,768]{1,0:T(1,128)S(1)}) custom-call(s32[1]{0:T(128)} %bitcast.head, bf16[1152,2048]{1,0:T(8,128)(2,1)S(1)} %bitcast.117, bf16[1152,768]{1,0:T(8,128)(2,1)S(1)} %pad_maximum_fusion.weight, bf16[1024,768]{1,0:T(8,128)(2,1)S(1)} %collective-permute-done.50.other, bf16[1024,768]{1,0:T(8,128)(2,1)S(1)} %copy-done.8, ...), custom_call_target="tpu_custom_call" | custom-call | tf_op jit(solution)/shard_map/input_backward/pallas_call | solution.py:509
  314.4 4.1 %collective-permute-done.57 = bf16[1,1,1,1,48,960]{5,4,3,2,1,0:T(8,128)(2,1)S(1)} collective-permute-done((bf16[1,1,1,1,48,960]{5,4,3,2,1,0:T(8,128)(2,1)S(1)}, bf16[1,1,1,1,48,960]{5,4,3,2,1,0:T(8,128)(2,1)S(1)}, u32[]{:S(2)}, u32[]{:S(2)}) %collective-permute-start.57) | collective-permute-done | bytes 92192 | tf_op jit(solution)/shard_map/ppermute | solution.py:701
  324.4 2.0 collective-permute-start.63
  326.8 13.7 %collective-permute-done.63 = bf16[2,1,1,1,48,960]{5,4,3,2,1,0:T(8,128)(2,1)S(1)} collective-permute-done((bf16[2,1,1,1,48,960]{5,4,3,2,1,0:T(8,128)(2,1)S(1)}, bf16[2,1,1,1,48,960]{5,4,3,2,1,0:T(8,128)(2,1)S(1)}, u32[]{:S(2)}, u32[]{:S(2)}) %collective-permute-start.63) | collective-permute-done | bytes 184352 | tf_op jit(solution)/shard_map/ppermute | solution.py:701
  347.7 2.5 schulz_early.1
  350.2 2.4 collective-permute-done.69
  352.9 2.0 collective-permute-start.70
  358.3 11.9 %schulz_late.1 = f32[72,768]{1,0:T(8,128)} custom-call(f32[72,768]{1,0:T(8,128)S(1)} %get-tuple-element.237.rows, f32[768,768]{1,0:T(8,128)S(1)} %get-tuple-element.238.gram_in, bf16[768,768]{1,0:T(8,128)(2,1)S(1)} %get-tuple-element.239.low_in, f32[72,768]{1,0:T(8,128)S(1)} %bitcast.141), custom_call_target="tpu_custom_call" | custom-call | tf_op jit(solution)/shard_map/schulz_late/pallas_call | solution.py:900
  376.6 7.6 %schulz_shrink.1 = f32[48,576]{1,0:T(8,128)} custom-call(bf16[768,960]{1,0:T(8,128)(2,1)S(1)} %bitcast.123, f32[48,576]{1,0:T(8,128)S(1)} %get-tuple-element.265.refs_1_, f32[48,576]{1,0:T(8,128)S(1)} %bitcast.142), custom_call_target="tpu_custom_call" | custom-call | tf_op jit(solution)/shard_map/schulz_shrink/pallas_call | solution.py:872
  389.5 3.8 schulz_mixer.1
  395.9 13.8 %schulz_joined.1 = f32[72,768]{1,0:T(8,128)} custom-call(bf16[1152,256]{1,0:T(8,128)(2,1)S(1)} %bitcast.135, bf16[1152,256]{1,0:T(8,128)(2,1)S(1)} %bitcast.136, bf16[1152,256]{1,0:T(8,128)(2,1)S(1)} %bitcast.137, f32[72,768]{1,0:T(8,128)S(1)} %get-tuple-element.261.refs_3_, f32[72,768]{1,0:T(8,128)S(1)} %bitcast.140), custom_call_target="tpu_custom_call" | custom-call | tf_op jit(solution)/shard_map/schulz_joined/pallas_call | solution.py:872
  (399 shorter events, 109.9 us)
Async XLA Ops:
  0.6 48.3 %collective-permute-start = (bf16[1024,768]{1,0:T(8,128)(2,1)}, bf16[1024,768]{1,0:T(8,128)(2,1)S(1)}, u32[]{:S(2)}, u32[]{:S(2)}) collective-permute-start(bf16[1024,768]{1,0:T(8,128)(2,1)} %rows.1), channel_id=1, source_target_pairs={{0,1},{1,0},{2,3},{3,2},{4,5},{5,4},{6,7},{7,6},{8,9},{9,8},{10,11... | collective-permute-start | bytes 4718600 | tf_op jit(solution)/shard_map/ppermute | solution.py:701
  2.2 14.2 %collective-permute-start.3 = (bf16[1,1,1,1,72,256]{5,4,3,2,1,0:T(8,128)(2,1)S(1)}, bf16[1,1,1,1,72,256]{5,4,3,2,1,0:T(8,128)(2,1)S(1)}, u32[]{:S(2)}, u32[]{:S(2)}) collective-permute-start(bf16[1,1,1,1,72,256]{5,4,3,2,1,0:T(8,128)(2,1)S(1)} %get-tuple-element.340), channel_id=1, source_target_pairs={{0,16},{2,18},{4,20},{6,22},{8,24},{10,26},{12,28},{14,30},{16,0},... | collective-permute-start | bytes 110600 | tf_op jit(solution)/shard_map/ppermute | solution.py:701
  5.8 10.5 %collective-permute-start.2 = (bf16[1,1,1,1,72,256]{5,4,3,2,1,0:T(8,128)(2,1)S(1)}, bf16[1,1,1,1,72,256]{5,4,3,2,1,0:T(8,128)(2,1)S(1)}, u32[]{:S(2)}, u32[]{:S(2)}) collective-permute-start(bf16[1,1,1,1,72,256]{5,4,3,2,1,0:T(8,128)(2,1)S(1)} %get-tuple-element.341), channel_id=1, source_target_pairs={{0,16},{2,18},{4,20},{6,22},{8,24},{10,26},{12,28},{14,30},{16,0},... | collective-permute-start | bytes 110600 | tf_op jit(solution)/shard_map/ppermute | solution.py:701
  5.9 10.5 %collective-permute-start.1 = (bf16[1,1,1,1,72,256]{5,4,3,2,1,0:T(8,128)(2,1)S(1)}, bf16[1,1,1,1,72,256]{5,4,3,2,1,0:T(8,128)(2,1)S(1)}, u32[]{:S(2)}, u32[]{:S(2)}) collective-permute-start(bf16[1,1,1,1,72,256]{5,4,3,2,1,0:T(8,128)(2,1)S(1)} %get-tuple-element.342), channel_id=1, source_target_pairs={{0,16},{2,18},{4,20},{6,22},{8,24},{10,26},{12,28},{14,30},{16,0},... | collective-permute-start | bytes 110600 | tf_op jit(solution)/shard_map/ppermute | solution.py:701
  16.7 12.6 %collective-permute-start.4 = (bf16[2,1,1,1,72,256]{5,4,3,2,1,0:T(8,128)(2,1)S(1)}, bf16[2,1,1,1,72,256]{5,4,3,2,1,0:T(8,128)(2,1)S(1)}, u32[]{:S(2)}, u32[]{:S(2)}) collective-permute-start(bf16[2,1,1,1,72,256]{5,4,3,2,1,0:T(8,128)(2,1)S(1)} %get-tuple-element.135), channel_id=1, source_target_pairs={{0,8},{2,10},{4,12},{6,14},{8,0},{10,2},{12,4},{14,6},{16,24},{18,... | collective-permute-start | bytes 221192 | tf_op jit(solution)/shard_map/ppermute | solution.py:701
  18.6 10.8 %collective-permute-start.5 = (bf16[2,1,1,1,72,256]{5,4,3,2,1,0:T(8,128)(2,1)S(1)}, bf16[2,1,1,1,72,256]{5,4,3,2,1,0:T(8,128)(2,1)S(1)}, u32[]{:S(2)}, u32[]{:S(2)}) collective-permute-start(bf16[2,1,1,1,72,256]{5,4,3,2,1,0:T(8,128)(2,1)S(1)} %get-tuple-element.136), channel_id=1, source_target_pairs={{0,2},{2,0},{4,6},{6,4},{8,10},{10,8},{12,14},{14,12},{16,18},{18,... | collective-permute-start | bytes 221192 | tf_op jit(solution)/shard_map/ppermute | solution.py:701
  20.1 9.3 %collective-permute-start.6 = (bf16[2,1,1,1,72,256]{5,4,3,2,1,0:T(8,128)(2,1)S(1)}, bf16[2,1,1,1,72,256]{5,4,3,2,1,0:T(8,128)(2,1)S(1)}, u32[]{:S(2)}, u32[]{:S(2)}) collective-permute-start(bf16[2,1,1,1,72,256]{5,4,3,2,1,0:T(8,128)(2,1)S(1)} %pad_maximum_fusion.48), channel_id=1, source_target_pairs={{0,4},{2,6},{4,0},{6,2},{8,12},{10,14},{12,8},{14,10},{16,20},{18,... | collective-permute-start | bytes 221192 | tf_op jit(solution)/shard_map/ppermute | solution.py:701
  34.1 10.2 %collective-permute-start.10 = (bf16[2,2,1,1,72,256]{5,4,3,2,1,0:T(8,128)(2,1)S(1)}, bf16[2,2,1,1,72,256]{5,4,3,2,1,0:T(8,128)(2,1)S(1)}, u32[]{:S(2)}, u32[]{:S(2)}) collective-permute-start(bf16[2,2,1,1,72,256]{5,4,3,2,1,0:T(8,128)(2,1)S(1)} %pad_maximum_fusion.34), channel_id=1, source_target_pairs={{0,4},{2,6},{4,0},{6,2},{8,12},{10,14},{12,8},{14,10},{16,20},{18,... | collective-permute-start | bytes 442376 | tf_op jit(solution)/shard_map/ppermute | solution.py:701
  60.7 19.8 %collective-permute-start.18 = (bf16[2,1,2,1,48,960]{5,4,3,2,1,0:T(8,128)(2,1)S(1)}, bf16[2,1,2,1,48,960]{5,4,3,2,1,0:T(8,128)(2,1)S(1)}, u32[]{:S(2)}, u32[]{:S(2)}) collective-permute-start(bf16[2,1,2,1,48,960]{5,4,3,2,1,0:T(8,128)(2,1)S(1)} %pad_maximum_fusion.20), channel_id=1, source_target_pairs={{0,2},{2,0},{4,6},{6,4},{8,10},{10,8},{12,14},{14,12},{16,18},{18,... | collective-permute-start | bytes 1105928 | tf_op jit(solution)/shard_map/ppermute | solution.py:701
  80.7 24.6 %collective-permute-start.22 = (bf16[2,2,2,1,72,384]{5,4,3,2,1,0:T(8,128)(2,1)S(1)}, bf16[2,2,2,1,72,384]{5,4,3,2,1,0:T(8,128)(2,1)S(1)}, u32[]{:S(2)}, u32[]{:S(2)}) collective-permute-start(bf16[2,2,2,1,72,384]{5,4,3,2,1,0:T(8,128)(2,1)S(1)} %pad_maximum_fusion.16), channel_id=1, source_target_pairs={{0,2},{2,0},{4,6},{6,4},{8,10},{10,8},{12,14},{14,12},{16,18},{18,... | collective-permute-start | bytes 1327112 | tf_op jit(solution)/shard_map/ppermute | solution.py:701
  81.8 24.1 %collective-permute-start.23 = (bf16[2,2,1,2,72,384]{5,4,3,2,1,0:T(8,128)(2,1)S(1)}, bf16[2,2,1,2,72,384]{5,4,3,2,1,0:T(8,128)(2,1)S(1)}, u32[]{:S(2)}, u32[]{:S(2)}) collective-permute-start(bf16[2,2,1,2,72,384]{5,4,3,2,1,0:T(8,128)(2,1)S(1)} %pad_maximum_fusion.17), channel_id=1, source_target_pairs={{0,4},{2,6},{4,0},{6,2},{8,12},{10,14},{12,8},{14,10},{16,20},{18,... | collective-permute-start | bytes 1327112 | tf_op jit(solution)/shard_map/ppermute | solution.py:701
  82.9 23.2 %collective-permute-start.24 = (bf16[2,1,2,2,48,960]{5,4,3,2,1,0:T(8,128)(2,1)S(1)}, bf16[2,1,2,2,48,960]{5,4,3,2,1,0:T(8,128)(2,1)S(1)}, u32[]{:S(2)}, u32[]{:S(2)}) collective-permute-start(bf16[2,1,2,2,48,960]{5,4,3,2,1,0:T(8,128)(2,1)S(1)} %pad_maximum_fusion.8), channel_id=1, source_target_pairs={{0,8},{2,10},{4,12},{6,14},{8,0},{10,2},{12,4},{14,6},{16,24},{18,... | collective-permute-start | bytes 2211848 | tf_op jit(solution)/shard_map/ppermute | solution.py:701
  148.5 20.6 %collective-permute-start.29 = (bf16[2048,768]{1,0:T(8,128)(2,1)}, bf16[2048,768]{1,0:T(8,128)(2,1)S(1)}, u32[]{:S(2)}, u32[]{:S(2)}) collective-permute-start(bf16[2048,768]{1,0:T(8,128)(2,1)} %get-tuple-element.170.own), channel_id=1, source_target_pairs={{0,1},{1,0},{2,3},{3,2},{4,5},{5,4},{6,7},{7,6},{8,9},{9,8},{10,11... | collective-permute-start | bytes 9437192 | tf_op jit(solution)/shard_map/ppermute | solution.py:701
  152.9 12.8 %collective-permute-start.27 = (bf16[2,2,2,1,72,384]{5,4,3,2,1,0:T(8,128)(2,1)}, bf16[2,2,2,1,72,384]{5,4,3,2,1,0:T(8,128)(2,1)}, u32[]{:S(2)}, u32[]{:S(2)}) collective-permute-start(bf16[2,2,2,1,72,384]{5,4,3,2,1,0:T(8,128)(2,1)} %constant_dynamic-slice_fusion.22), channel_id=1, source_target_pairs={{0,2},{2,0},{4,6},{6,4},{8,10},{10,8},{12,14},{14,12},{16,18},{18,... | collective-permute-start | bytes 1327112 | tf_op jit(solution)/shard_map/ppermute | solution.py:701
  154.1 13.8 %collective-permute-start.28 = (bf16[2,2,1,2,72,384]{5,4,3,2,1,0:T(8,128)(2,1)S(1)}, bf16[2,2,1,2,72,384]{5,4,3,2,1,0:T(8,128)(2,1)S(1)}, u32[]{:S(2)}, u32[]{:S(2)}) collective-permute-start(bf16[2,2,1,2,72,384]{5,4,3,2,1,0:T(8,128)(2,1)S(1)} %constant_dynamic-slice_fusion.21), channel_id=1, source_target_pairs={{0,4},{2,6},{4,0},{6,2},{8,12},{10,14},{12,8},{14,10},{16,20},{18,... | collective-permute-start | bytes 1327112 | tf_op jit(solution)/shard_map/ppermute | solution.py:701
  183.5 9.0 %collective-permute-start.30 = (bf16[2,2,1,1,72,384]{5,4,3,2,1,0:T(8,128)(2,1)S(1)}, bf16[2,2,1,1,72,384]{5,4,3,2,1,0:T(8,128)(2,1)S(1)}, u32[]{:S(2)}, u32[]{:S(2)}) collective-permute-start(bf16[2,2,1,1,72,384]{5,4,3,2,1,0:T(8,128)(2,1)S(1)} %constant_dynamic-slice_fusion.20), channel_id=1, source_target_pairs={{0,4},{2,6},{4,0},{6,2},{8,12},{10,14},{12,8},{14,10},{16,20},{18,... | collective-permute-start | bytes 663560 | tf_op jit(solution)/shard_map/ppermute | solution.py:701
  193.4 42.6 %collective-permute-start.34 = (bf16[2,1,2,2,48,960]{5,4,3,2,1,0:T(8,128)(2,1)S(1)}, bf16[2,1,2,2,48,960]{5,4,3,2,1,0:T(8,128)(2,1)S(1)}, u32[]{:S(2)}, u32[]{:S(2)}) collective-permute-start(bf16[2,1,2,2,48,960]{5,4,3,2,1,0:T(8,128)(2,1)S(1)} %constant_dynamic-slice_fusion.16), channel_id=1, source_target_pairs={{0,8},{2,10},{4,12},{6,14},{8,0},{10,2},{12,4},{14,6},{16,24},{18,... | collective-permute-start | bytes 2211848 | tf_op jit(solution)/shard_map/ppermute | solution.py:701
  195.2 40.7 %collective-permute-start.32 = (bf16[2,1,1,1,72,384]{5,4,3,2,1,0:T(8,128)(2,1)S(1)}, bf16[2,1,1,1,72,384]{5,4,3,2,1,0:T(8,128)(2,1)S(1)}, u32[]{:S(2)}, u32[]{:S(2)}) collective-permute-start(bf16[2,1,1,1,72,384]{5,4,3,2,1,0:T(8,128)(2,1)S(1)} %constant_dynamic-slice_fusion.18), channel_id=1, source_target_pairs={{0,8},{2,10},{4,12},{6,14},{8,0},{10,2},{12,4},{14,6},{16,24},{18,... | collective-permute-start | bytes 331784 | tf_op jit(solution)/shard_map/ppermute | solution.py:701
  195.6 40.3 %collective-permute-start.33 = (bf16[2,1,1,1,72,384]{5,4,3,2,1,0:T(8,128)(2,1)S(1)}, bf16[2,1,1,1,72,384]{5,4,3,2,1,0:T(8,128)(2,1)S(1)}, u32[]{:S(2)}, u32[]{:S(2)}) collective-permute-start(bf16[2,1,1,1,72,384]{5,4,3,2,1,0:T(8,128)(2,1)S(1)} %constant_dynamic-slice_fusion.17), channel_id=1, source_target_pairs={{0,2},{2,0},{4,6},{6,4},{8,10},{10,8},{12,14},{14,12},{16,18},{18,... | collective-permute-start | bytes 331784 | tf_op jit(solution)/shard_map/ppermute | solution.py:701
  196.8 102.0 %collective-permute-start.51 = (bf16[1024,768]{1,0:T(8,128)(2,1)}, bf16[1024,768]{1,0:T(8,128)(2,1)S(1)}, u32[]{:S(2)}, u32[]{:S(2)}) collective-permute-start(bf16[1024,768]{1,0:T(8,128)(2,1)} %convolution_convert_fusion), channel_id=1, source_target_pairs={{0,1},{1,0},{2,3},{3,2},{4,5},{5,4},{6,7},{7,6},{8,9},{9,8},{10,11... | collective-permute-start | bytes 4718600 | tf_op jit(solution)/shard_map/ppermute | solution.py:701
  236.3 10.4 %collective-permute-start.35 = (bf16[1,1,1,1,72,384]{5,4,3,2,1,0:T(8,128)(2,1)S(1)}, bf16[1,1,1,1,72,384]{5,4,3,2,1,0:T(8,128)(2,1)S(1)}, u32[]{:S(2)}, u32[]{:S(2)}) collective-permute-start(bf16[1,1,1,1,72,384]{5,4,3,2,1,0:T(8,128)(2,1)S(1)} %constant_dynamic-slice_fusion.15), channel_id=1, source_target_pairs={{0,16},{2,18},{4,20},{6,22},{8,24},{10,26},{12,28},{14,30},{16,0},... | collective-permute-start | bytes 165896 | tf_op jit(solution)/shard_map/ppermute | solution.py:701
  236.4 10.4 %collective-permute-start.36 = (bf16[1,1,1,1,72,384]{5,4,3,2,1,0:T(8,128)(2,1)S(1)}, bf16[1,1,1,1,72,384]{5,4,3,2,1,0:T(8,128)(2,1)S(1)}, u32[]{:S(2)}, u32[]{:S(2)}) collective-permute-start(bf16[1,1,1,1,72,384]{5,4,3,2,1,0:T(8,128)(2,1)S(1)} %constant_dynamic-slice_fusion.14), channel_id=1, source_target_pairs={{0,16},{2,18},{4,20},{6,22},{8,24},{10,26},{12,28},{14,30},{16,0},... | collective-permute-start | bytes 165896 | tf_op jit(solution)/shard_map/ppermute | solution.py:701
  239.3 11.0 %collective-permute-start.37 = (bf16[2,1,2,1,48,960]{5,4,3,2,1,0:T(8,128)(2,1)S(1)}, bf16[2,1,2,1,48,960]{5,4,3,2,1,0:T(8,128)(2,1)S(1)}, u32[]{:S(2)}, u32[]{:S(2)}) collective-permute-start(bf16[2,1,2,1,48,960]{5,4,3,2,1,0:T(8,128)(2,1)S(1)} %constant_dynamic-slice_fusion.13), channel_id=1, source_target_pairs={{0,2},{2,0},{4,6},{6,4},{8,10},{10,8},{12,14},{14,12},{16,18},{18,... | collective-permute-start | bytes 1105928 | tf_op jit(solution)/shard_map/ppermute | solution.py:701
  250.7 17.7 %collective-permute-start.38 = (bf16[2,2,2,1,72,256]{5,4,3,2,1,0:T(8,128)(2,1)S(1)}, bf16[2,2,2,1,72,256]{5,4,3,2,1,0:T(8,128)(2,1)S(1)}, u32[]{:S(2)}, u32[]{:S(2)}) collective-permute-start(bf16[2,2,2,1,72,256]{5,4,3,2,1,0:T(8,128)(2,1)S(1)} %constant_dynamic-slice_fusion.12), channel_id=1, source_target_pairs={{0,2},{2,0},{4,6},{6,4},{8,10},{10,8},{12,14},{14,12},{16,18},{18,... | collective-permute-start | bytes 884744 | tf_op jit(solution)/shard_map/ppermute | solution.py:701
  251.1 17.5 %collective-permute-start.39 = (bf16[2,2,1,2,72,256]{5,4,3,2,1,0:T(8,128)(2,1)S(1)}, bf16[2,2,1,2,72,256]{5,4,3,2,1,0:T(8,128)(2,1)S(1)}, u32[]{:S(2)}, u32[]{:S(2)}) collective-permute-start(bf16[2,2,1,2,72,256]{5,4,3,2,1,0:T(8,128)(2,1)S(1)} %constant_dynamic-slice_fusion.11), channel_id=1, source_target_pairs={{0,4},{2,6},{4,0},{6,2},{8,12},{10,14},{12,8},{14,10},{16,20},{18,... | collective-permute-start | bytes 884744 | tf_op jit(solution)/shard_map/ppermute | solution.py:701
  262.8 10.5 %collective-permute-start.40 = (bf16[2,1,2,2,72,256]{5,4,3,2,1,0:T(8,128)(2,1)S(1)}, bf16[2,1,2,2,72,256]{5,4,3,2,1,0:T(8,128)(2,1)S(1)}, u32[]{:S(2)}, u32[]{:S(2)}) collective-permute-start(bf16[2,1,2,2,72,256]{5,4,3,2,1,0:T(8,128)(2,1)S(1)} %constant_dynamic-slice_fusion.10), channel_id=1, source_target_pairs={{0,8},{2,10},{4,12},{6,14},{8,0},{10,2},{12,4},{14,6},{16,24},{18,... | collective-permute-start | bytes 884744 | tf_op jit(solution)/shard_map/ppermute | solution.py:701
  273.4 20.7 %collective-permute-start.44 = (bf16[2,2,1,1,72,256]{5,4,3,2,1,0:T(8,128)(2,1)S(1)}, bf16[2,2,1,1,72,256]{5,4,3,2,1,0:T(8,128)(2,1)S(1)}, u32[]{:S(2)}, u32[]{:S(2)}) collective-permute-start(bf16[2,2,1,1,72,256]{5,4,3,2,1,0:T(8,128)(2,1)S(1)} %constant_dynamic-slice_fusion.8), channel_id=1, source_target_pairs={{0,4},{2,6},{4,0},{6,2},{8,12},{10,14},{12,8},{14,10},{16,20},{18,... | collective-permute-start | bytes 442376 | tf_op jit(solution)/shard_map/ppermute | solution.py:701
  274.8 19.4 %collective-permute-start.45 = (bf16[2,1,1,2,72,256]{5,4,3,2,1,0:T(8,128)(2,1)S(1)}, bf16[2,1,1,2,72,256]{5,4,3,2,1,0:T(8,128)(2,1)S(1)}, u32[]{:S(2)}, u32[]{:S(2)}) collective-permute-start(bf16[2,1,1,2,72,256]{5,4,3,2,1,0:T(8,128)(2,1)S(1)} %constant_dynamic-slice_fusion.7), channel_id=1, source_target_pairs={{0,8},{2,10},{4,12},{6,14},{8,0},{10,2},{12,4},{14,6},{16,24},{18,... | collective-permute-start | bytes 442376 | tf_op jit(solution)/shard_map/ppermute | solution.py:701
  278.9 21.8 %collective-permute-start.50 = (bf16[1024,768]{1,0:T(8,128)(2,1)S(1)}, bf16[1024,768]{1,0:T(8,128)(2,1)S(1)}, u32[]{:S(2)}, u32[]{:S(2)}) collective-permute-start(bf16[1024,768]{1,0:T(8,128)(2,1)S(1)} %pull_other.1), channel_id=1, source_target_pairs={{0,1},{1,0},{2,3},{3,2},{4,5},{5,4},{6,7},{7,6},{8,9},{9,8},{10,11... | collective-permute-start | bytes 4718600 | tf_op jit(solution)/shard_map/ppermute | solution.py:701
  300.8 11.6 %collective-permute-start.52 = (bf16[2,1,1,1,72,256]{5,4,3,2,1,0:T(8,128)(2,1)S(1)}, bf16[2,1,1,1,72,256]{5,4,3,2,1,0:T(8,128)(2,1)S(1)}, u32[]{:S(2)}, u32[]{:S(2)}) collective-permute-start(bf16[2,1,1,1,72,256]{5,4,3,2,1,0:T(8,128)(2,1)S(1)} %constant_dynamic-slice_fusion.4), channel_id=1, source_target_pairs={{0,8},{2,10},{4,12},{6,14},{8,0},{10,2},{12,4},{14,6},{16,24},{18,... | collective-permute-start | bytes 221192 | tf_op jit(solution)/shard_map/ppermute | solution.py:701
  300.9 13.4 %collective-permute-start.53 = (bf16[2,1,1,1,72,256]{5,4,3,2,1,0:T(8,128)(2,1)S(1)}, bf16[2,1,1,1,72,256]{5,4,3,2,1,0:T(8,128)(2,1)S(1)}, u32[]{:S(2)}, u32[]{:S(2)}) collective-permute-start(bf16[2,1,1,1,72,256]{5,4,3,2,1,0:T(8,128)(2,1)S(1)} %constant_dynamic-slice_fusion.3), channel_id=1, source_target_pairs={{0,2},{2,0},{4,6},{6,4},{8,10},{10,8},{12,14},{14,12},{16,18},{18,... | collective-permute-start | bytes 221192 | tf_op jit(solution)/shard_map/ppermute | solution.py:701
  302.3 12.0 %collective-permute-start.54 = (bf16[2,1,1,1,72,256]{5,4,3,2,1,0:T(8,128)(2,1)S(1)}, bf16[2,1,1,1,72,256]{5,4,3,2,1,0:T(8,128)(2,1)S(1)}, u32[]{:S(2)}, u32[]{:S(2)}) collective-permute-start(bf16[2,1,1,1,72,256]{5,4,3,2,1,0:T(8,128)(2,1)S(1)} %constant_dynamic-slice_fusion.2), channel_id=1, source_target_pairs={{0,4},{2,6},{4,0},{6,2},{8,12},{10,14},{12,8},{14,10},{16,20},{18,... | collective-permute-start | bytes 221192 | tf_op jit(solution)/shard_map/ppermute | solution.py:701
  302.7 15.9 %collective-permute-start.55 = (bf16[2,2,1,1,72,384]{5,4,3,2,1,0:T(8,128)(2,1)S(1)}, bf16[2,2,1,1,72,384]{5,4,3,2,1,0:T(8,128)(2,1)S(1)}, u32[]{:S(2)}, u32[]{:S(2)}) collective-permute-start(bf16[2,2,1,1,72,384]{5,4,3,2,1,0:T(8,128)(2,1)S(1)} %pad_maximum_fusion.30), channel_id=1, source_target_pairs={{0,4},{2,6},{4,0},{6,2},{8,12},{10,14},{12,8},{14,10},{16,20},{18,... | collective-permute-start | bytes 663560 | tf_op jit(solution)/shard_map/ppermute | solution.py:701
  304.3 14.3 %collective-permute-start.56 = (bf16[2,1,1,2,72,384]{5,4,3,2,1,0:T(8,128)(2,1)S(1)}, bf16[2,1,1,2,72,384]{5,4,3,2,1,0:T(8,128)(2,1)S(1)}, u32[]{:S(2)}, u32[]{:S(2)}) collective-permute-start(bf16[2,1,1,2,72,384]{5,4,3,2,1,0:T(8,128)(2,1)S(1)} %pad_maximum_fusion.31), channel_id=1, source_target_pairs={{0,8},{2,10},{4,12},{6,14},{8,0},{10,2},{12,4},{14,6},{16,24},{18,... | collective-permute-start | bytes 663560 | tf_op jit(solution)/shard_map/ppermute | solution.py:701
  323.1 17.3 %collective-permute-start.61 = (bf16[2,2,2,1,72,384]{5,4,3,2,1,0:T(8,128)(2,1)S(1)}, bf16[2,2,2,1,72,384]{5,4,3,2,1,0:T(8,128)(2,1)S(1)}, u32[]{:S(2)}, u32[]{:S(2)}) collective-permute-start(bf16[2,2,2,1,72,384]{5,4,3,2,1,0:T(8,128)(2,1)S(1)} %pad_maximum_fusion.18), channel_id=1, source_target_pairs={{0,2},{2,0},{4,6},{6,4},{8,10},{10,8},{12,14},{14,12},{16,18},{18,... | collective-permute-start | bytes 1327112 | tf_op jit(solution)/shard_map/ppermute | solution.py:701
  324.3 16.3 %collective-permute-start.62 = (bf16[2,2,1,2,72,384]{5,4,3,2,1,0:T(8,128)(2,1)S(1)}, bf16[2,2,1,2,72,384]{5,4,3,2,1,0:T(8,128)(2,1)S(1)}, u32[]{:S(2)}, u32[]{:S(2)}) collective-permute-start(bf16[2,2,1,2,72,384]{5,4,3,2,1,0:T(8,128)(2,1)S(1)} %pad_maximum_fusion.19), channel_id=1, source_target_pairs={{0,4},{2,6},{4,0},{6,2},{8,12},{10,14},{12,8},{14,10},{16,20},{18,... | collective-permute-start | bytes 1327112 | tf_op jit(solution)/shard_map/ppermute | solution.py:701
  324.4 16.0 %collective-permute-start.63 = (bf16[2,1,1,1,48,960]{5,4,3,2,1,0:T(8,128)(2,1)S(1)}, bf16[2,1,1,1,48,960]{5,4,3,2,1,0:T(8,128)(2,1)S(1)}, u32[]{:S(2)}, u32[]{:S(2)}) collective-permute-start(bf16[2,1,1,1,48,960]{5,4,3,2,1,0:T(8,128)(2,1)S(1)} %pad_maximum_fusion.33), channel_id=1, source_target_pairs={{0,4},{2,6},{4,0},{6,2},{8,12},{10,14},{12,8},{14,10},{16,20},{18,... | collective-permute-start | bytes 552968 | tf_op jit(solution)/shard_map/ppermute | solution.py:701
  341.5 11.2 %collective-permute-start.65 = (bf16[1,1,1,1,72,256]{5,4,3,2,1,0:T(8,128)(2,1)S(1)}, bf16[1,1,1,1,72,256]{5,4,3,2,1,0:T(8,128)(2,1)S(1)}, u32[]{:S(2)}, u32[]{:S(2)}) collective-permute-start(bf16[1,1,1,1,72,256]{5,4,3,2,1,0:T(8,128)(2,1)S(1)} %get-tuple-element.327), channel_id=1, source_target_pairs={{0,16},{2,18},{4,20},{6,22},{8,24},{10,26},{12,28},{14,30},{16,0},... | collective-permute-start | bytes 110600 | tf_op jit(solution)/shard_map/ppermute | solution.py:701
  342.7 10.0 %collective-permute-start.68 = (bf16[2,1,2,1,48,960]{5,4,3,2,1,0:T(8,128)(2,1)S(1)}, bf16[2,1,2,1,48,960]{5,4,3,2,1,0:T(8,128)(2,1)S(1)}, u32[]{:S(2)}, u32[]{:S(2)}) collective-permute-start(bf16[2,1,2,1,48,960]{5,4,3,2,1,0:T(8,128)(2,1)S(1)} %pad_maximum_fusion.21), channel_id=1, source_target_pairs={{0,2},{2,0},{4,6},{6,4},{8,10},{10,8},{12,14},{14,12},{16,18},{18,... | collective-permute-start | bytes 1105928 | tf_op jit(solution)/shard_map/ppermute | solution.py:701
  352.8 19.1 %collective-permute-start.73 = (bf16[2,1,2,2,48,960]{5,4,3,2,1,0:T(8,128)(2,1)S(1)}, bf16[2,1,2,2,48,960]{5,4,3,2,1,0:T(8,128)(2,1)S(1)}, u32[]{:S(2)}, u32[]{:S(2)}) collective-permute-start(bf16[2,1,2,2,48,960]{5,4,3,2,1,0:T(8,128)(2,1)S(1)} %pad_maximum_fusion.9), channel_id=1, source_target_pairs={{0,8},{2,10},{4,12},{6,14},{8,0},{10,2},{12,4},{14,6},{16,24},{18,... | collective-permute-start | bytes 2211848 | tf_op jit(solution)/shard_map/ppermute | solution.py:701
  352.9 18.9 %collective-permute-start.70 = (bf16[2,1,1,1,72,256]{5,4,3,2,1,0:T(8,128)(2,1)S(1)}, bf16[2,1,1,1,72,256]{5,4,3,2,1,0:T(8,128)(2,1)S(1)}, u32[]{:S(2)}, u32[]{:S(2)}) collective-permute-start(bf16[2,1,1,1,72,256]{5,4,3,2,1,0:T(8,128)(2,1)S(1)} %pad_maximum_fusion.49), channel_id=1, source_target_pairs={{0,8},{2,10},{4,12},{6,14},{8,0},{10,2},{12,4},{14,6},{16,24},{18,... | collective-permute-start | bytes 221192 | tf_op jit(solution)/shard_map/ppermute | solution.py:701
  354.9 15.3 %collective-permute-start.74 = (f32[2,768]{1,0:T(2,128)S(1)}, f32[2,768]{1,0:T(2,128)S(1)}, u32[]{:S(2)}, u32[]{:S(2)}) collective-permute-start(f32[2,768]{1,0:T(2,128)S(1)} %add.263), channel_id=1, source_target_pairs={{0,4},{2,6},{4,0},{6,2},{8,12},{10,14},{12,8},{14,10},{16,20},{18,... | collective-permute-start | bytes 18440 | tf_op jit(solution)/shard_map/ppermute | solution.py:701
  355.6 16.1 %collective-permute-start.71 = (bf16[2,1,1,1,72,256]{5,4,3,2,1,0:T(8,128)(2,1)S(1)}, bf16[2,1,1,1,72,256]{5,4,3,2,1,0:T(8,128)(2,1)S(1)}, u32[]{:S(2)}, u32[]{:S(2)}) collective-permute-start(bf16[2,1,1,1,72,256]{5,4,3,2,1,0:T(8,128)(2,1)S(1)} %pad_maximum_fusion.50), channel_id=1, source_target_pairs={{0,2},{2,0},{4,6},{6,4},{8,10},{10,8},{12,14},{14,12},{16,18},{18,... | collective-permute-start | bytes 221192 | tf_op jit(solution)/shard_map/ppermute | solution.py:701
  356.6 15.2 %collective-permute-start.72 = (bf16[2,1,1,1,72,256]{5,4,3,2,1,0:T(8,128)(2,1)S(1)}, bf16[2,1,1,1,72,256]{5,4,3,2,1,0:T(8,128)(2,1)S(1)}, u32[]{:S(2)}, u32[]{:S(2)}) collective-permute-start(bf16[2,1,1,1,72,256]{5,4,3,2,1,0:T(8,128)(2,1)S(1)} %pad_maximum_fusion.51), channel_id=1, source_target_pairs={{0,4},{2,6},{4,0},{6,2},{8,12},{10,14},{12,8},{14,10},{16,20},{18,... | collective-permute-start | bytes 221192 | tf_op jit(solution)/shard_map/ppermute | solution.py:701
  372.0 12.2 %collective-permute-start.75 = (bf16[2,2,1,1,72,256]{5,4,3,2,1,0:T(8,128)(2,1)S(1)}, bf16[2,2,1,1,72,256]{5,4,3,2,1,0:T(8,128)(2,1)S(1)}, u32[]{:S(2)}, u32[]{:S(2)}) collective-permute-start(bf16[2,2,1,1,72,256]{5,4,3,2,1,0:T(8,128)(2,1)S(1)} %pad_maximum_fusion.37), channel_id=1, source_target_pairs={{0,4},{2,6},{4,0},{6,2},{8,12},{10,14},{12,8},{14,10},{16,20},{18,... | collective-permute-start | bytes 442376 | tf_op jit(solution)/shard_map/ppermute | solution.py:701
  372.8 11.4 %collective-permute-start.76 = (bf16[2,1,1,2,72,256]{5,4,3,2,1,0:T(8,128)(2,1)S(1)}, bf16[2,1,1,2,72,256]{5,4,3,2,1,0:T(8,128)(2,1)S(1)}, u32[]{:S(2)}, u32[]{:S(2)}) collective-permute-start(bf16[2,1,1,2,72,256]{5,4,3,2,1,0:T(8,128)(2,1)S(1)} %pad_maximum_fusion.38), channel_id=1, source_target_pairs={{0,8},{2,10},{4,12},{6,14},{8,0},{10,2},{12,4},{14,6},{16,24},{18,... | collective-permute-start | bytes 442376 | tf_op jit(solution)/shard_map/ppermute | solution.py:701
  373.1 11.0 %collective-permute-start.78 = (f32[2,768]{1,0:T(2,128)S(1)}, f32[2,768]{1,0:T(2,128)S(1)}, u32[]{:S(2)}, u32[]{:S(2)}) collective-permute-start(f32[2,768]{1,0:T(2,128)S(1)} %add.264), channel_id=1, source_target_pairs={{0,8},{2,10},{4,12},{6,14},{8,0},{10,2},{12,4},{14,6},{16,24},{18,... | collective-permute-start | bytes 18440 | tf_op jit(solution)/shard_map/ppermute | solution.py:701
  384.3 8.9 %collective-permute-start.82 = (f32[2,768]{1,0:T(2,128)S(1)}, f32[2,768]{1,0:T(2,128)S(1)}, u32[]{:S(2)}, u32[]{:S(2)}) collective-permute-start(f32[2,768]{1,0:T(2,128)S(1)} %add.265), channel_id=1, source_target_pairs={{0,16},{2,18},{4,20},{6,22},{8,24},{10,26},{12,28},{14,30},{16,0},... | collective-permute-start | bytes 18440 | tf_op jit(solution)/shard_map/ppermute | solution.py:701
  (81 other events, 824.8 us)
